TPU v7x, 32 devices: a whole 2x2x4 slice. The times are simulated.
32 devices in a mesh: seq: 4 (over z), fsdp: 8 (over y, x, core).
Axes of the slice: x: 2, y: 2, z: 4, core: 2. Of those that a mesh axis runs over, the one named last changes fastest.
Arguments:
- tokens: bfloat16 [4, 2, 1024, 2048], P('seq', None, 'fsdp'), may hold values from -9 to 9
- doc_starts: int32 [4, 4], P('seq'), may hold values from 0 to 1919, as said below
- norm_in: float32 [2048], P('fsdp'), may hold values from 0.5 to 1.5
- w_query: bfloat16 [2048, 2048], P('fsdp'), may hold values from -0.125 to 0.125
- w_key: bfloat16 [2048, 2048], P('fsdp'), may hold values from -0.125 to 0.125
- w_value: bfloat16 [2048, 2048], P('fsdp'), may hold values from -0.125 to 0.125
- mix_bias: float32 [16], P('fsdp'), may hold values from -0.5 to 2.5
- w_out: bfloat16 [2048, 2048], P('fsdp'), may hold values from -0.1875 to 0.1875
- norm_mid: float32 [2048], P('fsdp'), may hold values from 0.5 to 1.5
- w_gate: bfloat16 [2048, 8192], P('fsdp'), may hold values from -0.125 to 0.125
- w_up: bfloat16 [2048, 8192], P('fsdp'), may hold values from -0.125 to 0.125
- w_down: bfloat16 [8192, 2048], P('fsdp'), may hold values from -0.0625 to 0.0625
- cotangent: bfloat16 [4, 2, 1024, 2048], P('seq', None, 'fsdp'), may hold values from -6 to 6
Outputs:
- block_out: bfloat16 [4, 2, 1024, 2048], P('seq', None, 'fsdp')
- grad_tokens: float32 [4, 2, 1024, 2048], P('seq', None, 'fsdp')
- grad_norm_in: float32 [2048], P('fsdp')
- grad_query: float32 [2048, 2048], P('fsdp')
- grad_key: float32 [2048, 2048], P('fsdp')
- grad_value: float32 [2048, 2048], P('fsdp')
- grad_mix_bias: float32 [16], P('fsdp')
- grad_out: float32 [2048, 2048], P('fsdp')
- grad_norm_mid: float32 [2048], P('fsdp')
- grad_gate: float32 [2048, 8192], P('fsdp')
- grad_up: float32 [2048, 8192], P('fsdp')
- grad_down: float32 [8192, 2048], P('fsdp')
Inputs may be any that keep to these rules, and one draw needn't show every extreme that they name: `doc_starts`: entry 0 of every row is 0 and the entries rise strictly; document d of a sequence covers the positions from its entry up to the next entry (or 2048) minus one.
All inputs are finite; a program needn't handle non-finite values.
Results may differ from a plain program's by a relative error of at most 0.035.
Values may be sent and summed in bfloat16 or wider, within the bound.
A program may use at most 704 MiB of HBM per device.

v0:
```python
import jax
import jax.numpy as jnp
from jax import lax
from jax.sharding import PartitionSpec as P

HEADS = 16
HEAD_DIM = 128
NSEG = 2


highest = lax.Precision.HIGHEST
norm_eps = 1e-05


def doc_number(start_row, places):
    return jnp.sum((start_row[None, :] <= places[:, None]).astype(jnp.int32), axis=1) - 1


def feature(values):
    return jax.nn.elu(values) + 1.0


def feature_slope(values):
    return jnp.where(values > 0, 1.0, jnp.exp(jnp.minimum(values, 0.0)))


def silu_slope(values):
    sigmoid_value = jax.nn.sigmoid(values)
    return sigmoid_value * (1.0 + values * (1.0 - sigmoid_value))


def norm_back(grad_in, normed, inverse):
    return inverse * (grad_in - normed * jnp.mean(grad_in * normed, axis=-1, keepdims=True))


def contract_last(left_side, right_side):
    return lax.dot_general(
        left_side, right_side, (((1,), (1,)), ((), ())), preferred_element_type=jnp.float32
    )


def contract_first(left_side, right_side):
    return lax.dot_general(
        left_side, right_side, (((0,), (0,)), ((), ())), preferred_element_type=jnp.float32
    )


def shards(
    tokens,
    doc_starts,
    norm_in,
    w_query,
    w_key,
    w_value,
    mix_bias,
    w_out,
    norm_mid,
    w_gate,
    w_up,
    w_down,
    cotangent,
):
    seg_rows = tokens.shape[2]
    model_width = tokens.shape[3]
    inner_width = w_gate.shape[1]
    groups = lax.axis_size("fsdp")
    device_rank = lax.axis_index("fsdp")
    seg_len = seg_rows * groups
    tok_count = NSEG * seg_rows
    score_scale = HEAD_DIM ** (-0.5)
    local_index = jnp.arange(tok_count, dtype=jnp.int32)
    seg_index = local_index // seg_rows
    places = seg_index * seg_len + device_rank * seg_rows + local_index % seg_rows
    start_row = doc_starts[0]
    own_docs = doc_number(start_row, places)
    key_places = jnp.arange(seg_len, dtype=jnp.int32)
    cross_doc = doc_number(start_row, jnp.full((1,), seg_len, jnp.int32))[0]
    use_mask = ((seg_index == 1) & (own_docs == cross_doc)).astype(jnp.float32)
    own_weight = ((seg_index == 0) & (own_docs == cross_doc)).astype(jnp.float32)
    flat_in = tokens.reshape(tok_count, model_width).astype(jnp.float32)
    inv_in = lax.rsqrt(jnp.mean(flat_in * flat_in, axis=1, keepdims=True) + norm_eps)
    normed_in = flat_in * inv_in
    empty_rows = jnp.zeros((tok_count, model_width), jnp.float32)
    empty_inner = jnp.zeros((tok_count, inner_width), jnp.float32)
    empty_gain = jnp.zeros((model_width,), jnp.float32)
    attn_init = (empty_rows, empty_rows, empty_rows, empty_gain)
    mlp_init = (empty_inner, empty_inner, empty_gain)
    pieces = (
        lax.all_gather(w_query, "fsdp", axis=0, tiled=True),
        lax.all_gather(w_key, "fsdp", axis=0, tiled=True),
        lax.all_gather(w_value, "fsdp", axis=0, tiled=True),
        lax.all_gather(norm_in.astype(jnp.bfloat16), "fsdp", axis=0, tiled=True).astype(
            jnp.float32
        ),
    )
    offset = jnp.int32(0)
    left_rows = (normed_in * pieces[3][None, :]).astype(jnp.bfloat16)
    updated = (
        jnp.dot(left_rows, pieces[0], preferred_element_type=jnp.float32),
        jnp.dot(left_rows, pieces[1], preferred_element_type=jnp.float32),
        jnp.dot(left_rows, pieces[2], preferred_element_type=jnp.float32),
        lax.dynamic_update_slice_in_dim(attn_init[3], pieces[3], offset, 0),
    )
    folded = updated + tuple(
        (
            lax.dynamic_update_slice_in_dim(held_rows, fresh_rows, offset, 0)
            for held_rows, fresh_rows in zip(attn_init[4:], pieces[:3])
        )
    )
    query_rows = folded[0].astype(jnp.bfloat16)
    key_rows = folded[1].astype(jnp.bfloat16)
    value_rows = folded[2].astype(jnp.bfloat16)
    gain_in = folded[3]
    key_all, value_all = (
        lax.all_gather(
            key_rows.reshape(1, NSEG, seg_rows, model_width), "fsdp", axis=2, tiled=True
        ),
        lax.all_gather(
            value_rows.reshape(1, NSEG, seg_rows, model_width), "fsdp", axis=2, tiled=True
        ),
    )
    key_all = key_all.reshape(NSEG, seg_len, HEADS, HEAD_DIM)
    value_all = value_all.reshape(NSEG, seg_len, HEADS, HEAD_DIM)
    query_heads = query_rows.reshape(tok_count, HEADS, HEAD_DIM)
    key_heads = key_rows.reshape(tok_count, HEADS, HEAD_DIM)
    value_heads = value_rows.reshape(tok_count, HEADS, HEAD_DIM)
    feat_query = feature(query_heads.astype(jnp.float32))
    first_docs = doc_number(start_row, key_places)
    key_mask = (first_docs == cross_doc).astype(jnp.float32)
    feat_first = feature(key_all[0].astype(jnp.float32))
    value_first = value_all[0].astype(jnp.float32)
    feat_own = feature(key_heads.astype(jnp.float32))
    weighted = feat_own * own_weight[:, None, None]
    part_memory = jnp.einsum(
        "thd,the->hde", weighted, value_heads.astype(jnp.float32), precision=highest
    )
    memory, norm_vec = (
        lax.psum(part_memory.astype(jnp.bfloat16), "fsdp").astype(jnp.float32),
        lax.psum(jnp.sum(weighted, axis=0).astype(jnp.bfloat16), "fsdp").astype(jnp.float32),
    )
    numerator = jnp.einsum("thd,hde->the", feat_query, memory, precision=highest)
    denominator = jnp.einsum("thd,hd->th", feat_query, norm_vec, precision=highest) + 1.0
    retrieved = use_mask[:, None, None] * numerator / denominator[:, :, None]

    def scores_of(segment):
        query_part = query_heads[segment * seg_rows : (segment + 1) * seg_rows]
        raw_scores = (
            jnp.einsum(
                "qhe,khe->hqk", query_part, key_all[segment], preferred_element_type=jnp.float32
            )
            * score_scale
        )
        query_pos = device_rank * seg_rows + jnp.arange(seg_rows, dtype=jnp.int32)
        query_docs = own_docs[segment * seg_rows : (segment + 1) * seg_rows]
        key_docs = doc_number(start_row, segment * seg_len + key_places)
        allowed = (key_places[None, :] <= query_pos[:, None]) & (
            key_docs[None, :] == query_docs[:, None]
        )
        return jnp.where(allowed[None], raw_scores, -1000000000.0)

    direct_parts = []
    lse_parts = []
    for segment in range(NSEG):
        masked = scores_of(segment)
        log_total = jax.nn.logsumexp(masked, axis=2, keepdims=True)
        prob_rows = jnp.exp(masked - log_total).astype(jnp.bfloat16)
        direct_parts.append(
            jnp.einsum(
                "hqk,khe->qhe", prob_rows, value_all[segment], preferred_element_type=jnp.float32
            )
        )
        lse_parts.append(log_total)
    direct = jnp.concatenate(direct_parts, axis=0)
    ret_flat = retrieved.reshape(tok_count, model_width)
    direct_flat = direct.reshape(tok_count, model_width)
    bias_rows = jnp.repeat(mix_bias, HEAD_DIM)
    pieces = (
        lax.all_gather(w_out, "fsdp", axis=0, tiled=True),
        lax.all_gather(bias_rows.astype(jnp.bfloat16), "fsdp", axis=0, tiled=True).astype(
            jnp.float32
        ),
    )
    blend_gate = jax.nn.sigmoid(pieces[1])[None, :]
    left_rows = (blend_gate * ret_flat + (1.0 - blend_gate) * direct_flat).astype(jnp.bfloat16)
    attn_sum = jnp.dot(left_rows, pieces[0], preferred_element_type=jnp.float32)
    bias_full = lax.dynamic_update_slice_in_dim(
        (empty_rows, empty_gain)[1], pieces[1], jnp.int32(0), 0
    )
    residual = flat_in + attn_sum
    inv_mid = lax.rsqrt(jnp.mean(residual * residual, axis=1, keepdims=True) + norm_eps)
    normed_mid = residual * inv_mid
    pieces = (
        lax.all_gather(w_gate, "fsdp", axis=0, tiled=True),
        lax.all_gather(w_up, "fsdp", axis=0, tiled=True),
        lax.all_gather(norm_mid.astype(jnp.bfloat16), "fsdp", axis=0, tiled=True).astype(
            jnp.float32
        ),
    )
    offset = jnp.int32(0)
    left_rows = (normed_mid * pieces[2][None, :]).astype(jnp.bfloat16)
    updated = (
        jnp.dot(left_rows, pieces[0], preferred_element_type=jnp.float32),
        jnp.dot(left_rows, pieces[1], preferred_element_type=jnp.float32),
        lax.dynamic_update_slice_in_dim(mlp_init[2], pieces[2], offset, 0),
    )
    mlp_folded = updated + tuple(
        (
            lax.dynamic_update_slice_in_dim(held_rows, fresh_rows, offset, 0)
            for held_rows, fresh_rows in zip(mlp_init[3:], pieces[:2])
        )
    )
    gate_pre = mlp_folded[0]
    up_pre = mlp_folded[1]
    gain_mid = mlp_folded[2]
    inner_rows = (jax.nn.silu(gate_pre) * up_pre).astype(jnp.bfloat16)
    grad_rows = cotangent.reshape(tok_count, model_width)
    weight_piece = lax.all_gather(w_down, "fsdp", axis=0, tiled=True)
    left_rows = inner_rows
    mlp_sum = jnp.dot(left_rows, weight_piece, preferred_element_type=jnp.float32)
    d_inner = contract_last(grad_rows, weight_piece)
    block_out = (residual + mlp_sum).astype(jnp.bfloat16).reshape(tokens.shape)
    grad_down = lax.psum_scatter(
        contract_first(inner_rows, grad_rows).astype(jnp.bfloat16),
        "fsdp",
        scatter_dimension=0,
        tiled=True,
    )
    d_gate = (d_inner * up_pre * silu_slope(gate_pre)).astype(jnp.bfloat16)
    d_up = (d_inner * jax.nn.silu(gate_pre)).astype(jnp.bfloat16)
    pieces = lax.all_gather((w_gate, w_up), "fsdp", axis=0, tiled=True)
    d_hmid = contract_last(d_gate, pieces[0]) + contract_last(d_up, pieces[1])
    h_mid = (normed_mid * gain_mid[None, :]).astype(jnp.bfloat16)
    left_rows = h_mid
    both_grads = lax.psum_scatter(
        jnp.concatenate(
            [contract_first(left_rows, d_gate), contract_first(left_rows, d_up)], axis=1
        ).astype(jnp.bfloat16),
        "fsdp",
        scatter_dimension=0,
        tiled=True,
    ).astype(jnp.float32)
    gain_mid_term = jnp.sum(normed_mid * d_hmid, axis=0)
    d_resid = grad_rows.astype(jnp.float32) + norm_back(
        d_hmid * gain_mid[None, :], normed_mid, inv_mid
    )
    d_attn = d_resid.astype(jnp.bfloat16)
    d_mixed = contract_last(d_attn, lax.all_gather(w_out, "fsdp", axis=0, tiled=True))
    blend_full = jax.nn.sigmoid(bias_full)[None, :]
    mixed_rows = (blend_full * ret_flat + (1.0 - blend_full) * direct_flat).astype(jnp.bfloat16)
    out_term = contract_first(mixed_rows, d_attn)
    bias_term = (
        jnp.sum(d_mixed * (ret_flat - direct_flat), axis=0) * (blend_full * (1.0 - blend_full))[0]
    )
    d_ret = (blend_full * d_mixed).reshape(tok_count, HEADS, HEAD_DIM)
    d_direct = (
        ((1.0 - blend_full) * d_mixed).astype(jnp.bfloat16).reshape(tok_count, HEADS, HEAD_DIM)
    )
    d_num = use_mask[:, None, None] * d_ret / denominator[:, :, None]
    d_den = -jnp.sum(d_num * numerator, axis=2) / denominator
    d_memory = jnp.einsum("thd,the->hde", feat_query, d_num, precision=highest)
    d_norm = jnp.einsum("thd,th->hd", feat_query, d_den, precision=highest)
    d_featq = (
        jnp.einsum("the,hde->thd", d_num, memory, precision=highest)
        + d_den[:, :, None] * norm_vec[None]
    )
    d_query_mem = d_featq * feature_slope(query_heads.astype(jnp.float32))
    key_term_parts = []
    value_term_parts = []
    d_query_parts = []
    balance_parts = []
    for segment in range(NSEG):
        query_part = query_heads[segment * seg_rows : (segment + 1) * seg_rows]
        grad_part = d_direct[segment * seg_rows : (segment + 1) * seg_rows]
        exp_rows = jnp.exp(scores_of(segment) - lse_parts[segment])
        d_prob = jnp.einsum(
            "qhe,khe->hqk", grad_part, value_all[segment], preferred_element_type=jnp.float32
        )
        balance = jnp.sum(exp_rows * d_prob, axis=2, keepdims=True)
        balance_parts.append(balance)
        d_score = (exp_rows * (d_prob - balance)).astype(jnp.bfloat16)
        d_query_parts.append(
            jnp.einsum(
                "hqk,khe->qhe", d_score, key_all[segment], preferred_element_type=jnp.float32
            )
            * score_scale
        )
        prob_rows = exp_rows.astype(jnp.bfloat16)
        key_term_parts.append(
            jnp.einsum("hqk,qhe->khe", d_score, query_part, preferred_element_type=jnp.float32)
            * score_scale
        )
        value_term_parts.append(
            jnp.einsum("hqk,qhe->khe", prob_rows, grad_part, preferred_element_type=jnp.float32)
        )
    mem_value = key_mask[:, None, None] * jnp.einsum(
        "khd,hde->khe", feat_first, d_memory, precision=highest
    )
    mem_key = (
        key_mask[:, None, None]
        * (jnp.einsum("khe,hde->khd", value_first, d_memory, precision=highest) + d_norm[None])
        * feature_slope(key_all[0].astype(jnp.float32))
    )
    key_term_parts[0] = key_term_parts[0] + mem_key
    value_term_parts[0] = value_term_parts[0] + mem_value
    key_term = jnp.stack(key_term_parts).reshape(1, NSEG, seg_len, model_width)
    value_term = jnp.stack(value_term_parts).reshape(1, NSEG, seg_len, model_width)
    d_key_sum, d_value_sum = (
        lax.psum_scatter(
            key_term.astype(jnp.bfloat16), "fsdp", scatter_dimension=2, tiled=True
        ).astype(jnp.float32),
        lax.psum_scatter(
            value_term.astype(jnp.bfloat16), "fsdp", scatter_dimension=2, tiled=True
        ).astype(jnp.float32),
    )
    d_key = d_key_sum.reshape(tok_count, model_width).astype(jnp.bfloat16)
    d_value = d_value_sum.reshape(tok_count, model_width).astype(jnp.bfloat16)
    d_query = (
        (jnp.concatenate(d_query_parts, axis=0) + d_query_mem)
        .reshape(tok_count, model_width)
        .astype(jnp.bfloat16)
    )
    pieces = lax.all_gather((w_query, w_key, w_value), "fsdp", axis=0, tiled=True)
    d_hin = (
        contract_last(d_query, pieces[0])
        + contract_last(d_key, pieces[1])
        + contract_last(d_value, pieces[2])
    )
    h_in = (normed_in * gain_in[None, :]).astype(jnp.bfloat16)
    gain_in_term = jnp.sum(normed_in * d_hin, axis=0)
    grad_tokens = d_resid + norm_back(d_hin * gain_in[None, :], normed_in, inv_in)
    scattered = (
        lax.psum_scatter(
            contract_first(h_in, d_query).astype(jnp.bfloat16),
            "fsdp",
            scatter_dimension=0,
            tiled=True,
        ).astype(jnp.float32),
        lax.psum_scatter(
            contract_first(h_in, d_key).astype(jnp.bfloat16),
            "fsdp",
            scatter_dimension=0,
            tiled=True,
        ).astype(jnp.float32),
        lax.psum_scatter(
            contract_first(h_in, d_value).astype(jnp.bfloat16),
            "fsdp",
            scatter_dimension=0,
            tiled=True,
        ).astype(jnp.float32),
        lax.psum_scatter(
            out_term.astype(jnp.bfloat16), "fsdp", scatter_dimension=0, tiled=True
        ).astype(jnp.float32),
        lax.psum_scatter(
            gain_in_term.astype(jnp.bfloat16), "fsdp", scatter_dimension=0, tiled=True
        ).astype(jnp.float32),
        lax.psum_scatter(
            gain_mid_term.astype(jnp.bfloat16), "fsdp", scatter_dimension=0, tiled=True
        ).astype(jnp.float32),
        lax.psum_scatter(
            bias_term.astype(jnp.bfloat16), "fsdp", scatter_dimension=0, tiled=True
        ).astype(jnp.float32),
    )
    summed = (
        lax.psum(scattered[0].astype(jnp.bfloat16), "seq").astype(jnp.float32),
        lax.psum(scattered[1].astype(jnp.bfloat16), "seq").astype(jnp.float32),
        lax.psum(scattered[2].astype(jnp.bfloat16), "seq").astype(jnp.float32),
        lax.psum(scattered[3].astype(jnp.bfloat16), "seq").astype(jnp.float32),
        lax.psum(scattered[4].astype(jnp.bfloat16), "seq").astype(jnp.float32),
        lax.psum(scattered[5].astype(jnp.bfloat16), "seq").astype(jnp.float32),
        lax.psum(scattered[6].astype(jnp.bfloat16), "seq").astype(jnp.float32),
        lax.psum(both_grads[:, :inner_width].astype(jnp.bfloat16), "seq").astype(jnp.float32),
        lax.psum(both_grads[:, inner_width:].astype(jnp.bfloat16), "seq").astype(jnp.float32),
        lax.psum(grad_down, "seq").astype(jnp.float32),
    )
    grad_bias = summed[6].reshape(-1, HEAD_DIM).sum(axis=1)
    return (
        block_out,
        grad_tokens.reshape(tokens.shape),
        summed[4],
        summed[0],
        summed[1],
        summed[2],
        grad_bias,
        summed[3],
        summed[5],
        summed[7],
        summed[8],
        summed[9],
    )


def solution(mesh):
    placed = (
        P("seq", None, "fsdp", None),
        P("seq", None),
        P("fsdp"),
        P("fsdp", None),
        P("fsdp", None),
        P("fsdp", None),
        P("fsdp"),
        P("fsdp", None),
        P("fsdp"),
        P("fsdp", None),
        P("fsdp", None),
        P("fsdp", None),
        P("seq", None, "fsdp", None),
    )
    return jax.shard_map(
        shards,
        mesh=mesh,
        in_specs=placed,
        out_specs=(
            P("seq", None, "fsdp", None),
            P("seq", None, "fsdp", None),
            P("fsdp"),
            P("fsdp", None),
            P("fsdp", None),
            P("fsdp", None),
            P("fsdp"),
            P("fsdp", None),
            P("fsdp"),
            P("fsdp", None),
            P("fsdp", None),
            P("fsdp", None),
        ),
        check_vma=False,
    )
```

profile of v0, /device:TPU:0, one launch (start us, length us, event | category | flops | bytes accessed | tf_op | source)
XLA Modules:
  0.0 2717.9 jit_solution(2218314182387447483)
XLA Ops:
  25.9 41.2 %all-gather.15.cloned.1.call-done = bf16[2048,2048]{1,0:T(8,128)(2,1)} async-done(((bf16[256,2048]{1,0:T(8,128)(2,1)}), bf16[2048,2048]{1,0:T(8,128)(2,1)}) %all-gather.15.cloned.1.call-update) | async-done | bytes 8388624 | tf_op jit(solution)/shard_map/all_gather | solution.py:91
  72.8 50.6 %all-gather.13.cloned.1.call-done = bf16[2048,2048]{1,0:T(8,128)(2,1)} async-done(((bf16[256,2048]{1,0:T(8,128)(2,1)}), bf16[2048,2048]{1,0:T(8,128)(2,1)}) %all-gather.13.cloned.1.call-update) | async-done | bytes 8388624 | tf_op jit(solution)/shard_map/all_gather | solution.py:90
  157.6 22.0 all-gather.17.cloned.1.call-done
  187.6 13.2 psum.85
  203.9 34.0 %all-reduce.9.cloned.1.call-done = bf16[16,128,128]{2,1,0:T(8,128)(2,1)} async-done(((bf16[16,128,128]{2,1,0:T(8,128)(2,1)}), bf16[16,128,128]{2,1,0:T(8,128)(2,1)}) %all-reduce.9.cloned.1.call-update) | async-done | bytes 524304 | tf_op jit(solution)/shard_map/psum | solution.py:138
  245.3 50.2 %all-gather.21.cloned.1.call-done = bf16[1,2,1024,2048]{2,3,1,0:T(8,128)(2,1)} async-done(((bf16[1,2,128,2048]{2,3,1,0:T(8,128)(2,1)}), bf16[1,2,1024,2048]{2,3,1,0:T(8,128)(2,1)}) %all-gather.21.cloned.1.call-update) | async-done | bytes 8388624 | tf_op jit(solution)/shard_map/all_gather | solution.py:115
  310.7 43.3 %all-gather.19.cloned.1.call-done = bf16[1,2,1024,2048]{2,3,1,0:T(8,128)(2,1)} async-done(((bf16[1,2,128,2048]{2,3,1,0:T(8,128)(2,1)}), bf16[1,2,1024,2048]{2,3,1,0:T(8,128)(2,1)}) %all-gather.19.cloned.1.call-update) | async-done | bytes 8388624 | tf_op jit(solution)/shard_map/all_gather | solution.py:118
  381.0 29.5 %all-gather.23.cloned.1.call-done = bf16[2048,2048]{1,0:T(8,128)(2,1)} async-done(((bf16[256,2048]{1,0:T(8,128)(2,1)}), bf16[2048,2048]{1,0:T(8,128)(2,1)}) %all-gather.23.cloned.1.call-update) | async-done | bytes 8388624 | tf_op jit(solution)/shard_map/all_gather | solution.py:178
  418.3 155.1 %all-gather.25.cloned.1.call-done = bf16[2048,8192]{1,0:T(8,128)(2,1)} async-done(((bf16[256,8192]{1,0:T(8,128)(2,1)}), bf16[2048,8192]{1,0:T(8,128)(2,1)}) %all-gather.25.cloned.1.call-update) | async-done | bytes 33554448 | tf_op jit(solution)/shard_map/all_gather | solution.py:193
  573.4 19.9 fusion.93
  593.3 142.9 %all-gather.27.cloned.1.call-done = bf16[2048,8192]{1,0:T(8,128)(2,1)} async-done(((bf16[256,8192]{1,0:T(8,128)(2,1)}), bf16[2048,8192]{1,0:T(8,128)(2,1)}) %all-gather.27.cloned.1.call-update) | async-done | bytes 33554448 | tf_op jit(solution)/shard_map/all_gather | solution.py:194
  736.3 20.1 fusion.94
  756.4 142.6 %all-gather.29.cloned.1.call-done = bf16[8192,2048]{1,0:T(8,128)(2,1)} async-done(((bf16[1024,2048]{1,0:T(8,128)(2,1)}), bf16[8192,2048]{1,0:T(8,128)(2,1)}) %all-gather.29.cloned.1.call-update) | async-done | bytes 33554448 | tf_op jit(solution)/shard_map/all_gather | solution.py:217
  899.0 23.8 multiply_convert_fusion.3
  922.8 16.9 fusion.95
  939.7 19.7 multiply_reduce_fusion.2
  1038.9 21.4 copy.337
  1105.5 21.7 copy.339
  1127.3 12.9 copy.352
  1141.4 17.9 convolution_convert_fusion.1
  1159.3 16.9 convolution_convert_fusion.2
  1176.2 45.2 %pad_maximum_fusion = bf16[2048,16384]{1,0:T(8,128)(2,1)} fusion(bf16[2048,8192]{1,0:T(8,128)(2,1)} %convolution_convert_fusion.1, bf16[2048,8192]{1,0:T(8,128)(2,1)} %convolution_convert_fusion.2), kind=kLoop, calls=%fused_computation | loop fusion | flops 134217728 | bytes 134217728 | tf_op jit(solution)/shard_map/concatenate | solution.py:235
  1284.9 23.0 convolution_convert_fusion
  1307.9 298.9 %reduce-scatter.21.cloned.1.call-done = bf16[256,16384]{1,0:T(8,128)(2,1)} async-done(((bf16[2048,16384]{1,0:T(8,128)(2,1)}), bf16[256,16384]{1,0:T(8,128)(2,1)}) %reduce-scatter.21.cloned.1.call-update) | async-done | bytes 8388624 | tf_op jit(solution)/shard_map/reduce_scatter | solution.py:234
  1612.8 69.2 %reduce-scatter.13.cloned.1.call-done = bf16[256,2048]{1,0:T(8,128)(2,1)} async-done(((bf16[2048,2048]{1,0:T(8,128)(2,1)}), bf16[256,2048]{1,0:T(8,128)(2,1)}) %reduce-scatter.13.cloned.1.call-update) | async-done | bytes 1048592 | tf_op jit(solution)/shard_map/reduce_scatter | solution.py:332
  1682.0 75.0 %reduce-scatter.19.cloned.1.call-done = bf16[256,2048]{1,0:T(8,128)(2,1)} async-done(((bf16[2048,2048]{1,0:T(8,128)(2,1)}), bf16[256,2048]{1,0:T(8,128)(2,1)}) %reduce-scatter.19.cloned.1.call-update) | async-done | bytes 1048592 | tf_op jit(solution)/shard_map/reduce_scatter | solution.py:350
  1757.1 75.2 %reduce-scatter.15.cloned.1.call-done = bf16[256,2048]{1,0:T(8,128)(2,1)} async-done(((bf16[2048,2048]{1,0:T(8,128)(2,1)}), bf16[256,2048]{1,0:T(8,128)(2,1)}) %reduce-scatter.15.cloned.1.call-update) | async-done | bytes 1048592 | tf_op jit(solution)/shard_map/reduce_scatter | solution.py:338
  1832.3 75.6 %reduce-scatter.17.cloned.1.call-done = bf16[256,2048]{1,0:T(8,128)(2,1)} async-done(((bf16[2048,2048]{1,0:T(8,128)(2,1)}), bf16[256,2048]{1,0:T(8,128)(2,1)}) %reduce-scatter.17.cloned.1.call-update) | async-done | bytes 1048592 | tf_op jit(solution)/shard_map/reduce_scatter | solution.py:344
  1907.9 208.7 %reduce-scatter.23.cloned.1.call-done = bf16[1024,2048]{1,0:T(8,128)(2,1)} async-done(((bf16[8192,2048]{1,0:T(8,128)(2,1)}), bf16[1024,2048]{1,0:T(8,128)(2,1)}) %reduce-scatter.23.cloned.1.call-update) | async-done | bytes 4194320 | tf_op jit(solution)/shard_map/reduce_scatter | solution.py:222
  2125.7 17.7 fusion.16
  2155.3 25.5 all-reduce.3
  2198.7 490.2 %all-reduce.11.cloned.1.call-done = (bf16[256,2048]{1,0:T(8,128)(2,1)}, bf16[256,2048]{1,0:T(8,128)(2,1)}, bf16[256,2048]{1,0:T(8,128)(2,1)}, bf16[256,2048]{1,0...) async-done(((bf16[256,2048]{1,0:T(8,128)(2,1)}, bf16[256,2048]{1,0:T(8,128)(2,1)}, bf16[256,2048]{1,0:T(8,128)(2,1)}, ...) | async-done | bytes 16777232 | tf_op jit(solution)/shard_map/psum | solution.py:364
  (329 shorter events, 381.1 us)
Async XLA Ops:
  7.2 18.1 copy-start.13
  7.2 59.8 %all-gather.15.cloned.1.call-start = ((), (), s32[]{:S(2)}) async-start(), calls=%async_computation.9 | async-start | bytes 9437184 | tf_op jit(solution)/shard_map/all_gather | solution.py:91
  7.9 115.4 %all-gather.13.cloned.1.call-start = ((), (), s32[]{:S(2)}) async-start(), calls=%async_computation.8 | async-start | bytes 9437184 | tf_op jit(solution)/shard_map/all_gather | solution.py:90
  8.7 171.0 %all-gather.17.cloned.1.call-start = ((), (), s32[]{:S(2)}) async-start(), calls=%async_computation.11 | async-start | bytes 9437184 | tf_op jit(solution)/shard_map/all_gather | solution.py:89
  9.4 228.4 %all-reduce.9.cloned.1.call-start = ((), (), s32[]{:S(2)}) async-start(), calls=%async_computation.10 | async-start | bytes 1048576 | tf_op jit(solution)/shard_map/psum | solution.py:138
  25.3 212.5 %copy-start.60 = (f32[256]{0:T(256)}, f32[256]{0:T(256)S(1)}, u32[]{:S(2)}) copy-start(f32[256]{0:T(256)S(1)} %get-tuple-element.51) | copy-start | bytes 3076
  25.9 46.9 %copy-start.43 = (bf16[256,2048]{1,0:T(8,128)(2,1)}, bf16[256,2048]{1,0:T(8,128)(2,1)S(1)}, u32[]{:S(2)}) copy-start(bf16[256,2048]{1,0:T(8,128)(2,1)S(1)} %multiply_convert_fusion.9) | copy-start | bytes 3145732
  133.7 161.9 %all-gather.21.cloned.1.call-start = ((), (), s32[]{:S(2)}) async-start(), calls=%async_computation.13 | async-start | bytes 9437184 | tf_op jit(solution)/shard_map/all_gather | solution.py:115
  135.1 218.9 %all-gather.19.cloned.1.call-start = ((), (), s32[]{:S(2)}) async-start(), calls=%async_computation.12 | async-start | bytes 9437184 | tf_op jit(solution)/shard_map/all_gather | solution.py:118
  136.5 274.0 %all-gather.23.cloned.1.call-start = ((), (), s32[]{:S(2)}) async-start(), calls=%async_computation.14 | async-start | bytes 9437184 | tf_op jit(solution)/shard_map/all_gather | solution.py:178
  137.2 436.1 %all-gather.25.cloned.1.call-start = ((), (), s32[]{:S(2)}) async-start(), calls=%async_computation.15 | async-start | bytes 37748736 | tf_op jit(solution)/shard_map/all_gather | solution.py:193
  138.0 18.6 copy-start.64
  138.0 41.7 %copy-start.44 = (bf16[256,2048]{1,0:T(8,128)(2,1)S(1)}, bf16[256,2048]{1,0:T(8,128)(2,1)}, u32[]{:S(2)}) copy-start(bf16[256,2048]{1,0:T(8,128)(2,1)} %copy-done.43) | copy-start | bytes 3145732
  138.0 598.2 %all-gather.27.cloned.1.call-start = ((), (), s32[]{:S(2)}) async-start(), calls=%async_computation.16 | async-start | bytes 37748736 | tf_op jit(solution)/shard_map/all_gather | solution.py:194
  138.8 760.2 %all-gather.29.cloned.1.call-start = ((), (), s32[]{:S(2)}) async-start(), calls=%async_computation.17 | async-start | bytes 37748736 | tf_op jit(solution)/shard_map/all_gather | solution.py:217
  139.4 1114.3 %reduce-scatter.25.cloned.1.call-start = ((), (), s32[]{:S(2)}) async-start(), calls=%async_computation.24 | async-start | bytes 9437184
  185.4 52.4 %copy-start.41 = (bf16[256,2048]{1,0:T(8,128)(2,1)}, bf16[256,2048]{1,0:T(8,128)(2,1)S(1)}, u32[]{:S(2)}) copy-start(bf16[256,2048]{1,0:T(8,128)(2,1)S(1)} %convolution_convert_fusion.6) | copy-start | bytes 3145732
  203.9 39.2 %copy-start.50 = (f32[256,16]{0,1:T(8,128)}, f32[256,16]{0,1:T(8,128)S(1)}, u32[]{:S(2)}) copy-start(f32[256,16]{0,1:T(8,128)S(1)} %fusion.59) | copy-start | bytes 49156
  354.0 14.3 slice-start
  418.3 318.0 %copy-start.19 = (bf16[256,2048]{1,0:T(8,128)(2,1)}, bf16[256,2048]{1,0:T(8,128)(2,1)S(1)}, u32[]{:S(2)}) copy-start(bf16[256,2048]{1,0:T(8,128)(2,1)S(1)} %multiply_convert_fusion.8) | copy-start | bytes 3145732
  939.7 19.7 copy-start.35
  1072.5 196.2 %reduce-scatter.27.cloned.1.call-start = ((), (), s32[]{:S(2)}) async-start(), calls=%async_computation.25 | async-start | bytes 9437184
  1073.0 19.1 slice-start.4
  1140.2 466.7 %reduce-scatter.21.cloned.1.call-start = ((), (), s32[]{:S(2)}) async-start(), calls=%async_computation.22 | async-start | bytes 75497472 | tf_op jit(solution)/shard_map/reduce_scatter | solution.py:234
  1221.5 460.5 %reduce-scatter.13.cloned.1.call-start = ((), (), s32[]{:S(2)}) async-start(), calls=%async_computation.18 | async-start | bytes 9437184 | tf_op jit(solution)/shard_map/reduce_scatter | solution.py:332
  1243.3 513.7 %reduce-scatter.19.cloned.1.call-start = ((), (), s32[]{:S(2)}) async-start(), calls=%async_computation.21 | async-start | bytes 9437184 | tf_op jit(solution)/shard_map/reduce_scatter | solution.py:350
  1253.6 578.7 %reduce-scatter.15.cloned.1.call-start = ((), (), s32[]{:S(2)}) async-start(), calls=%async_computation.19 | async-start | bytes 9437184 | tf_op jit(solution)/shard_map/reduce_scatter | solution.py:338
  1268.5 639.4 %reduce-scatter.17.cloned.1.call-start = ((), (), s32[]{:S(2)}) async-start(), calls=%async_computation.20 | async-start | bytes 9437184 | tf_op jit(solution)/shard_map/reduce_scatter | solution.py:344
  1283.5 833.0 %reduce-scatter.23.cloned.1.call-start = ((), (), s32[]{:S(2)}) async-start(), calls=%async_computation.23 | async-start | bytes 37748736 | tf_op jit(solution)/shard_map/reduce_scatter | solution.py:222
  1307.9 1381.0 %all-reduce.11.cloned.1.call-start = ((), (), s32[]{:S(2)}) async-start(), calls=%async_computation.26 | async-start | bytes 33554432 | tf_op jit(solution)/shard_map/psum | solution.py:364
  2125.7 17.7 copy-start.21
  2125.7 18.0 copy-start.22
  (67 other events, 321.0 us)
Sparse Core Ops, SparseCore 0:
  9.9 57.0 all-gather.14
  68.9 54.3 all-gather.12
  125.2 54.3 all-gather.16
  183.2 54.5 all-reduce.8
  240.3 55.2 all-gather.20
  298.0 55.9 all-gather.18
  356.1 54.3 all-gather.22
  412.5 160.8 all-gather.24
  575.4 160.7 all-gather.26
  738.1 160.7 all-gather.28
  1072.6 71.2 reduce-scatter.24
  1147.8 71.2 reduce-scatter.26
  1223.1 383.7 reduce-scatter.20
  1610.7 71.2 reduce-scatter.12
  1685.7 71.2 reduce-scatter.18
  1760.9 71.2 reduce-scatter.14
  1836.5 71.2 reduce-scatter.16
  1911.3 205.2 reduce-scatter.22
  2120.4 568.5 all-reduce.10
where the time goes:
time: 2730 us; the launch traced here: 2720 us
  waiting for transfers between devices  2010 us (74%)
  matrix products  364 us (13%)
  local copies, waits for them, and re-layouts  131 us (5%)
  other arithmetic  116 us (4%)
  blocking collectives  78.5 us (3%)
    psum x1, waiting for transfers between devices, shards(): lax.psum(scattered[0].astype(jnp.bfloat16), 'seq').astype(jnp.float32)  490 us
    reduce_scatter x1, waiting for transfers between devices, shards(): lax.psum_scatter(jnp.concatenate([contract_first(left_rows, d_gate), cont...  299 us
    reduce_scatter x1, waiting for transfers between devices, shards(): lax.psum_scatter(contract_first(inner_rows, grad_rows).astype(jnp.bfloat1...  209 us
    all_gather x1, waiting for transfers between devices, shards(): lax.all_gather(w_gate, 'fsdp', axis=0, tiled=True)  155 us
    all_gather x1, waiting for transfers between devices, shards(): lax.all_gather(w_up, 'fsdp', axis=0, tiled=True)  143 us
    all_gather x1, waiting for transfers between devices, shards(): weight_piece = lax.all_gather(w_down, 'fsdp', axis=0, tiled=True)  143 us
    unnamed x175, local copies, waits for them, and re-layouts  99.5 us
    dot_general x7, matrix products, contract_first(): lax.dot_general(left_side, right_side, (((0,), (0,)), ((), ())), preferre...  89.8 us
  transfers between devices with their start and end apart: 19, of which 17 were waited for; matrix products, arithmetic and copies ran while one was open for 15% of the time, Pallas kernels for 0%

commit v1 on v0

v1 whole, which is shorter than its diff:
```python
import functools

import jax
import jax.numpy as jnp
from jax import lax
from jax.experimental import pallas as pl
from jax.experimental.pallas import tpu as pltpu
from jax.sharding import PartitionSpec as P

HEADS = 16
HEAD_DIM = 128
NSEG = 2

highest = lax.Precision.HIGHEST
norm_eps = 1e-05
f32 = jnp.float32
bf16 = jnp.bfloat16


def doc_number(start_row, places):
    return jnp.sum((start_row[None, :] <= places[:, None]).astype(jnp.int32), axis=1) - 1


def norm_back(grad_in, normed, inverse):
    return inverse * (grad_in - normed * jnp.mean(grad_in * normed, axis=-1, keepdims=True))


def mm(a, b):
    return lax.dot_general(a, b, (((1,), (0,)), ((), ())), preferred_element_type=f32)


def mm_t(a, b):
    return lax.dot_general(a, b, (((1,), (1,)), ((), ())), preferred_element_type=f32)


def t_mm(a, b):
    return lax.dot_general(a, b, (((0,), (0,)), ((), ())), preferred_element_type=f32)


def dots(a, b, ca, cb, precision=None):
    return lax.dot_general(a, b, (((ca,), (cb,)), ((), ())), preferred_element_type=f32, precision=precision)


def phi(u):
    return jnp.where(u > 0, u + 1.0, jnp.exp(jnp.minimum(u, 0.0)))


def phi_slope(u):
    return jnp.where(u > 0, 1.0, jnp.exp(jnp.minimum(u, 0.0)))


def attention_kernel(heads, qkv_ref, doc_col, doc_row, side_ref, blend_ref, mixed_ref, diff_ref, lse_ref, mem_ref, nv_ref):
    n, _, rows, _ = qkv_ref.shape
    length = n * rows
    cw = heads * HEAD_DIM
    take = max(1, 256 // rows)
    block = take * rows
    scale = HEAD_DIM ** (-0.5)
    segment = pl.program_id(0)

    def part(kind, h, lo, hi):
        cols = slice(kind * cw + h * HEAD_DIM, kind * cw + (h + 1) * HEAD_DIM)
        return qkv_ref[lo:hi, 0, :, cols].reshape((hi - lo) * rows, HEAD_DIM)

    for h in range(heads):
        cols = slice(h * HEAD_DIM, (h + 1) * HEAD_DIM)

        @pl.when(segment == 0)
        def _():
            fk = phi(part(1, h, 0, n).astype(f32)) * side_ref[0]
            mem_ref[h] = dots(fk, part(2, h, 0, n).astype(f32), 0, 0, highest)
            nv_ref[h] = jnp.sum(fk, axis=0, keepdims=True)

        blend = blend_ref[:, cols]
        for i in range(n // take):
            lo, hi = i * take, (i + 1) * take
            span = (i + 1) * block
            q = part(0, h, lo, hi)
            s = dots(q, part(1, h, 0, hi), 1, 1) * scale
            at = lax.broadcasted_iota(jnp.int32, (block, span), 0) + i * block
            allowed = (lax.broadcasted_iota(jnp.int32, (block, span), 1) <= at) & (
                doc_row[0, :, :span] == doc_col[0, i * block : (i + 1) * block]
            )
            s = jnp.where(allowed, s, -1000000000.0)
            top = jnp.max(s, axis=1, keepdims=True)
            p = jnp.exp(s - top)
            tot = jnp.sum(p, axis=1, keepdims=True)
            lse_ref[h, 0, i * block : (i + 1) * block] = top + jnp.log(tot)
            direct = dots((p / tot).astype(bf16), part(2, h, 0, hi), 1, 0)
            shape = (take, rows, HEAD_DIM)

            @pl.when(segment == 0)
            def _():
                mixed_ref[lo:hi, 0, :, cols] = ((1.0 - blend) * direct).astype(bf16).reshape(shape)
                diff_ref[lo:hi, 0, :, cols] = (-direct).reshape(shape)

            @pl.when(segment != 0)
            def _():
                fq = phi(q.astype(f32))
                numer = dots(fq, mem_ref[h], 1, 0, highest)
                den = jnp.sum(fq * nv_ref[h], axis=1, keepdims=True) + 1.0
                ret = side_ref[0, i * block : (i + 1) * block] * numer / den
                mixed_ref[lo:hi, 0, :, cols] = (blend * ret + (1.0 - blend) * direct).astype(bf16).reshape(shape)
                diff_ref[lo:hi, 0, :, cols] = (ret - direct).reshape(shape)


def attention_back_kernel(
    heads, qkv_ref, dmix_ref, diff_ref, lse_ref, doc_col, doc_row, side_ref, blend_ref, mem_ref, nv_ref,
    out_ref, bias_ref, dk_acc, dv_acc, dmem, dnv,
):
    n, _, rows, _ = qkv_ref.shape
    length = n * rows
    cw = heads * HEAD_DIM
    take = max(1, 256 // rows)
    block = take * rows
    scale = HEAD_DIM ** (-0.5)
    step = pl.program_id(0)
    shape = (take, rows, HEAD_DIM)

    def part(kind, h, lo, hi):
        cols = slice(kind * cw + h * HEAD_DIM, kind * cw + (h + 1) * HEAD_DIM)
        return qkv_ref[lo:hi, 0, :, cols].reshape((hi - lo) * rows, HEAD_DIM)

    @pl.when(step == 0)
    def _():
        bias_ref[...] = jnp.zeros_like(bias_ref)
        dmem[...] = jnp.zeros_like(dmem)
        dnv[...] = jnp.zeros_like(dnv)

    for h in range(heads):
        cols = slice(h * HEAD_DIM, (h + 1) * HEAD_DIM)
        blend = blend_ref[:, cols]
        dk_acc[...] = jnp.zeros_like(dk_acc)
        dv_acc[...] = jnp.zeros_like(dv_acc)
        for i in range(n // take):
            lo, hi = i * take, (i + 1) * take
            span = (i + 1) * block
            here = slice(i * block, (i + 1) * block)
            q, k, v = part(0, h, lo, hi), part(1, h, 0, hi), part(2, h, 0, hi)
            dmix = dmix_ref[lo:hi, 0, :, cols].reshape(block, HEAD_DIM)
            bias_ref[:, cols] += jnp.sum(dmix * diff_ref[lo:hi, 0, :, cols].reshape(block, HEAD_DIM), axis=0, keepdims=True)
            ddir = ((1.0 - blend) * dmix).astype(bf16)
            s = dots(q, k, 1, 1) * scale
            at = lax.broadcasted_iota(jnp.int32, (block, span), 0) + i * block
            allowed = (lax.broadcasted_iota(jnp.int32, (block, span), 1) <= at) & (
                doc_row[0, :, :span] == doc_col[0, here]
            )
            e = jnp.exp(jnp.where(allowed, s, -1000000000.0) - lse_ref[h, 0, here])
            dp = dots(ddir, v, 1, 1)
            bal = jnp.sum(e * dp, axis=1, keepdims=True)
            ds = (e * (dp - bal)).astype(bf16)
            dv_acc[:span] += dots(e.astype(bf16), ddir, 0, 0)
            dk_acc[:span] += dots(ds, q, 0, 0) * scale
            dq = dots(ds, k, 1, 0) * scale

            @pl.when(step != 0)
            def _():
                out_ref[lo:hi, 0, :, cols] = dq.astype(bf16).reshape(shape)

            @pl.when(step == 0)
            def _():
                q32 = q.astype(f32)
                fq = phi(q32)
                numer = dots(fq, mem_ref[h], 1, 0, highest)
                den = jnp.sum(fq * nv_ref[h], axis=1, keepdims=True) + 1.0
                dnum = side_ref[0, here] * (blend * dmix) / den
                dden = -jnp.sum(dnum * numer, axis=1, keepdims=True) / den
                dmem[h] += dots(fq, dnum, 0, 0, highest)
                dnv[h] += jnp.sum(dden * fq, axis=0, keepdims=True)
                dfq = dots(dnum, mem_ref[h], 1, 1, highest) + dden * nv_ref[h]
                out_ref[lo:hi, 0, :, cols] = (dq + dfq * phi_slope(q32)).astype(bf16).reshape(shape)

        whole = (n, rows, HEAD_DIM)
        kcols = slice(cw + h * HEAD_DIM, cw + (h + 1) * HEAD_DIM)
        vcols = slice(2 * cw + h * HEAD_DIM, 2 * cw + (h + 1) * HEAD_DIM)

        @pl.when(step == 0)
        def _():
            out_ref[:, 0, :, kcols] = dk_acc[...].astype(bf16).reshape(whole)
            out_ref[:, 0, :, vcols] = dv_acc[...].astype(bf16).reshape(whole)

        @pl.when(step != 0)
        def _():
            k32 = part(1, h, 0, n).astype(f32)
            v32 = part(2, h, 0, n).astype(f32)
            key_set = side_ref[0]
            mem_v = key_set * dots(phi(k32), dmem[h], 1, 0, highest)
            mem_k = key_set * (dots(v32, dmem[h], 1, 1, highest) + dnv[h]) * phi_slope(k32)
            out_ref[:, 0, :, kcols] = (dk_acc[...] + mem_k).astype(bf16).reshape(whole)
            out_ref[:, 0, :, vcols] = (dv_acc[...] + mem_v).astype(bf16).reshape(whole)


def attention_specs(n, rows, heads, pick):
    length = n * rows
    cw = heads * HEAD_DIM
    wide = pl.BlockSpec((n, 1, rows, 3 * cw), lambda g: (0, pick(g), 0, 0))
    narrow = pl.BlockSpec((n, 1, rows, cw), lambda g: (0, pick(g), 0, 0))
    lse = pl.BlockSpec((heads, 1, length, 1), lambda g: (0, pick(g), 0, 0))
    col = pl.BlockSpec((1, length, 1), lambda g: (pick(g), 0, 0))
    row = pl.BlockSpec((1, 1, length), lambda g: (pick(g), 0, 0))
    line = pl.BlockSpec((1, cw), lambda g: (0, 0))
    mem = pl.BlockSpec((heads, HEAD_DIM, HEAD_DIM), lambda g: (0, 0, 0))
    nv = pl.BlockSpec((heads, 1, HEAD_DIM), lambda g: (0, 0, 0))
    return wide, narrow, lse, col, row, line, mem, nv


def attention(qkv, doc_col, doc_row, side, blend, heads):
    n, _, rows, _ = qkv.shape
    length = n * rows
    cw = heads * HEAD_DIM
    wide, narrow, lse, col, row, line, mem, nv = attention_specs(n, rows, heads, lambda g: g)
    pairs = heads * NSEG * length * length // 2
    return pl.pallas_call(
        functools.partial(attention_kernel, heads),
        grid=(NSEG,),
        in_specs=[wide, col, row, col, line],
        out_specs=[narrow, narrow, lse, mem, nv],
        out_shape=[
            jax.ShapeDtypeStruct((n, NSEG, rows, cw), bf16),
            jax.ShapeDtypeStruct((n, NSEG, rows, cw), f32),
            jax.ShapeDtypeStruct((heads, NSEG, length, 1), f32),
            jax.ShapeDtypeStruct((heads, HEAD_DIM, HEAD_DIM), f32),
            jax.ShapeDtypeStruct((heads, 1, HEAD_DIM), f32),
        ],
        compiler_params=pltpu.CompilerParams(vmem_limit_bytes=48 << 20),
        cost_estimate=pl.CostEstimate(flops=pairs * 4 * HEAD_DIM, transcendentals=pairs, bytes_accessed=8 << 20),
        name="attention",
    )(qkv, doc_col, doc_row, side, blend)


def attention_back(qkv, dmix, diff, lse_rows, doc_col, doc_row, side, blend, mem_all, nv_all, heads):
    n, _, rows, _ = qkv.shape
    length = n * rows
    cw = heads * HEAD_DIM
    wide, narrow, lse, col, row, line, mem, nv = attention_specs(n, rows, heads, lambda g: NSEG - 1 - g)
    pairs = heads * NSEG * length * length // 2
    return pl.pallas_call(
        functools.partial(attention_back_kernel, heads),
        grid=(NSEG,),
        in_specs=[wide, narrow, narrow, lse, col, row, col, line, mem, nv],
        out_specs=[wide, line],
        out_shape=[
            jax.ShapeDtypeStruct((n, NSEG, rows, 3 * cw), bf16),
            jax.ShapeDtypeStruct((1, cw), f32),
        ],
        scratch_shapes=[
            pltpu.VMEM((length, HEAD_DIM), f32),
            pltpu.VMEM((length, HEAD_DIM), f32),
            pltpu.VMEM((heads, HEAD_DIM, HEAD_DIM), f32),
            pltpu.VMEM((heads, 1, HEAD_DIM), f32),
        ],
        compiler_params=pltpu.CompilerParams(vmem_limit_bytes=56 << 20),
        cost_estimate=pl.CostEstimate(flops=pairs * 10 * HEAD_DIM, transcendentals=pairs, bytes_accessed=16 << 20),
        name="attention_back",
    )(qkv, dmix, diff, lse_rows, doc_col, doc_row, side, blend, mem_all, nv_all)


def flip(index, bit):
    return index + bit - 2 * bit * lax.rem(lax.div(index, bit), 2)


def send(src, dst, sems, slot, peer):
    return pltpu.make_async_remote_copy(
        src_ref=src, dst_ref=dst, send_sem=sems[0].at[slot], recv_sem=sems[1].at[slot],
        device_id={"fsdp": peer}, device_id_type=pl.DeviceIdType.MESH,
    )


def greet(peers):
    barrier = pltpu.get_barrier_semaphore()
    for peer in peers:
        pl.semaphore_signal(barrier, inc=1, device_id={"fsdp": peer}, device_id_type=pl.DeviceIdType.MESH)
    pl.semaphore_wait(barrier, len(peers))


PIECES = 4


def gather_kernel(x_ref, out_ref, local_sem, *sems):
    me = lax.axis_index("fsdp")
    sib, xn, yn = flip(me, 1), flip(me, 2), flip(me, 4)
    rows = x_ref.shape[0] // PIECES
    own, over_x, over_y, far = sems[0:2], sems[2:4], sems[4:6], sems[6:8]
    side_x, side_y, side_far = sems[8:10], sems[10:12], sems[12:14]
    greet([sib, xn, yn])

    def at(owner, c):
        return out_ref.at[owner, pl.ds(c * rows, rows)]

    def mine(c):
        return x_ref.at[pl.ds(c * rows, rows)]

    half = PIECES // 2
    started = []

    def go(copy):
        copy.start()
        started.append(copy)

    for j in range(PIECES):
        c, d = j, (j + half) % PIECES
        go(send(mine(c), at(me, c), over_x, c, xn))
        go(send(mine(d), at(me, d), over_y, d, yn))
    for c in range(PIECES):
        go(send(mine(c), at(me, c), own, c, sib))
    local = pltpu.make_async_copy(x_ref, out_ref.at[me], local_sem)
    local.start()
    x_owner, y_owner, far_owner = xn, yn, flip(xn, 4)
    for j in range(PIECES):
        c, d = j, (j + half) % PIECES
        send(at(x_owner, c), at(x_owner, c), over_x, c, xn).wait_recv()
        if c < half:
            go(send(at(x_owner, c), at(x_owner, c), far, c, yn))
        go(send(at(x_owner, c), at(x_owner, c), side_x, c, sib))
        send(at(y_owner, d), at(y_owner, d), over_y, d, yn).wait_recv()
        if d >= half:
            go(send(at(y_owner, d), at(y_owner, d), far, d, xn))
        go(send(at(y_owner, d), at(y_owner, d), side_y, d, sib))
    for j in range(half):
        for c in (j, j + half):
            send(at(far_owner, c), at(far_owner, c), far, c, yn).wait_recv()
            go(send(at(far_owner, c), at(far_owner, c), side_far, c, sib))
    for c in range(PIECES):
        for owner, pair in ((sib, own), (flip(sib, 2), side_x), (flip(sib, 4), side_y), (flip(far_owner, 1), side_far)):
            send(at(owner, c), at(owner, c), pair, c, sib).wait_recv()
    for copy in started:
        copy.wait_send()
    local.wait()


def gather(x, collective_id):
    n = lax.axis_size("fsdp")
    if n != 8:
        return lax.all_gather(x, "fsdp", axis=0)
    return pl.pallas_call(
        gather_kernel,
        in_specs=[pl.BlockSpec(memory_space=pl.ANY)],
        out_specs=pl.BlockSpec(memory_space=pl.ANY),
        out_shape=jax.ShapeDtypeStruct((n, *x.shape), x.dtype),
        scratch_shapes=[pltpu.SemaphoreType.DMA] + [pltpu.SemaphoreType.DMA((PIECES,))] * 14,
        compiler_params=pltpu.CompilerParams(collective_id=collective_id, has_side_effects=True),
        name="gather",
    )(x)


OWN, ACROSS_X, ACROSS_Y, FAR = 0, 1, 2, 3


def scatter_kernel(p_ref, out_ref, part, side, near, last, load_sems, *sems):
    me = lax.axis_index("fsdp")
    sib, xn, yn = flip(me, 1), flip(me, 2), flip(me, 4)
    dest = [me, xn, yn, flip(xn, 4)]
    rows = out_ref.shape[0] // PIECES
    half = PIECES // 2
    core = sems[0:2]
    hop = {"xf": sems[2:4], "xo": sems[4:6], "yf": sems[6:8], "yo": sems[8:10], "last": sems[10:12]}
    order = (FAR, ACROSS_X, ACROSS_Y, OWN)
    loads = [pltpu.make_async_copy(p_ref.at[dest[kind]], part.at[kind], load_sems.at[kind]) for kind in range(4)]
    for kind in order:
        loads[kind].start()
    greet([sib, xn, yn])
    started = []

    def go(copy):
        copy.start()
        started.append(copy)

    for kind in order:
        go(send(p_ref.at[flip(dest[kind], 1)], side.at[kind], core, kind, sib))

    def span(c):
        return pl.ds(c * rows, rows)

    def add(kind, c, other):
        part[kind, span(c)] = (part[kind, span(c)].astype(f32) + other.astype(f32)).astype(bf16)

    for kind in order:
        loads[kind].wait()
        send(side.at[kind], side.at[kind], core, kind, sib).wait_recv()
        for j in range(PIECES):
            add(kind, j, side[kind, span(j)])
            mine = part.at[kind, span(j)]
            if kind == FAR:
                if j < half:
                    go(send(mine, near.at[0, span(j)], hop["xf"], j, xn))
                else:
                    go(send(mine, near.at[0, span(j)], hop["yf"], j, yn))
            if kind == ACROSS_X and j < half:
                go(send(mine, near.at[1, span(j)], hop["xo"], j, xn))
            if kind == ACROSS_Y and j >= half:
                go(send(mine, near.at[1, span(j)], hop["yo"], j, yn))
    for j in range(half):
        for c in (j, j + half):
            kind, came, onward, to = (ACROSS_Y, "xf", yn, xn) if c < half else (ACROSS_X, "yf", xn, yn)
            send(near.at[0, span(c)], near.at[0, span(c)], hop[came], c, to).wait_recv()
            add(kind, c, near[0, span(c)])
            go(send(part.at[kind, span(c)], last.at[span(c)], hop["last"], c, onward))
    for j in range(half):
        for c in (j, j + half):
            send(near.at[1, span(c)], near.at[1, span(c)], hop["xo" if c < half else "yo"], c, xn).wait_recv()
            send(last.at[span(c)], last.at[span(c)], hop["last"], c, xn).wait_recv()
            out_ref[span(c)] = (
                part[OWN, span(c)].astype(f32) + near[1, span(c)].astype(f32) + last[span(c)].astype(f32)
            )
    for copy in started:
        copy.wait_send()


def scatter(x, collective_id):
    n, rows, columns = x.shape
    if n != 8:
        return lax.psum_scatter(x, "fsdp", scatter_dimension=0).astype(f32)
    sems = [4, 4] + [PIECES] * 10
    return pl.pallas_call(
        scatter_kernel,
        in_specs=[pl.BlockSpec(memory_space=pl.ANY)],
        out_specs=pl.BlockSpec(memory_space=pltpu.VMEM),
        out_shape=jax.ShapeDtypeStruct((rows, columns), f32),
        scratch_shapes=[
            pltpu.VMEM((4, rows, columns), bf16),
            pltpu.VMEM((4, rows, columns), bf16),
            pltpu.VMEM((2, rows, columns), bf16),
            pltpu.VMEM((rows, columns), bf16),
            pltpu.SemaphoreType.DMA((4,)),
        ]
        + [pltpu.SemaphoreType.DMA((k,)) for k in sems],
        compiler_params=pltpu.CompilerParams(
            collective_id=collective_id, has_side_effects=True, vmem_limit_bytes=40 << 20
        ),
        name="scatter",
    )(x)


def other(index, bits):
    for bit in (1, 2, 4):
        if bits & bit:
            index = flip(index, bit)
    return index


def link(src, dst, sems, slot, axis, peer):
    return pltpu.make_async_remote_copy(
        src_ref=src, dst_ref=dst, send_sem=sems[0].at[slot], recv_sem=sems[1].at[slot],
        device_id={axis: peer}, device_id_type=pl.DeviceIdType.MESH,
    )


ORDER = (0, 1, 2, 4, 3, 5, 6, 7)
SLOTS = 4


def chunks_of(still, moved):
    out = []
    for t, rows in enumerate(still):
        out += [(t, None, r, 128) for r in range(0, rows, 128)]
    for t, (rows, size) in enumerate(moved):
        out += [(len(still) + t, d, r, size) for d in ORDER for r in range(0, rows, size)]
    return out


def line_kernel(still, moved, *refs):
    kinds = len(still) + len(moved)
    ins, refs = refs[:kinds], refs[kinds:]
    outs, refs = refs[:kinds], refs[kinds:]
    first, refs = refs[:kinds], refs[kinds:]
    second, refs = refs[:kinds], refs[kinds:]
    come, refs = refs[: len(moved)], refs[len(moved) :]
    g_buf, a_buf, t_buf, b_buf, u_buf, loads, stores, *sems = refs
    move = [sems[2 * t : 2 * t + 2] for t in range(len(moved))]
    sems = sems[2 * len(moved) :]
    go_in, cross, back = sems[0:2], sems[2:4], sems[4:6]
    me, place = lax.axis_index("fsdp"), lax.axis_index("seq")
    is_end = (place == 0) | (place == 3)
    chunks = chunks_of(still, moved)
    inward = jnp.where(place < 2, 1, 2)
    outward = jnp.where(place < 2, 0, 3)
    opposite = 3 - inward
    barrier = pltpu.get_barrier_semaphore()
    for d in range(1, 8):
        pl.semaphore_signal(barrier, inc=1, device_id={"fsdp": other(me, d)}, device_id_type=pl.DeviceIdType.MESH)

    @pl.when(is_end)
    def _():
        pl.semaphore_signal(barrier, inc=1, device_id={"seq": inward}, device_id_type=pl.DeviceIdType.MESH)
        pl.semaphore_wait(barrier, 8)

    @pl.when(jnp.logical_not(is_end))
    def _():
        for peer in (outward, opposite):
            pl.semaphore_signal(barrier, inc=1, device_id={"seq": peer}, device_id_type=pl.DeviceIdType.MESH)
        pl.semaphore_wait(barrier, 9)

    def moving(t, d):
        ref = ins[len(still) + t]
        return link(ref.at[other(me, d)], come[t].at[me], move[t], d, "fsdp", other(me, d))

    def arrival(t, d):
        owner = other(me, d)
        return link(come[t].at[owner], come[t].at[owner], move[t], d, "fsdp", owner)

    plan = [(t, d) for t in range(len(moved)) for d in ORDER[1:]]
    begun = []

    def feed(count):
        while plan and count:
            t, d = plan.pop(0)
            moving(t, d).start()
            begun.append((t, d))
            count -= 1

    def view(refs, k):
        t, d, r, rows = chunks[k]
        if d is None:
            return refs[t].at[pl.ds(r, rows)]
        return refs[t].at[other(me, d), pl.ds(r, rows)]

    def source(k):
        t, d, r, rows = chunks[k]
        if d is None:
            return ins[t].at[pl.ds(r, rows)]
        if d == 0:
            return ins[t].at[me, pl.ds(r, rows)]
        return come[t - len(still)].at[other(me, d), pl.ds(r, rows)]

    def await_source(k):
        t, d, r, rows = chunks[k]
        if d and r == 0:
            arrival(t - len(still), d).wait_recv()

    def box(buf, k, depth):
        t, d, r, rows = chunks[k]
        return buf.at[k % depth, pl.ds(0, rows), pl.ds(0, ins[t].shape[-1])]

    def add(dst, left, right):
        rows = dst.shape[0]

        def body(i, _):
            here = pl.ds(pl.multiple_of(i * 16, 16), 16)
            dst[here] = (left[here].astype(f32) + right[here].astype(f32)).astype(bf16)
            return 0

        lax.fori_loop(0, rows // 16, body, 0)

    def end_send(k):
        return link(source(k), view(first, k), go_in, k, "seq", inward)

    def mid_cross(k):
        return link(box(t_buf, k, SLOTS), view(second, k), cross, k, "seq", opposite)

    def mid_back(k):
        return link(box(u_buf, k, SLOTS), view(outs, k), back, k, "seq", outward)

    def store(k):
        return pltpu.make_async_copy(box(u_buf, k, SLOTS), view(outs, k), stores.at[k % SLOTS])

    def finish(k):
        link(view(second, k), view(second, k), cross, k, "seq", opposite).wait_recv()
        load = pltpu.make_async_copy(view(second, k), box(b_buf, k, 2), loads.at[2])
        load.start()
        if k >= SLOTS:
            mid_back(k - SLOTS).wait_send()
            store(k - SLOTS).wait()
        load.wait()
        add(box(u_buf, k, SLOTS), box(t_buf, k, SLOTS), box(b_buf, k, 2))
        mid_back(k).start()
        store(k).start()

    count = len(chunks)
    feed(3)
    for k in range(count):
        if k % 2 == 1:
            feed(1)
        await_source(k)

        @pl.when(is_end)
        def _():
            end_send(k).start()

        @pl.when(jnp.logical_not(is_end))
        def _():
            own = pltpu.make_async_copy(source(k), box(g_buf, k, 2), loads.at[0])
            own.start()
            link(view(first, k), view(first, k), go_in, k, "seq", outward).wait_recv()
            got = pltpu.make_async_copy(view(first, k), box(a_buf, k, 2), loads.at[1])
            got.start()
            if k >= SLOTS:
                mid_cross(k - SLOTS).wait_send()
            own.wait()
            got.wait()
            add(box(t_buf, k, SLOTS), box(g_buf, k, 2), box(a_buf, k, 2))
            mid_cross(k).start()
            if k >= 1:
                finish(k - 1)

    @pl.when(is_end)
    def _():
        for k in range(count):
            link(view(outs, k), view(outs, k), back, k, "seq", inward).wait_recv()
            end_send(k).wait_send()

    @pl.when(jnp.logical_not(is_end))
    def _():
        finish(count - 1)
        for k in range(max(0, count - SLOTS), count):
            mid_cross(k).wait_send()
            mid_back(k).wait_send()
            store(k).wait()

    for t, d in begun:
        moving(t, d).wait_send()


def line_sum(still, moved, collective_id):
    if lax.axis_size("seq") != 4 or lax.axis_size("fsdp") != 8:
        swapped = [lax.all_to_all(x, "fsdp", split_axis=0, concat_axis=0, tiled=True) for x in moved]
        return [lax.psum(x, "seq") for x in still], [lax.psum(x, "seq") for x in swapped]
    still_rows = [x.shape[0] for x in still]
    moved_rows = [(x.shape[1], 128 if x.shape[2] > 1024 else 256) for x in moved]
    arrays = [*still, *moved]
    shapes = [jax.ShapeDtypeStruct(x.shape, bf16) for x in arrays]
    count = len(chunks_of(still_rows, moved_rows))
    rows = max([128] + [size for _, size in moved_rows])
    width = max(x.shape[-1] for x in arrays)
    anywhere = pl.BlockSpec(memory_space=pl.ANY)
    outs = pl.pallas_call(
        functools.partial(line_kernel, still_rows, moved_rows),
        in_specs=[anywhere] * len(arrays),
        out_specs=[anywhere] * (3 * len(arrays) + len(moved)),
        out_shape=shapes * 3 + shapes[len(still) :],
        scratch_shapes=[pltpu.VMEM((depth, rows, width), bf16) for depth in (2, 2, SLOTS, 2, SLOTS)]
        + [pltpu.SemaphoreType.DMA((3,)), pltpu.SemaphoreType.DMA((SLOTS,))]
        + [pltpu.SemaphoreType.DMA((8,))] * (2 * len(moved))
        + [pltpu.SemaphoreType.DMA((count,))] * 6,
        compiler_params=pltpu.CompilerParams(
            collective_id=collective_id, has_side_effects=True, vmem_limit_bytes=40 << 20
        ),
        name="line_sum",
    )(*arrays)
    return outs[: len(still)], outs[len(still) : len(arrays)]


def to_columns(weights, n):
    rows, cols = weights[0].shape
    parts = jnp.stack([w.reshape(rows, n, cols // n) for w in weights], axis=2)
    parts = parts.reshape(rows, n, len(weights) * (cols // n))
    out = lax.all_to_all(parts, "fsdp", split_axis=1, concat_axis=0, tiled=True)
    return out.reshape(n * rows, len(weights) * (cols // n))


def to_columns_in_turns(weights, n):
    s = lax.axis_size("seq")
    share = weights[0].shape[0] // s
    first = lax.axis_index("seq") * share
    part = to_columns([lax.dynamic_slice_in_dim(w, first, share, 0) for w in weights], n)
    part = part.reshape(n, share, part.shape[1])
    return lax.all_gather(part, "seq", axis=1, tiled=True).reshape(n * share * s, part.shape[2])


def to_rows(parts, count):
    n, rows, c = parts.shape
    parts = parts.reshape(n, rows, count, c // count).astype(f32)
    return [parts[:, :, i].transpose(1, 0, 2).reshape(rows, n * (c // count)) for i in range(count)]


def shards(
    tokens,
    doc_starts,
    norm_in,
    w_query,
    w_key,
    w_value,
    mix_bias,
    w_out,
    norm_mid,
    w_gate,
    w_up,
    w_down,
    cotangent,
):
    rows = tokens.shape[2]
    width = tokens.shape[3]
    n = lax.axis_size("fsdp")
    s = lax.axis_size("seq")
    own = NSEG * rows
    total = n * own
    seg_len = rows * n
    heads = HEADS // n
    cw = heads * HEAD_DIM
    fw = w_gate.shape[1] // n

    gains = lax.all_gather(jnp.stack([norm_in, norm_mid]), "fsdp", axis=1, tiled=True)
    gain_in, gain_mid = gains[0][None], gains[1][None]
    wqkv = to_columns([w_query, w_key, w_value], n)
    wgu = to_columns_in_turns([w_gate, w_up], n)

    flat_in = tokens.reshape(own, width).astype(f32)
    inv_in = lax.rsqrt(jnp.mean(flat_in * flat_in, axis=1, keepdims=True) + norm_eps)
    normed_in = flat_in * inv_in
    h_in = gather((normed_in * gain_in).astype(bf16), 0).reshape(total, width)
    dy = lax.all_gather(cotangent.reshape(own, width), "fsdp", axis=0, tiled=True)

    qkv = mm(h_in, wqkv).astype(bf16)

    qkv = qkv.reshape(n, NSEG, rows, 3 * cw)
    start_row = doc_starts[0]
    docs = doc_number(start_row, jnp.arange(NSEG * seg_len, dtype=jnp.int32)).reshape(NSEG, seg_len)
    side = (docs == docs[1, 0]).astype(f32)[:, :, None]
    doc_col, doc_row = docs[:, :, None], docs[:, None, :]
    blend = jax.nn.sigmoid(mix_bias)
    blend_row = jnp.repeat(blend, HEAD_DIM)[None]
    mixed, diff, lse, memory, norm_vec = attention(qkv, doc_col, doc_row, side, blend_row, heads)
    mixed = mixed.reshape(total, cw)

    attn_sum = scatter(mm(mixed, w_out).astype(bf16).reshape(n, own, width), 3)
    residual = flat_in + attn_sum
    inv_mid = lax.rsqrt(jnp.mean(residual * residual, axis=1, keepdims=True) + norm_eps)
    normed_mid = residual * inv_mid
    h_mid = gather((normed_mid * gain_mid).astype(bf16), 1).reshape(total, width)

    gate_up = mm(h_mid, wgu)
    gate, up = gate_up[:, :fw], gate_up[:, fw:]
    sig = jax.nn.sigmoid(gate)
    inner = (gate * sig * up).astype(bf16)
    mlp_sum = lax.psum_scatter(mm(inner, w_down).astype(bf16), "fsdp", scatter_dimension=0, tiled=True)
    block_out = (residual + mlp_sum.astype(f32)).astype(bf16).reshape(tokens.shape)

    grad_down = lax.psum(t_mm(inner, dy).astype(bf16), "seq").astype(f32)
    d_inner = mm_t(dy, w_down)
    d_gate = (d_inner * up * (sig * (1.0 + gate * (1.0 - sig)))).astype(bf16)
    d_up = (d_inner * (gate * sig)).astype(bf16)
    d_gu = jnp.concatenate([d_gate, d_up], axis=1)
    d_hmid = scatter(mm_t(d_gu, wgu).astype(bf16).reshape(n, own, width), 4)
    part_gu = t_mm(h_mid, d_gu).astype(bf16).reshape(n, width // n, 2 * fw)

    gain_mid_term = jnp.sum(normed_mid * d_hmid, axis=0)
    d_resid = cotangent.reshape(own, width).astype(f32) + norm_back(d_hmid * gain_mid, normed_mid, inv_mid)
    d_attn = gather(d_resid.astype(bf16), 2).reshape(total, width)

    part_out = t_mm(mixed, d_attn).astype(bf16)
    d_mixed = mm_t(d_attn, w_out).reshape(n, NSEG, rows, cw)
    d_qkv, bias_rows = attention_back(
        qkv, d_mixed, diff, lse, doc_col, doc_row, side, blend_row, memory, norm_vec, heads
    )
    d_qkv = d_qkv.reshape(total, 3 * cw)
    bias_term = jnp.sum(bias_rows.reshape(heads, HEAD_DIM), axis=1) * blend * (1.0 - blend)

    d_hin = scatter(mm_t(d_qkv, wqkv).astype(bf16).reshape(n, own, width), 5)
    part_qkv = t_mm(h_in, d_qkv).astype(bf16).reshape(n, width // n, 3 * cw)
    (sum_out,), (sum_gu, sum_qkv) = line_sum([part_out], [part_gu, part_qkv], 6)
    grad_out = sum_out.astype(f32)
    grad_gate, grad_up = to_rows(sum_gu, 2)
    grad_q, grad_k, grad_v = to_rows(sum_qkv, 3)
    gain_in_term = jnp.sum(normed_in * d_hin, axis=0)
    grad_tokens = (d_resid + norm_back(d_hin * gain_in, normed_in, inv_in)).reshape(tokens.shape)

    gain_grads = lax.psum_scatter(
        jnp.stack([gain_in_term, gain_mid_term]), "fsdp", scatter_dimension=1, tiled=True
    )
    small = lax.psum(jnp.concatenate([gain_grads.reshape(-1), bias_term]), "seq")
    per = width // n
    return (
        block_out,
        grad_tokens,
        small[:per],
        grad_q,
        grad_k,
        grad_v,
        small[2 * per :],
        grad_out,
        small[per : 2 * per],
        grad_gate,
        grad_up,
        grad_down,
    )


def solution(mesh):
    whole = P("seq", None, "fsdp", None)
    matrix, vector = P("fsdp", None), P("fsdp")
    return jax.shard_map(
        shards,
        mesh=mesh,
        in_specs=(whole, P("seq", None), vector, matrix, matrix, matrix, vector, matrix, vector, matrix, matrix, matrix, whole),
        out_specs=(whole, whole, vector, matrix, matrix, matrix, vector, matrix, vector, matrix, matrix, matrix),
        check_vma=False,
    )
```

time: 2730 us -> 1170 us (0.43)
  waiting for transfers between devices: 2010 us -> 0.83 us
  Pallas kernels: 0 us -> 730 us
  matrix products: 364 us -> 166 us
  other arithmetic: 116 us -> 25.1 us
    reduce_scatter x6 -> x1, waiting for transfers between devices: 803 us -> 0.01 us  [shards(): lax.psum_scatter(mm(inner, w_down).astype(bf16), 'fsdp', scatter_dimensio...]
    pallas_call x0 -> x9, Pallas kernels: none -> 730 us  [the longest x1 414 us: line_sum(): pl.pallas_call(functools.partial(line_kernel, still_rows, moved_rows), in...]
    all_gather x9 -> x2, waiting for transfers between devices: 677 us -> 0.02 us  [the longest x1 0.02 us: to_columns_in_turns(): lax.all_gather(part, 'seq', axis=1, tiled=True)]
    psum x2 -> x1, waiting for transfers between devices: 524 us -> 0.02 us  [shards(): grad_down = lax.psum(t_mm(inner, dy).astype(bf16), 'seq').astype(f32)]
    dot_general x41 -> x12, matrix products: 364 us -> 166 us  [the longest x4 60.6 us: mm_t(): lax.dot_general(a, b, (((1,), (1,)), ((), ())), preferred_element_type=f32)]
    unnamed x175 -> x95, local copies, waits for them, and re-layouts: 99.5 us -> 44 us
    concatenate x2 -> x1, other arithmetic: 46.7 us -> 0.01 us  [shards(): jnp.concatenate([gain_grads.reshape(-1), bias_term])]
    all_to_all x0 -> x1, blocking collectives: none -> 31.8 us  [to_columns(): out = lax.all_to_all(parts, 'fsdp', split_axis=1, concat_axis=0, tiled=True)]
  transfers between devices with their start and end apart: 19 -> 6, of which waited for: 17 -> 0; matrix products, arithmetic and copies ran while one was open for 15% -> 21% of each run, Pallas kernels for 0% -> 50%
where the time goes in v1:
time: 1170 us; the launch traced here: 1160 us
  Pallas kernels  730 us (62%)
  matrix products  166 us (14%)
  local copies, waits for them, and re-layouts  137 us (12%)
  blocking collectives  79.9 us (7%)
  other arithmetic  25.1 us (2%)
  between operations  14.9 us (1%)
    pallas_call x1, Pallas kernels, line_sum(): pl.pallas_call(functools.partial(line_kernel, still_rows, moved_rows), in...  414 us
    pallas_call x3, Pallas kernels, gather(): pl.pallas_call(gather_kernel, in_specs=[pl.BlockSpec(memory_space=pl.ANY)...  139 us
    pallas_call x3, Pallas kernels, scatter(): pl.pallas_call(scatter_kernel, in_specs=[pl.BlockSpec(memory_space=pl.ANY...  132 us
    dot_general x4, matrix products, mm_t(): lax.dot_general(a, b, (((1,), (1,)), ((), ())), preferred_element_type=f32)  60.6 us
    dot_general x4, matrix products, t_mm(): lax.dot_general(a, b, (((0,), (0,)), ((), ())), preferred_element_type=f32)  52.7 us
    dot_general x4, matrix products, mm(): lax.dot_general(a, b, (((1,), (0,)), ((), ())), preferred_element_type=f32)  52.2 us
    unnamed x95, local copies, waits for them, and re-layouts  44 us
    all_gather x1, blocking collectives, shards(): lax.all_gather(jnp.stack([norm_in, norm_mid]), 'fsdp', axis=1, tiled=True)  39.2 us
  transfers between devices with their start and end apart: 6, of which 0 were waited for; matrix products, arithmetic and copies ran while one was open for 21% of the time, Pallas kernels for 50%

profile of v1, /device:TPU:0, one launch (start us, length us, event | category | flops | bytes accessed | tf_op | source)
XLA Modules:
  0.0 1158.4 jit_solution(4236221744729234387)
XLA Ops:
  15.4 31.8 %all_to_all.30 = bf16[64,8,2048]{2,0,1:T(8,128)(2,1)S(1)} all-to-all(bf16[64,8,2048]{2,0,1:T(8,128)(2,1)} %reshape.216), channel_id=1, replica_groups=mesh['seq'=4,'fsdp'=8] {'fsdp'}, dimensions={1} | all-to-all | bytes 4194304 | tf_op jit(solution)/shard_map/all_to_all | solution.py:646
  64.4 39.2 %all_gather.9 = f32[2,2048]{1,0:T(2,128)S(1)} all-gather(f32[2,256]{1,0:T(2,128)S(1)} %pad_maximum_fusion.7), channel_id=1, replica_groups=mesh['seq'=4,'fsdp'=8] {'fsdp'}, dimensions={1}, use_global_device_ids=true | all-gather | bytes 18432 | tf_op jit(solution)/shard_map/all_gather | solution.py:691
  105.8 39.3 %gather.3 = bf16[8,256,2048]{2,1,0:T(8,128)(2,1)} custom-call(bf16[256,2048]{1,0:T(8,128)(2,1)} %fusion.5.x_ref), custom_call_target="tpu_custom_call" | custom-call | tf_op jit(solution)/shard_map/gather/pallas_call | solution.py:335
  151.0 11.2 convolution_convert_fusion.6
  162.2 18.6 %attention.1 = (bf16[8,2,128,256]{3,2,1,0:T(8,128)(2,1)S(1)}, f32[8,2,128,256]{3,2,1,0:T(8,128)S(1)}, f32[2,2,1024,1]{3,2,1,0:T(8,128)}, f32[2,128,128]{2,1,0:T(8,128)S(1)}, f32[2,1,128]{2,1,0:T(1,128)S(1)}) custom-call(bf16[8,2,128,768]{3,2,1,0:T(8,128)(2,1)} %bitcast.152, s32[2,1024,1]{2,1,0:T(8,128)S(1)} %sub.30.doc_col, s32[2,1,1024]{2,1,0:T(1,128)S(1)} %bitcast.142, ...), custom_call_target="tpu_custom_call" | custom-call | flops 1073741824 | bytes 8388608 | tf_op jit(solution)/shard_map/attention/pallas_call | solution.py:213
  183.3 51.6 %scatter.3 = f32[256,2048]{1,0:T(8,128)S(1)} custom-call(bf16[8,256,2048]{2,1,0:T(8,128)(2,1)S(1)} %bitcast.137), custom_call_target="tpu_custom_call" | custom-call | tf_op jit(solution)/shard_map/scatter/pallas_call | solution.py:414
  236.8 61.3 %gather.4 = bf16[8,256,2048]{2,1,0:T(8,128)(2,1)} custom-call(bf16[256,2048]{1,0:T(8,128)(2,1)} %multiply_convert_fusion.3.x_ref), custom_call_target="tpu_custom_call" | custom-call | tf_op jit(solution)/shard_map/gather/pallas_call | solution.py:335
  298.1 11.4 copy.103
  309.5 24.5 %fusion.21 = f32[2048,2048]{0,1:T(8,128)} fusion(bf16[2048,2048]{1,0:T(8,128)(2,1)} %bitcast.157, bf16[2048,2048]{1,0:T(8,128)(2,1)} %bitcast.164), kind=kOutput, calls=%fused_computation.61 | convolution fusion | flops 17179869184 | bytes 33554432 | tf_op jit(solution)/shard_map/dot_general | solution.py:29
  334.0 22.1 %multiply_convert_fusion.1 = (bf16[2048,1024]{0,1:T(8,128)(2,1)}, bf16[2048,1024]{0,1:T(8,128)(2,1)}, bf16[2048,1024]{0,1:T(8,128)(2,1)}) fusion(f32[2048,2048]{0,1:T(8,128)} %fusion.21, bf16[2048,2048]{1,0:T(8,128)(2,1)} %all-gather.4.cloned.1.call-done, bf16[1024,2048]{1,0:T(8,128)(2,1)} %param.24), kind=kOutput, calls=%fused_computation.2 | convolution fusion | flops 8621391872 | bytes 41943040 | tf_op jit(solution)/shard_map/dot_general | solution.py:33
  356.1 22.6 %convolution_convert_fusion.2 = bf16[2048,2048]{1,0:T(8,128)(2,1)S(1)} fusion(bf16[2048,2048]{1,0:T(8,128)(2,1)} %bitcast.165, bf16[2048,1024]{0,1:T(8,128)(2,1)} %get-tuple-element.99, bf16[2048,1024]{0,1:T(8,128)(2,1)} %get-tuple-element.98), kind=kOutput, calls=%fused_computation.8 | convolution fusion | flops 17200840704 | bytes 25165824 | tf_op jit(solution)/shard_map/dot_general | solution.py:33
  378.6 40.4 %scatter.4 = f32[256,2048]{1,0:T(8,128)S(1)} custom-call(bf16[8,256,2048]{2,1,0:T(8,128)(2,1)S(1)} %bitcast.140), custom_call_target="tpu_custom_call" | custom-call | tf_op jit(solution)/shard_map/scatter/pallas_call | solution.py:414
  422.7 38.8 %gather.5 = bf16[8,256,2048]{2,1,0:T(8,128)(2,1)} custom-call(bf16[256,2048]{1,0:T(8,128)(2,1)} %fusion.16.x_ref), custom_call_target="tpu_custom_call" | custom-call | tf_op jit(solution)/shard_map/gather/pallas_call | solution.py:335
  461.5 7.1 fusion.12.dmix_ref
  468.6 26.0 %attention_back.1 = (bf16[8,2,128,768]{3,2,1,0:T(8,128)(2,1)}, f32[1,256]{1,0:T(1,128)}) custom-call(bf16[8,2,128,768]{3,2,1,0:T(8,128)(2,1)} %bitcast.153, f32[8,2,128,256]{3,2,1,0:T(8,128)} %fusion.12.dmix_ref, f32[8,2,128,256]{3,2,1,0:T(8,128)} %copy-done.10, f32[2,2,1024,1]{3,2,1,0:T(8,128)} %get-tuple-element.24.lse_ref, s32[2,1024,1]{2,1,0:T(8,128)} %copy-done.5, ...), custom_call_target="tpu_custom_call" | custom-call | flops 2684354560 | bytes 16777216 | tf_op jit(solution)/shard_map/attention_back/pallas_call | solution.py:237
  494.6 8.9 convolution_convert_fusion.1
  503.5 40.4 %scatter.5 = f32[256,2048]{1,0:T(8,128)S(1)} custom-call(bf16[8,256,2048]{2,1,0:T(8,128)(2,1)S(1)} %bitcast.141), custom_call_target="tpu_custom_call" | custom-call | tf_op jit(solution)/shard_map/scatter/pallas_call | solution.py:414
  547.4 13.9 %convolution_convert_fusion.5 = bf16[1024,2048]{1,0:T(8,128)(2,1)} fusion(bf16[2048,1024]{0,1:T(8,128)(2,1)} %get-tuple-element.102, bf16[2048,2048]{1,0:T(8,128)(2,1)} %all-gather.4.cloned.1.call-done), kind=kOutput, calls=%fused_computation.11 | convolution fusion | flops 8592031744 | bytes 16777216 | tf_op jit(solution)/shard_map/dot_general | solution.py:37
  561.3 14.2 %convolution_convert_fusion.3 = bf16[2048,2048]{1,0:T(8,128)(2,1)} fusion(bf16[2048,1024]{0,1:T(8,128)(2,1)} %get-tuple-element.102, bf16[1024,2048]{1,0:T(8,128)(2,1)} %param.24), kind=kOutput, calls=%fused_computation.9 | convolution fusion | flops 8594128896 | bytes 16777216 | tf_op jit(solution)/shard_map/dot_general | solution.py:29
  576.8 6.0 convolution_convert_fusion.8.refs_0_
  582.8 10.6 convolution_convert_fusion.7
  593.4 22.2 %convolution_convert_fusion = bf16[2048,2048]{1,0:T(8,128)(2,1)} fusion(bf16[2048,2048]{1,0:T(8,128)(2,1)S(1)} %bitcast.160, bf16[2048,1024]{0,1:T(8,128)(2,1)} %get-tuple-element.99, bf16[2048,1024]{0,1:T(8,128)(2,1)} %get-tuple-element.98), kind=kOutput, calls=%fused_computation.6 | convolution fusion | flops 17200840704 | bytes 25165824 | tf_op jit(solution)/shard_map/dot_general | solution.py:37
  615.7 413.9 %line_sum.1 = (bf16[256,2048]{1,0:T(8,128)(2,1)S(1)}, bf16[8,256,2048]{2,1,0:T(8,128)(2,1)}, bf16[8,256,768]{2,1,0:T(8,128)(2,1)S(1)}, bf16[256,2048]{1,0:T(8,12...) custom-call(bf16[256,2048]{1,0:T(8,128)(2,1)S(1)} %convolution_conve, ...), custom_call_target="tpu_custom_call" | custom-call | tf_op jit(solution)/shard_map/line_sum/pallas_call | solution.py:625
  1038.2 5.5 fusion.18
  1051.2 21.4 %reshape.212 = f32[8,256,2,1024]{3,2,1,0:T(2,128)} reshape(bf16[8,256,2048]{2,1,0:T(8,128)(2,1)} %get-tuple-element.31) | data formatting | bytes 25165824 | tf_op jit(solution)/shard_map/convert_element_type | solution.py:661
  1072.6 19.3 %fusion.17 = (f32[8,256,1,1024]{3,2,1,0:T(1,128)}, f32[8,256,1,1024]{3,2,1,0:T(1,128)S(1)}) fusion(f32[8,256,2,1024]{3,2,1,0:T(2,128)} %reshape.212), kind=kLoop, calls=%fused_computation.57 | loop fusion | bytes 33554432 | tf_op jit(solution)/shard_map/slice | solution.py:662
  1092.0 8.2 copy.119
  1100.2 11.2 copy.124
  1116.3 11.2 copy.123
  1128.7 8.9 psum.14
  1138.7 6.8 convert_element_type.122
  1145.6 5.9 fusion.9
  (149 shorter events, 69.0 us)
Async XLA Ops:
  7.2 173.7 %copy-start = (bf16[256,2048]{1,0:T(8,128)(2,1)S(1)}, bf16[256,2048]{1,0:T(8,128)(2,1)}, u32[]{:S(2)}) copy-start(bf16[256,2048]{1,0:T(8,128)(2,1)} %param.20) | copy-start | bytes 3145732
  7.2 290.9 %all-gather.6.cloned.1.call-start = ((), (), s32[]{:S(2)}) async-start(), calls=%async_computation.7 | async-start | bytes 10485760 | tf_op jit(solution)/shard_map/all_gather | solution.py:656
  49.6 284.3 %all-gather.4.cloned.1.call-start = ((), (), s32[]{:S(2)}) async-start(), calls=%async_computation.5 | async-start | bytes 9437184 | tf_op jit(solution)/shard_map/all_gather | solution.py:700
  58.0 6.3 copy-start.33
  58.0 6.3 copy-start.34
  58.1 45.6 %copy-start.16 = (bf16[1,2,128,2048]{3,2,1,0:T(8,128)(2,1)S(1)}, bf16[1,2,128,2048]{3,2,1,0:T(8,128)(2,1)}, u32[]{:S(2)}) copy-start(bf16[1,2,128,2048]{3,2,1,0:T(8,128)(2,1)} %param.13) | copy-start | bytes 3145732
  58.1 87.9 %all-to-all-start = ((bf16[256,8,768]{0,2,1:T(8,128)(2,1)}), bf16[256,8,768]{0,2,1:T(8,128)(2,1)}, u32[]{:S(2)}, u32[]{:S(2)}) async-start(bf16[256,8,768]{0,2,1:T(8,128)(2,1)} %bitcast.151), calls=%async_computation | async-start | bytes 6291456 | tf_op jit(solution)/shard_map/all_to_all | solution.py:646
  62.7 1064.9 %reduce-scatter.7.cloned.1.call-start = ((), (), s32[]{:S(2)}) async-start(), calls=%async_computation.8 | async-start | bytes 1179648
  62.9 99.3 %copy-start.11 = (s32[2048]{0:T(1024)}, s32[2048]{0:T(1024)S(1)}, u32[]{:S(2)}) copy-start(s32[2048]{0:T(1024)S(1)} %broadcast_add_fusion) | copy-start | bytes 24580
  63.8 98.4 %copy-start.5 = (s32[2,1024,1]{2,1,0:T(8,128)}, s32[2,1024,1]{2,1,0:T(8,128)S(1)}, u32[]{:S(2)}) copy-start(s32[2,1024,1]{2,1,0:T(8,128)S(1)} %sub.30.doc_col) | copy-start | bytes 24580
  103.9 315.8 %copy-start.22 = (f32[1,2048]{1,0:T(1,128)}, f32[1,2048]{1,0:T(1,128)S(1)}, u32[]{:S(2)}) copy-start(f32[1,2048]{1,0:T(1,128)S(1)} %get-tuple-element.108) | copy-start | bytes 24580
  105.8 39.3 %copy-start.37 = (f32[2]{0:T(128)S(1)}, f32[2]{0:T(128)}, u32[]{:S(2)}) copy-start(f32[2]{0:T(128)} %param.19) | copy-start | bytes 28
  145.9 16.3 %copy-start.6 = (f32[2,1024,1]{2,1,0:T(8,128)}, f32[2,1024,1]{2,1,0:T(8,128)S(1)}, u32[]{:S(2)}) copy-start(f32[2,1024,1]{2,1,0:T(8,128)S(1)} %compare_convert_fusion.side_ref) | copy-start | bytes 24580
  162.2 21.1 %copy-start.13 = (f32[2,128]{1,0:T(2,128)}, f32[2,128]{1,0:T(2,128)S(1)}, u32[]{:S(2)}) copy-start(f32[2,128]{1,0:T(2,128)S(1)} %broadcast_in_dim.2) | copy-start | bytes 3076
  183.3 51.7 %copy-start.17 = (bf16[1,2,128,2048]{3,2,1,0:T(8,128)(2,1)S(1)}, bf16[1,2,128,2048]{3,2,1,0:T(8,128)(2,1)}, u32[]{:S(2)}) copy-start(bf16[1,2,128,2048]{3,2,1,0:T(8,128)(2,1)} %param.13) | copy-start | bytes 3145732
  235.3 184.4 %copy-start.15 = (f32[256,2048]{1,0:T(8,128)}, f32[256,2048]{1,0:T(8,128)S(1)}, u32[]{:S(2)}) copy-start(f32[256,2048]{1,0:T(8,128)S(1)} %get-tuple-element.97) | copy-start | bytes 6291460
  235.3 184.4 %copy-start.26 = (f32[256]{0:T(256)}, f32[256]{0:T(256)S(1)}, u32[]{:S(2)}) copy-start(f32[256]{0:T(256)S(1)} %add_rsqrt_fusion) | copy-start | bytes 3076
  468.6 26.0 %copy-start.20 = (bf16[8,256,1,768]{3,1,0,2:T(8,128)(2,1)S(1)}, bf16[8,256,1,768]{3,1,0,2:T(8,128)(2,1)}, u32[]{:S(2)}) copy-start(bf16[8,256,1,768]{3,1,0,2:T(8,128)(2,1)} %copy.96) | copy-start | bytes 9437188
  503.5 41.8 %copy-start.18 = (bf16[1,2,128,2048]{3,2,1,0:T(8,128)(2,1)S(1)}, bf16[1,2,128,2048]{3,2,1,0:T(8,128)(2,1)}, u32[]{:S(2)}) copy-start(bf16[1,2,128,2048]{3,2,1,0:T(8,128)(2,1)} %param.13) | copy-start | bytes 3145732
  503.5 41.8 %copy-start.25 = (f32[1,2048]{1,0:T(1,128)S(1)}, f32[1,2048]{1,0:T(1,128)}, u32[]{:S(2)}) copy-start(f32[1,2048]{1,0:T(1,128)} %copy-done.24) | copy-start | bytes 24580
  503.5 41.8 %copy-start.29 = (f32[256]{0:T(256)S(1)}, f32[256]{0:T(256)}, u32[]{:S(2)}) copy-start(f32[256]{0:T(256)} %copy-done.28) | copy-start | bytes 3076
  547.3 591.4 %all-reduce.2.cloned.1.call-start = ((), (), s32[]{:S(2)}) async-start(), calls=%async_computation.6 | async-start | bytes 8388608 | tf_op jit(solution)/shard_map/psum | solution.py:727
  561.3 584.2 %reduce-scatter.5.cloned.1.call-start = ((), (), s32[]{:S(2)}) async-start(), calls=%async_computation.4 | async-start | bytes 9437184 | tf_op jit(solution)/shard_map/reduce_scatter | solution.py:724
  576.8 16.6 %slice-start = ((s8[8388608]{0:T(1024)(128)(4,1)}), s8[4194304]{0:T(1024)(128)(4,1)S(1)}, s32[]{:S(2)}) async-start(s8[8388608]{0:T(1024)(128)(4,1)} %bitcast.158), calls=%async_computation.9 | async-start | bytes 8388608
  582.8 10.6 slice-start.1
  1116.2 11.2 copy-start.32
  1116.3 11.3 copy-start.38
  1138.7 6.9 copy-start.3
  1138.7 6.9 copy-start.23
  1138.7 6.9 copy-start.27
  1138.7 6.9 copy-start.31
  1138.7 12.7 %copy-start.1 = (bf16[256,2048]{1,0:T(8,128)(2,1)S(1)}, bf16[256,2048]{1,0:T(8,128)(2,1)}, u32[]{:S(2)}) copy-start(bf16[256,2048]{1,0:T(8,128)(2,1)} %param.20) | copy-start | bytes 3145732
  (15 other events, 32.9 us)
Sparse Core Ops, SparseCore 0:
  49.8 148.9 all-gather.5
  200.7 86.8 all-gather.3
  547.5 36.4 reduce-scatter.6
  586.2 260.2 all-reduce.1
  850.2 81.0 reduce-scatter.4

commit v2 on v1

v2 whole, which is shorter than its diff:
```python
import functools

import jax
import jax.numpy as jnp
from jax import lax
from jax.experimental import pallas as pl
from jax.experimental.pallas import tpu as pltpu
from jax.sharding import PartitionSpec as P

HEADS = 16
HEAD_DIM = 128
NSEG = 2

highest = lax.Precision.HIGHEST
norm_eps = 1e-05
f32 = jnp.float32
bf16 = jnp.bfloat16


def doc_number(start_row, places):
    return jnp.sum((start_row[None, :] <= places[:, None]).astype(jnp.int32), axis=1) - 1


def norm_back(grad_in, normed, inverse):
    return inverse * (grad_in - normed * jnp.mean(grad_in * normed, axis=-1, keepdims=True))


def mm(a, b):
    return lax.dot_general(a, b, (((1,), (0,)), ((), ())), preferred_element_type=f32)


def mm_t(a, b):
    return lax.dot_general(a, b, (((1,), (1,)), ((), ())), preferred_element_type=f32)


def t_mm(a, b):
    return lax.dot_general(a, b, (((0,), (0,)), ((), ())), preferred_element_type=f32)


def dots(a, b, ca, cb, precision=None):
    return lax.dot_general(a, b, (((ca,), (cb,)), ((), ())), preferred_element_type=f32, precision=precision)


def phi(u):
    return jnp.where(u > 0, u + 1.0, jnp.exp(jnp.minimum(u, 0.0)))


def phi_slope(u):
    return jnp.where(u > 0, 1.0, jnp.exp(jnp.minimum(u, 0.0)))


def attention_head(h, heads, segment, qkv_ref, doc_col, doc_row, side_ref, blend_ref, mixed_ref, diff_ref, lse_ref, mem_ref, nv_ref):
    n, _, rows, _ = qkv_ref.shape
    cw = heads * HEAD_DIM
    take = max(1, 256 // rows)
    block = take * rows
    scale = HEAD_DIM ** (-0.5)

    def part(kind, h, lo, hi):
        cols = slice(kind * cw + h * HEAD_DIM, kind * cw + (h + 1) * HEAD_DIM)
        return qkv_ref[lo:hi, 0, :, cols].reshape((hi - lo) * rows, HEAD_DIM)

    cols = slice(h * HEAD_DIM, (h + 1) * HEAD_DIM)

    @pl.when(segment == 0)
    def _():
        fk = phi(part(1, h, 0, n).astype(f32)) * side_ref[0]
        mem_ref[h] = dots(fk, part(2, h, 0, n).astype(f32), 0, 0, highest)
        nv_ref[h] = jnp.sum(fk, axis=0, keepdims=True)

    blend = blend_ref[:, cols]
    for i in range(n // take):
        lo, hi = i * take, (i + 1) * take
        span = (i + 1) * block
        q = part(0, h, lo, hi)
        s = dots(q, part(1, h, 0, hi), 1, 1) * scale
        at = lax.broadcasted_iota(jnp.int32, (block, span), 0) + i * block
        allowed = (lax.broadcasted_iota(jnp.int32, (block, span), 1) <= at) & (
            doc_row[0, :, :span] == doc_col[0, i * block : (i + 1) * block]
        )
        s = jnp.where(allowed, s, -1000000000.0)
        top = jnp.max(s, axis=1, keepdims=True)
        p = jnp.exp(s - top)
        tot = jnp.sum(p, axis=1, keepdims=True)
        lse_ref[h, 0, i * block : (i + 1) * block] = top + jnp.log(tot)
        direct = dots((p / tot).astype(bf16), part(2, h, 0, hi), 1, 0)
        shape = (take, rows, HEAD_DIM)

        @pl.when(segment == 0)
        def _():
            mixed_ref[lo:hi, 0, :, cols] = ((1.0 - blend) * direct).astype(bf16).reshape(shape)
            diff_ref[lo:hi, 0, :, cols] = (-direct).reshape(shape)

        @pl.when(segment != 0)
        def _():
            fq = phi(q.astype(f32))
            numer = dots(fq, mem_ref[h], 1, 0, highest)
            den = jnp.sum(fq * nv_ref[h], axis=1, keepdims=True) + 1.0
            ret = side_ref[0, i * block : (i + 1) * block] * numer / den
            mixed_ref[lo:hi, 0, :, cols] = (blend * ret + (1.0 - blend) * direct).astype(bf16).reshape(shape)
            diff_ref[lo:hi, 0, :, cols] = (ret - direct).reshape(shape)


def attention_kernel(heads, *refs):
    for h in range(heads):
        attention_head(h, heads, pl.program_id(0), *refs)


def attention_back_kernel(
    heads, qkv_ref, dmix_ref, diff_ref, lse_ref, doc_col, doc_row, side_ref, blend_ref, mem_ref, nv_ref,
    out_ref, bias_ref, dk_acc, dv_acc, dmem, dnv,
):
    n, _, rows, _ = qkv_ref.shape
    length = n * rows
    cw = heads * HEAD_DIM
    take = max(1, 256 // rows)
    block = take * rows
    scale = HEAD_DIM ** (-0.5)
    step = pl.program_id(0)
    shape = (take, rows, HEAD_DIM)

    def part(kind, h, lo, hi):
        cols = slice(kind * cw + h * HEAD_DIM, kind * cw + (h + 1) * HEAD_DIM)
        return qkv_ref[lo:hi, 0, :, cols].reshape((hi - lo) * rows, HEAD_DIM)

    @pl.when(step == 0)
    def _():
        bias_ref[...] = jnp.zeros_like(bias_ref)
        dmem[...] = jnp.zeros_like(dmem)
        dnv[...] = jnp.zeros_like(dnv)

    for h in range(heads):
        cols = slice(h * HEAD_DIM, (h + 1) * HEAD_DIM)
        blend = blend_ref[:, cols]
        dk_acc[...] = jnp.zeros_like(dk_acc)
        dv_acc[...] = jnp.zeros_like(dv_acc)
        for i in range(n // take):
            lo, hi = i * take, (i + 1) * take
            span = (i + 1) * block
            here = slice(i * block, (i + 1) * block)
            q, k, v = part(0, h, lo, hi), part(1, h, 0, hi), part(2, h, 0, hi)
            dmix = dmix_ref[lo:hi, 0, :, cols].reshape(block, HEAD_DIM)
            bias_ref[:, cols] += jnp.sum(dmix * diff_ref[lo:hi, 0, :, cols].reshape(block, HEAD_DIM), axis=0, keepdims=True)
            ddir = ((1.0 - blend) * dmix).astype(bf16)
            s = dots(q, k, 1, 1) * scale
            at = lax.broadcasted_iota(jnp.int32, (block, span), 0) + i * block
            allowed = (lax.broadcasted_iota(jnp.int32, (block, span), 1) <= at) & (
                doc_row[0, :, :span] == doc_col[0, here]
            )
            e = jnp.exp(jnp.where(allowed, s, -1000000000.0) - lse_ref[h, 0, here])
            dp = dots(ddir, v, 1, 1)
            bal = jnp.sum(e * dp, axis=1, keepdims=True)
            ds = (e * (dp - bal)).astype(bf16)
            dv_acc[:span] += dots(e.astype(bf16), ddir, 0, 0)
            dk_acc[:span] += dots(ds, q, 0, 0) * scale
            dq = dots(ds, k, 1, 0) * scale

            @pl.when(step != 0)
            def _():
                out_ref[lo:hi, 0, :, cols] = dq.astype(bf16).reshape(shape)

            @pl.when(step == 0)
            def _():
                q32 = q.astype(f32)
                fq = phi(q32)
                numer = dots(fq, mem_ref[h], 1, 0, highest)
                den = jnp.sum(fq * nv_ref[h], axis=1, keepdims=True) + 1.0
                dnum = side_ref[0, here] * (blend * dmix) / den
                dden = -jnp.sum(dnum * numer, axis=1, keepdims=True) / den
                dmem[h] += dots(fq, dnum, 0, 0, highest)
                dnv[h] += jnp.sum(dden * fq, axis=0, keepdims=True)
                dfq = dots(dnum, mem_ref[h], 1, 1, highest) + dden * nv_ref[h]
                out_ref[lo:hi, 0, :, cols] = (dq + dfq * phi_slope(q32)).astype(bf16).reshape(shape)

        whole = (n, rows, HEAD_DIM)
        kcols = slice(cw + h * HEAD_DIM, cw + (h + 1) * HEAD_DIM)
        vcols = slice(2 * cw + h * HEAD_DIM, 2 * cw + (h + 1) * HEAD_DIM)

        @pl.when(step == 0)
        def _():
            out_ref[:, 0, :, kcols] = dk_acc[...].astype(bf16).reshape(whole)
            out_ref[:, 0, :, vcols] = dv_acc[...].astype(bf16).reshape(whole)

        @pl.when(step != 0)
        def _():
            k32 = part(1, h, 0, n).astype(f32)
            v32 = part(2, h, 0, n).astype(f32)
            key_set = side_ref[0]
            mem_v = key_set * dots(phi(k32), dmem[h], 1, 0, highest)
            mem_k = key_set * (dots(v32, dmem[h], 1, 1, highest) + dnv[h]) * phi_slope(k32)
            out_ref[:, 0, :, kcols] = (dk_acc[...] + mem_k).astype(bf16).reshape(whole)
            out_ref[:, 0, :, vcols] = (dv_acc[...] + mem_v).astype(bf16).reshape(whole)


def attention_specs(n, rows, heads, pick):
    length = n * rows
    cw = heads * HEAD_DIM
    wide = pl.BlockSpec((n, 1, rows, 3 * cw), lambda g: (0, pick(g), 0, 0))
    narrow = pl.BlockSpec((n, 1, rows, cw), lambda g: (0, pick(g), 0, 0))
    lse = pl.BlockSpec((heads, 1, length, 1), lambda g: (0, pick(g), 0, 0))
    col = pl.BlockSpec((1, length, 1), lambda g: (pick(g), 0, 0))
    row = pl.BlockSpec((1, 1, length), lambda g: (pick(g), 0, 0))
    line = pl.BlockSpec((1, cw), lambda g: (0, 0))
    mem = pl.BlockSpec((heads, HEAD_DIM, HEAD_DIM), lambda g: (0, 0, 0))
    nv = pl.BlockSpec((heads, 1, HEAD_DIM), lambda g: (0, 0, 0))
    return wide, narrow, lse, col, row, line, mem, nv


def attention(qkv, doc_col, doc_row, side, blend, heads):
    n, _, rows, _ = qkv.shape
    length = n * rows
    cw = heads * HEAD_DIM
    wide, narrow, lse, col, row, line, mem, nv = attention_specs(n, rows, heads, lambda g: g)
    pairs = heads * NSEG * length * length // 2
    return pl.pallas_call(
        functools.partial(attention_kernel, heads),
        grid=(NSEG,),
        in_specs=[wide, col, row, col, line],
        out_specs=[narrow, narrow, lse, mem, nv],
        out_shape=[
            jax.ShapeDtypeStruct((n, NSEG, rows, cw), bf16),
            jax.ShapeDtypeStruct((n, NSEG, rows, cw), f32),
            jax.ShapeDtypeStruct((heads, NSEG, length, 1), f32),
            jax.ShapeDtypeStruct((heads, HEAD_DIM, HEAD_DIM), f32),
            jax.ShapeDtypeStruct((heads, 1, HEAD_DIM), f32),
        ],
        compiler_params=pltpu.CompilerParams(vmem_limit_bytes=48 << 20),
        cost_estimate=pl.CostEstimate(flops=pairs * 4 * HEAD_DIM, transcendentals=pairs, bytes_accessed=8 << 20),
        name="attention",
    )(qkv, doc_col, doc_row, side, blend)


def attention_back(qkv, dmix, diff, lse_rows, doc_col, doc_row, side, blend, mem_all, nv_all, heads):
    n, _, rows, _ = qkv.shape
    length = n * rows
    cw = heads * HEAD_DIM
    wide, narrow, lse, col, row, line, mem, nv = attention_specs(n, rows, heads, lambda g: NSEG - 1 - g)
    pairs = heads * NSEG * length * length // 2
    return pl.pallas_call(
        functools.partial(attention_back_kernel, heads),
        grid=(NSEG,),
        in_specs=[wide, narrow, narrow, lse, col, row, col, line, mem, nv],
        out_specs=[wide, line],
        out_shape=[
            jax.ShapeDtypeStruct((n, NSEG, rows, 3 * cw), bf16),
            jax.ShapeDtypeStruct((1, cw), f32),
        ],
        scratch_shapes=[
            pltpu.VMEM((length, HEAD_DIM), f32),
            pltpu.VMEM((length, HEAD_DIM), f32),
            pltpu.VMEM((heads, HEAD_DIM, HEAD_DIM), f32),
            pltpu.VMEM((heads, 1, HEAD_DIM), f32),
        ],
        compiler_params=pltpu.CompilerParams(vmem_limit_bytes=56 << 20),
        cost_estimate=pl.CostEstimate(flops=pairs * 10 * HEAD_DIM, transcendentals=pairs, bytes_accessed=16 << 20),
        name="attention_back",
    )(qkv, dmix, diff, lse_rows, doc_col, doc_row, side, blend, mem_all, nv_all)


def flip(index, bit):
    return index + bit - 2 * bit * lax.rem(lax.div(index, bit), 2)


def other(index, bits):
    for bit in (1, 2, 4):
        if bits & bit:
            index = flip(index, bit)
    return index


def link(src, dst, sems, slot, axis, peer):
    return pltpu.make_async_remote_copy(
        src_ref=src, dst_ref=dst, send_sem=sems[0].at[slot], recv_sem=sems[1].at[slot],
        device_id={axis: peer}, device_id_type=pl.DeviceIdType.MESH,
    )


def send(src, dst, sems, slot, peer):
    return link(src, dst, sems, slot, "fsdp", peer)


def greet(peers):
    barrier = pltpu.get_barrier_semaphore()
    for peer in peers:
        pl.semaphore_signal(barrier, inc=1, device_id={"fsdp": peer}, device_id_type=pl.DeviceIdType.MESH)
    pl.semaphore_wait(barrier, len(peers))


PIECES = 4
ORDER = (0, 1, 2, 4, 3, 5, 6, 7)
GATHER_SEMS = [pltpu.SemaphoreType.DMA] + [pltpu.SemaphoreType.DMA((PIECES,))] * 14


def gather_parts(x_ref, out_ref, local_sem, *sems):
    me = lax.axis_index("fsdp")
    sib, xn, yn, far_owner = flip(me, 1), flip(me, 2), flip(me, 4), other(me, 6)
    rows = x_ref.shape[0] // PIECES
    half = PIECES // 2
    own, over_x, over_y, far = sems[0:2], sems[2:4], sems[4:6], sems[6:8]
    side_x, side_y, side_far = sems[8:10], sems[10:12], sems[12:14]
    started = []

    def at(owner, c):
        return out_ref.at[owner, pl.ds(c * rows, rows)]

    def mine(c):
        return x_ref.at[pl.ds(c * rows, rows)]

    def go(make):
        make().start()
        started.append(make)

    def pass_on(owner, c, sems, peer):
        go(lambda: send(at(owner, c), at(owner, c), sems, c, peer))

    def arrived(owner, c, sems):
        send(at(owner, c), at(owner, c), sems, c, sib).wait_recv()

    local = pltpu.make_async_copy(x_ref, out_ref.at[me], local_sem)

    def begin_one(c, sems, peer):
        return send(mine(c), at(me, c), sems, c, peer)

    def begin():
        for j in range(PIECES):
            c, d = j, (j + half) % PIECES
            go(functools.partial(begin_one, c, over_x, xn))
            go(functools.partial(begin_one, d, over_y, yn))
        for c in range(PIECES):
            go(functools.partial(begin_one, c, own, sib))
        local.start()
        local.wait()

    def near(j):
        c, d = j, (j + half) % PIECES
        arrived(xn, c, over_x)
        if c < half:
            pass_on(xn, c, far, yn)
        pass_on(xn, c, side_x, sib)
        arrived(yn, d, over_y)
        if d >= half:
            pass_on(yn, d, far, xn)
        pass_on(yn, d, side_y, sib)

    def beyond(j):
        for c in (j, j + half):
            arrived(far_owner, c, far)
            pass_on(far_owner, c, side_far, sib)

    def wait_from(d):
        for c in range(PIECES):
            arrived(other(me, d), c, {1: own, 3: side_x, 5: side_y, 7: side_far}[d])

    def end():
        for make in started:
            make().wait_send()

    near_steps = [functools.partial(near, j) for j in range(PIECES)]
    far_steps = [functools.partial(beyond, j) for j in range(half)]
    return [begin, *near_steps, *far_steps, wait_from, end]


def gather_steps(x_ref, out_ref, *sems):
    *steps, wait_from, end = gather_parts(x_ref, out_ref, *sems)

    def finish():
        for d in (1, 3, 5, 7):
            wait_from(d)
        end()

    return [*steps, finish]


def params(collective_id, mib=32):
    return pltpu.CompilerParams(collective_id=collective_id, has_side_effects=True, vmem_limit_bytes=mib << 20)


ANYWHERE = pl.BlockSpec(memory_space=pl.ANY)


def move_steps(ins, out_ref, first, rows, sems, local_sem):
    me = lax.axis_index("fsdp")
    count = len(ins)
    c = out_ref.shape[1] // count

    def piece(kind, d):
        peer = other(me, d)
        src = ins[kind].at[pl.ds(first, rows), pl.ds(pl.multiple_of(peer * c, 128), c)]
        dst = out_ref.at[pl.ds(pl.multiple_of(me * rows, 16), rows), pl.ds(kind * c, c)]
        return src, dst, peer

    def moving(kind, d):
        src, dst, peer = piece(kind, d)
        return send(src, dst, sems, d * count + kind, peer)

    def local(kind):
        src, dst, _ = piece(kind, 0)
        return pltpu.make_async_copy(src, dst, local_sem.at[kind])

    def begin():
        for d in (6, 7, 2, 4, 3, 5, 1):
            for kind in range(count):
                moving(kind, d).start()
        for kind in range(count):
            local(kind).start()

    def end():
        for d in ORDER[1:]:
            for kind in range(count):
                there = out_ref.at[pl.ds(pl.multiple_of(other(me, d) * rows, 16), rows), pl.ds(kind * c, c)]
                send(there, there, sems, d * count + kind, other(me, d)).wait_recv()
                moving(kind, d).wait_send()
        for kind in range(count):
            local(kind).wait()

    return [begin, end]


def move_kernel(count, rows, *refs):
    ins, (out_ref, local_sem, *sems) = refs[:count], refs[count:]
    me = lax.axis_index("fsdp")
    greet([other(me, d) for d in range(1, 8)])
    for step in move_steps(ins, out_ref, lax.axis_index("seq") * rows, rows, sems, local_sem):
        step()


def to_columns(weights, first, rows):
    n = lax.axis_size("fsdp")
    cols = weights[0].shape[1]
    weights = [lax.dynamic_slice_in_dim(w, first, rows, 0) for w in weights]
    parts = jnp.stack([w.reshape(rows, n, cols // n) for w in weights], axis=2)
    parts = parts.reshape(rows, n, len(weights) * (cols // n))
    out = lax.all_to_all(parts, "fsdp", split_axis=1, concat_axis=0, tiled=True)
    return out.reshape(n * rows, len(weights) * (cols // n))


def to_columns_in_turns(weights, collective_id):
    n, s = lax.axis_size("fsdp"), lax.axis_size("seq")
    count = len(weights)
    share = weights[0].shape[0] // s
    width = count * (weights[0].shape[1] // n)
    if n != 8:
        part = to_columns(weights, lax.axis_index("seq") * share, share)
    else:
        part = pl.pallas_call(
            functools.partial(move_kernel, count, share),
            in_specs=[ANYWHERE] * count,
            out_specs=ANYWHERE,
            out_shape=jax.ShapeDtypeStruct((n * share, width), bf16),
            scratch_shapes=[pltpu.SemaphoreType.DMA((count,))] + [pltpu.SemaphoreType.DMA((n * count,))] * 2,
            compiler_params=params(collective_id),
            name="move",
        )(*weights)
    part = part.reshape(n, share, width)
    return lax.all_gather(part, "seq", axis=1, tiled=True).reshape(n * share * s, width)


def front_kernel(count, *refs):
    x_ref, gain_ref, *refs = refs
    ins, refs = refs[:count], refs[count:]
    out_ref, gains_ref, w_ref, *sems = refs
    gain_sems, sems = sems[:3], sems[3:]
    move_sems, sems = sems[:3], sems[3:]
    me = lax.axis_index("fsdp")
    greet([other(me, d) for d in range(1, 8)])

    def gain(d):
        return send(gain_ref, gains_ref.at[me], gain_sems[1:], d, other(me, d))

    own = pltpu.make_async_copy(gain_ref, gains_ref.at[me], gain_sems[0])
    own.start()
    for d in range(1, 8):
        gain(d).start()
    first, *steps = gather_steps(x_ref, out_ref, *sems)
    begin, end = move_steps(ins, w_ref, 0, ins[0].shape[0], move_sems[1:], move_sems[0])
    first()
    begin()
    for step in steps:
        step()
    end()
    own.wait()
    for d in range(1, 8):
        there = gains_ref.at[other(me, d)]
        send(there, there, gain_sems[1:], d, other(me, d)).wait_recv()
        gain(d).wait_send()


def front(x, gains, weights, collective_id):
    n = lax.axis_size("fsdp")
    if n != 8:
        return (
            lax.all_gather(x, "fsdp", axis=0),
            lax.all_gather(gains, "fsdp", axis=1, tiled=True),
            to_columns(weights, 0, weights[0].shape[0]),
        )
    count = len(weights)
    kinds, c = gains.shape
    gains = jnp.concatenate([gains, jnp.zeros((8 - kinds, c), f32)])
    rows, cols = weights[0].shape
    sems = pltpu.SemaphoreType.DMA
    x, gains, w = pl.pallas_call(
        functools.partial(front_kernel, count),
        in_specs=[ANYWHERE] * (2 + count),
        out_specs=[ANYWHERE] * 3,
        out_shape=[
            jax.ShapeDtypeStruct((n, *x.shape), x.dtype),
            jax.ShapeDtypeStruct((n, 8, c), f32),
            jax.ShapeDtypeStruct((n * rows, count * (cols // n)), bf16),
        ],
        scratch_shapes=[sems, sems((8,)), sems((8,)), sems((count,)), sems((8 * count,)), sems((8 * count,)), *GATHER_SEMS],
        compiler_params=params(collective_id),
        name="front",
    )(x, gains, *weights)
    return x, gains[:, :kinds].transpose(1, 0, 2).reshape(kinds, n * c), w


def attend_kernel(heads, all_ref, gain_ref, w_ref, dy_ref, doc_col, doc_row, side_ref, blend_ref, *refs):
    h_out, qkv_out, dy_out, mixed_ref, diff_ref, lse_ref, mem_ref, nv_ref, x, w, hid, qkv, load_sems, x_sems, h_sems, q_sems, *sems = refs
    n, tokens, width = all_ref.shape
    rows = tokens // NSEG
    me = lax.axis_index("fsdp")
    weights = pltpu.make_async_copy(w_ref, w, load_sems.at[0])
    weights.start()

    def load(i):
        return pltpu.make_async_copy(all_ref.at[i], x.at[rest(i, 2)], x_sems.at[rest(i, 2)])

    def store(i):
        return pltpu.make_async_copy(hid.at[rest(i, 2)], h_out.at[i], h_sems.at[rest(i, 2)])

    load(0).start()
    greet([other(me, d) for d in (1, 2, 4)])
    begin, near0, near1, near2, near3, far0, far1, wait_from, end = gather_parts(dy_ref, dy_out, *sems)
    begin()
    weights.wait()

    def project(i, _):
        slot = rest(i, 2)
        for at, fn in ((3, near0), (6, near1)):

            @pl.when(i == at)
            def _():
                fn()

        @pl.when(i < n - 1)
        def _():
            load(i + 1).start()

        @pl.when(i > 1)
        def _():
            store(i - 2).wait()

        load(i).wait()
        for r in range(0, tokens, 64):
            here = x[slot, r : r + 64].astype(f32)
            inverse = lax.rsqrt(jnp.mean(here * here, axis=1, keepdims=True) + norm_eps)
            hid[slot, r : r + 64] = (here * inverse * gain_ref[...]).astype(bf16)
        store(i).start()
        made = jnp.dot(hid[slot], w[...], preferred_element_type=f32).astype(bf16)
        qkv[i] = made.reshape(NSEG, rows, made.shape[1])
        return 0

    lax.fori_loop(0, n, project, 0)
    store(n - 2).wait()
    store(n - 1).wait()
    keep = pltpu.make_async_copy(qkv, qkv_out, q_sems.at[0])
    keep.start()
    hooks = {(0, 0): near2, (0, heads - 1): near3, (1, 0): far0, (1, heads - 1): far1} if heads > 1 else {}

    def segment(i, _):
        here = pl.ds(i, 1)
        for h in range(heads):
            for (seg, at), fn in hooks.items():
                if at == h:

                    @pl.when(i == seg)
                    def _():
                        fn()

            attention_head(
                h, heads, i, qkv.at[:, here], doc_col.at[here], doc_row.at[here], side_ref.at[here], blend_ref,
                mixed_ref.at[:, here], diff_ref.at[:, here], lse_ref.at[:, here], mem_ref, nv_ref,
            )
        return 0

    lax.fori_loop(0, NSEG, segment, 0)
    for d in (1, 3, 5, 7):
        wait_from(d)
    end()
    keep.wait()


def attend(x_all, gain, wqkv, dy, doc_col, doc_row, side, blend, heads, collective_id):
    n, tokens, width = x_all.shape
    rows = tokens // NSEG
    cw = heads * HEAD_DIM
    if n != 8 or heads == 1:
        here = x_all.reshape(n * tokens, width).astype(f32)
        inverse = lax.rsqrt(jnp.mean(here * here, axis=1, keepdims=True) + norm_eps)
        h_in = (here * inverse * gain).astype(bf16)
        qkv = mm(h_in, wqkv).astype(bf16).reshape(n, NSEG, rows, 3 * cw)
        dy = lax.all_gather(dy, "fsdp", axis=0)
        return h_in.reshape(x_all.shape), qkv, dy, *attention(qkv, doc_col, doc_row, side, blend, heads)
    length = n * rows
    sems = pltpu.SemaphoreType.DMA
    inside = pl.BlockSpec(memory_space=pltpu.VMEM)
    pairs = heads * NSEG * length * length // 2
    return pl.pallas_call(
        functools.partial(attend_kernel, heads),
        in_specs=[ANYWHERE, inside, ANYWHERE, ANYWHERE] + [inside] * 4,
        out_specs=[ANYWHERE] * 3 + [inside] * 5,
        out_shape=[
            jax.ShapeDtypeStruct(x_all.shape, bf16),
            jax.ShapeDtypeStruct((n, NSEG, rows, 3 * cw), bf16),
            jax.ShapeDtypeStruct((n, *dy.shape), bf16),
            jax.ShapeDtypeStruct((n, NSEG, rows, cw), bf16),
            jax.ShapeDtypeStruct((n, NSEG, rows, cw), f32),
            jax.ShapeDtypeStruct((heads, NSEG, length, 1), f32),
            jax.ShapeDtypeStruct((heads, HEAD_DIM, HEAD_DIM), f32),
            jax.ShapeDtypeStruct((heads, 1, HEAD_DIM), f32),
        ],
        scratch_shapes=[
            pltpu.VMEM((2, tokens, width), bf16),
            pltpu.VMEM(wqkv.shape, bf16),
            pltpu.VMEM((2, tokens, width), bf16),
            pltpu.VMEM((n, NSEG, rows, 3 * cw), bf16),
            *[sems((k,)) for k in (1, 2, 2, 1)],
            *GATHER_SEMS,
        ],
        compiler_params=params(collective_id, 48),
        cost_estimate=pl.CostEstimate(
            flops=pairs * 4 * HEAD_DIM + 6 * n * tokens * width * cw, transcendentals=pairs, bytes_accessed=32 << 20
        ),
        name="attend",
    )(x_all, gain, wqkv, dy, doc_col, doc_row, side, blend)


def quotient(a, b):
    return a // b if isinstance(a, int) else lax.div(a, b)


def rest(a, b):
    return a % b if isinstance(a, int) else lax.rem(a, b)


def xor(index, bits):
    total = 0
    for bit in (1, 2, 4):
        a, b = rest(quotient(index, bit), 2), rest(quotient(bits, bit), 2)
        total = total + bit * (a + b - 2 * a * b)
    return total


def nth_block(i):
    return i + quotient(i, 4) * (2 - 4 * rest(quotient(i, 2), 2))


def mlp_kernel(own_ref, wgu_ref, wd_ref, dy_ref, h_out, inner_out, dgu_out, out_ref, *refs):
    wgu, wd, h, dy, inner, dgu, mine, side, near, last, weight_sems, dy_sems, h_sems, inner_sems, dgu_sems, *sems = refs
    gather_sems, sems = sems[:15], sems[15:]
    me = lax.axis_index("fsdp")
    sib, xn, yn = flip(me, 1), flip(me, 2), flip(me, 4)
    tokens, width = own_ref.shape
    fw = wd.shape[0]
    begin, near0, near1, near2, near3, far0, far1, wait_from, gather_end = gather_parts(own_ref, h, *gather_sems)
    back = scatter_parts(mine, side, near, last, out_ref, sems)
    loads = [
        pltpu.make_async_copy(wgu_ref, wgu, weight_sems.at[0]),
        pltpu.make_async_copy(wd_ref, wd, weight_sems.at[1]),
    ]
    for load in loads:
        load.start()

    def load_dy(i):
        return pltpu.make_async_copy(dy_ref.at[xor(me, nth_block(i))], dy.at[rest(i, 2)], dy_sems.at[rest(i, 2)])

    load_dy(0).start()
    greet([sib, xn, yn])
    begin()
    back_x, back_far = back["combine"](2), back["combine"](6)
    hooks = {
        (0, 6): [near0],
        (1, 0): [lambda: wait_from(1)],
        (1, 2): [near1],
        (1, 6): [near2],
        (2, 0): [near3],
        (2, 6): [far0],
        (3, 0): [lambda: wait_from(3)],
        (3, 4): [far1],
        (4, 3): [back_x],
        (5, 0): [lambda: wait_from(7)],
        (6, 3): [back_far],
        (7, 0): [lambda: wait_from(5)],
        (7, 4): [lambda: back["onward"](0)],
        (7, 6): [lambda: back["onward"](1)],
    }
    loads[0].wait()
    loads[1].wait()
    tile = fw // 4
    wide = width // 4

    def store(i, ref, out, store_sems):
        slot = rest(i, 2)
        return pltpu.make_async_copy(ref.at[slot], out.at[xor(me, nth_block(i))], store_sems.at[slot])

    def keep(i):
        owner = xor(me, nth_block(i))
        return pltpu.make_async_copy(h.at[owner], h_out.at[owner], h_sems.at[i])

    def body(i, _):
        slot = rest(i, 2)
        block = nth_block(i)
        owner = xor(me, block)

        def point(p):
            for (step, at), fns in hooks.items():
                if at == p:

                    @pl.when(i == step)
                    def _():
                        for fn in fns:
                            fn()

        @pl.when(i < 7)
        def _():
            load_dy(i + 1).start()

        @pl.when(i > 1)
        def _():
            store(i - 2, inner, inner_out, inner_sems).wait()
            store(i - 2, dgu, dgu_out, dgu_sems).wait()

        for t in range(4):
            point(t)
            if t == 0:
                keep(i).start()
                load_dy(i).wait()
            left = h[owner]
            cols = slice(t * tile, (t + 1) * tile)
            gate = jnp.dot(left, wgu[:, cols], preferred_element_type=f32)
            up = jnp.dot(left, wgu[:, fw + t * tile : fw + (t + 1) * tile], preferred_element_type=f32)
            back_in = dots(dy[slot], wd[cols], 1, 1)
            sig = jax.nn.sigmoid(gate)
            act = gate * sig
            inner[slot, :, cols] = (act * up).astype(bf16)
            dgu[slot, :, cols] = (back_in * up * (sig * (1.0 + gate * (1.0 - sig)))).astype(bf16)
            dgu[slot, :, fw + t * tile : fw + (t + 1) * tile] = (back_in * act).astype(bf16)
        store(i, inner, inner_out, inner_sems).start()
        store(i, dgu, dgu_out, dgu_sems).start()
        for t in range(4):
            point(4 + t)
            cols = slice(t * wide, (t + 1) * wide)
            mine[block, :, cols] = dots(dgu[slot], wgu[cols], 1, 1).astype(bf16)

        @pl.when(lax.rem(block, 2) == 1)
        def _():
            back["to_core"](block).start()

        return 0

    lax.fori_loop(0, 8, body, 0)
    back["combine"](4)()
    back["onward"](2)
    back["combine"](0)()
    back["finish"]()
    for i in (6, 7):
        store(i, inner, inner_out, inner_sems).wait()
        store(i, dgu, dgu_out, dgu_sems).wait()
    for i in range(8):
        keep(i).wait()
    gather_end()


def scatter_parts(mine, side, near, last, out_ref, sems):
    me = lax.axis_index("fsdp")
    sib, xn, yn = flip(me, 1), flip(me, 2), flip(me, 4)
    rows = out_ref.shape[0] // PIECES
    half = PIECES // 2
    core, sems = sems[:2], sems[2:]
    hop = {"xf": sems[0:2], "xo": sems[2:4], "yf": sems[4:6], "yo": sems[6:8], "last": sems[8:10]}

    def to_core(d):
        kind = quotient(d, 2)
        return send(mine.at[d], side.at[kind], core, kind, sib)

    def span(c):
        return pl.ds(c * rows, rows)

    def go(copy):
        copy.start()

    def travel(d, c):
        if d == 6:
            return send(mine.at[6, span(c)], near.at[0, span(c)], hop["xf" if c < half else "yf"], c, xn if c < half else yn)
        if d == 2:
            return send(mine.at[2, span(c)], near.at[1, span(c)], hop["xo"], c, xn)
        return send(mine.at[4, span(c)], near.at[1, span(c)], hop["yo"], c, yn)

    def leaves(d, c):
        return d == 6 or (d == 2 and c < half) or (d == 4 and c >= half)

    def step_on(c):
        return send(mine.at[4 if c < half else 2, span(c)], last.at[span(c)], hop["last"], c, yn if c < half else xn)

    def add(d, c, ref):
        total = mine.at[d]

        def body(i, _):
            here = pl.ds(pl.multiple_of(c * rows + i * 16, 16), 16)
            total[here] = (total[here].astype(f32) + ref[here].astype(f32)).astype(bf16)
            return 0

        lax.fori_loop(0, rows // 16, body, 0)

    def combine(d):
        def run():
            send(side.at[d // 2], side.at[d // 2], core, d // 2, sib).wait_recv()
            for c in range(PIECES):
                add(d, c, side.at[d // 2])
                if leaves(d, c):
                    go(travel(d, c))

        return run

    def onward(which):
        for c in range(half) if which == 2 else [half + which]:
            d = 4 if c < half else 2
            send(near.at[0, span(c)], near.at[0, span(c)], hop["xf" if c < half else "yf"], c, xn).wait_recv()
            add(d, c, near.at[0])
            go(step_on(c))

    def finish():
        total, came = mine.at[0], near.at[1]
        for j in range(half):
            for c in (j + half, j):
                send(near.at[1, span(c)], near.at[1, span(c)], hop["xo" if c < half else "yo"], c, xn).wait_recv()
                send(last.at[span(c)], last.at[span(c)], hop["last"], c, xn).wait_recv()

                def body(i, _):
                    here = pl.ds(pl.multiple_of(c * rows + i * 16, 16), 16)
                    out_ref[here] = total[here].astype(f32) + came[here].astype(f32) + last[here].astype(f32)
                    return 0

                lax.fori_loop(0, rows // 16, body, 0)
        for d in (1, 3, 5, 7):
            to_core(d).wait_send()
        for d in (2, 4, 6):
            for c in range(PIECES):
                if leaves(d, c):
                    travel(d, c).wait_send()
        for c in range(PIECES):
            step_on(c).wait_send()

    return {"to_core": to_core, "combine": combine, "onward": onward, "finish": finish}


SCATTER_SEMS = [pltpu.SemaphoreType.DMA((4,))] * 2 + [pltpu.SemaphoreType.DMA((PIECES,))] * 10


def scatter_boxes(rows, columns):
    return [pltpu.VMEM((k, rows, columns), bf16) for k in (8, 4, 2)] + [pltpu.VMEM((rows, columns), bf16)]


def mlp(h_own, wgu, w_down, dy, collective_id):
    n, rows, width = dy.shape
    fw = w_down.shape[0]
    if n != 8:
        h = lax.all_gather(h_own, "fsdp", axis=0)
        gate_up = mm(h.reshape(n * rows, width), wgu)
        gate, up = gate_up[:, :fw], gate_up[:, fw:]
        sig = jax.nn.sigmoid(gate)
        inner = (gate * sig * up).astype(bf16)
        back_in = mm_t(dy.reshape(n * rows, width), w_down)
        d_gate = (back_in * up * (sig * (1.0 + gate * (1.0 - sig)))).astype(bf16)
        d_gu = jnp.concatenate([d_gate, (back_in * (gate * sig)).astype(bf16)], axis=1)
        d_h = lax.psum_scatter(mm_t(d_gu, wgu).astype(bf16), "fsdp", scatter_dimension=0, tiled=True).astype(f32)
        return h, inner.reshape(n, rows, fw), d_gu.reshape(n, rows, 2 * fw), d_h
    sems = pltpu.SemaphoreType.DMA
    return pl.pallas_call(
        mlp_kernel,
        in_specs=[ANYWHERE] * 4,
        out_specs=[ANYWHERE] * 3 + [pl.BlockSpec(memory_space=pltpu.VMEM)],
        out_shape=[
            jax.ShapeDtypeStruct((n, rows, width), bf16),
            jax.ShapeDtypeStruct((n, rows, fw), bf16),
            jax.ShapeDtypeStruct((n, rows, 2 * fw), bf16),
            jax.ShapeDtypeStruct((rows, width), f32),
        ],
        scratch_shapes=[
            pltpu.VMEM(wgu.shape, bf16),
            pltpu.VMEM(w_down.shape, bf16),
            pltpu.VMEM((n, rows, width), bf16),
            pltpu.VMEM((2, rows, width), bf16),
            pltpu.VMEM((2, rows, fw), bf16),
            pltpu.VMEM((2, rows, 2 * fw), bf16),
            *scatter_boxes(rows, width),
            *[sems((k,)) for k in (2, 2, 8, 2, 2)],
            *GATHER_SEMS,
            *SCATTER_SEMS,
        ],
        compiler_params=params(collective_id, 60),
        cost_estimate=pl.CostEstimate(flops=10 * n * rows * width * fw, transcendentals=n * rows * fw, bytes_accessed=64 << 20),
        name="mlp",
    )(h_own, wgu, w_down, dy)


def product_tiles(lhs, rhs, box, out_ref, sems, over_rows, hooks):
    columns = rhs.shape[1]
    count = out_ref.shape[0] // 256

    def rows(i):
        return pl.ds(pl.multiple_of(i * 256, 256), 256)

    def store(i):
        return pltpu.make_async_copy(
            box.at[rest(i, 2), :, pl.ds(0, columns)], out_ref.at[rows(i)], sems.at[rest(i, 2)]
        )

    def body(i, _):
        for step, fns in hooks.items():

            @pl.when(i == step)
            def _():
                for fn in fns:
                    fn()

        @pl.when(i > 1)
        def _():
            store(i - 2).wait()

        left = lhs[:, rows(i)] if over_rows else lhs[rows(i)]
        for at in range(0, columns, 512):
            here = slice(at, min(at + 512, columns))
            box[rest(i, 2), :, here] = dots(left, rhs[:, here], 0 if over_rows else 1, 0).astype(bf16)
        store(i).start()
        return 0

    lax.fori_loop(0, count, body, 0)
    for i in range(max(0, count - 2), count):
        store(i).wait()


def gather_grads_kernel(x_ref, inner_ref, dy_ref, h_ref, dgu_ref, out_ref, down_ref, gu_ref, inner, dy, h, dgu, box, load_sems, sems, *refs):
    loads = [
        pltpu.make_async_copy(src, dst, load_sems.at[i])
        for i, (src, dst) in enumerate(((inner_ref, inner), (dy_ref, dy), (h_ref, h), (dgu_ref, dgu)))
    ]
    for load in loads:
        load.start()
    me = lax.axis_index("fsdp")
    greet([other(me, d) for d in (1, 2, 4)])
    begin, near0, near1, near2, near3, far0, far1, wait_from, end = gather_parts(x_ref, out_ref, *refs)
    begin()
    loads[0].wait()
    loads[1].wait()
    product_tiles(inner, dy, box, down_ref, sems, True, {1: [near0], 3: [near1]})
    loads[2].wait()
    loads[3].wait()
    product_tiles(h, dgu, box, gu_ref, sems, True, {1: [near2], 3: [near3], 5: [far0], 7: [far1]})
    for d in (1, 3, 5, 7):
        wait_from(d)
    end()


def gather_grads(x, inner, dy, h, dgu, collective_id):
    n = lax.axis_size("fsdp")
    if n != 8:
        return lax.all_gather(x, "fsdp", axis=0), t_mm(inner, dy).astype(bf16), t_mm(h, dgu).astype(bf16)
    total, width = dy.shape
    sems = pltpu.SemaphoreType.DMA
    return pl.pallas_call(
        gather_grads_kernel,
        in_specs=[ANYWHERE] * 5,
        out_specs=[ANYWHERE] * 3,
        out_shape=[
            jax.ShapeDtypeStruct((n, *x.shape), bf16),
            jax.ShapeDtypeStruct((inner.shape[1], width), bf16),
            jax.ShapeDtypeStruct((width, dgu.shape[1]), bf16),
        ],
        scratch_shapes=[pltpu.VMEM(a.shape, bf16) for a in (inner, dy, h, dgu)]
        + [pltpu.VMEM((2, 256, max(width, dgu.shape[1])), bf16), sems((4,)), sems((2,)), *GATHER_SEMS],
        compiler_params=params(collective_id, 56),
        cost_estimate=pl.CostEstimate(
            flops=2 * total * width * (inner.shape[1] + dgu.shape[1]), transcendentals=0, bytes_accessed=48 << 20
        ),
        name="gather_grads",
    )(x, inner, dy, h, dgu)


def product_scatter_kernel(turned, tasks, *refs):
    (lhs_ref, rhs_ref), refs = refs[:2], refs[2:]
    task_ins, refs = refs[: 2 * len(tasks)], refs[2 * len(tasks) :]
    out_ref, refs = refs[0], refs[1:]
    task_outs, refs = refs[: len(tasks)], refs[len(tasks) :]
    (lhs, rhs, mine, side, near, last), refs = refs[:6], refs[6:]
    task_boxes, refs = refs[: 2 * len(tasks)], refs[2 * len(tasks) :]
    if tasks:
        box, store_sems, task_sems, *refs = refs
    load_sems, *sems = refs
    me = lax.axis_index("fsdp")
    loads = [pltpu.make_async_copy(lhs_ref, lhs, load_sems.at[0]), pltpu.make_async_copy(rhs_ref, rhs, load_sems.at[1])]
    task_loads = [pltpu.make_async_copy(task_ins[i], task_boxes[i], task_sems.at[i]) for i in range(2 * len(tasks))]
    for load in loads + task_loads:
        load.start()
    greet([other(me, d) for d in (1, 2, 4)])
    back = scatter_parts(mine, side, near, last, out_ref, sems)
    width = out_ref.shape[1]
    wide = width // 4
    combined = {2: back["combine"](6), 4: back["combine"](4), 6: back["combine"](2)}
    for load in loads:
        load.wait()

    def body(i, _):
        block = 6 - 2 * lax.div(i, 2) + lax.rem(i, 2)
        owner = xor(me, block)
        left = lhs[owner]
        for t in range(4):
            cols = slice(t * wide, (t + 1) * wide)
            made = dots(left, rhs[cols], 1, 1) if turned else dots(left, rhs[:, cols], 1, 0)
            mine[block, :, cols] = made.astype(bf16)

        @pl.when(lax.rem(block, 2) == 1)
        def _():
            back["to_core"](block).start()

        for step, fn in combined.items():

            @pl.when(i == step)
            def _():
                fn()

        return 0

    lax.fori_loop(0, 8, body, 0)
    todo = [lambda: back["combine"](0)(), lambda: back["onward"](0), lambda: back["onward"](1), lambda: back["onward"](2)]
    for k, (over_rows, places) in enumerate(tasks):
        task_loads[2 * k].wait()
        task_loads[2 * k + 1].wait()
        hooks = {place: [todo.pop(0)] for place in places}
        product_tiles(task_boxes[2 * k], task_boxes[2 * k + 1], box, task_outs[k], store_sems, over_rows, hooks)
    for fn in todo:
        fn()
    back["finish"]()


def product_scatter(lhs, rhs, turned, tasks, collective_id):
    n, rows, depth = lhs.shape
    width = rhs.shape[0] if turned else rhs.shape[1]
    if n != 8:
        made = (mm_t if turned else mm)(lhs.reshape(n * rows, depth), rhs).astype(bf16)
        made = lax.psum_scatter(made, "fsdp", scatter_dimension=0, tiled=True).astype(f32)
        return made, [(t_mm if over else mm)(a, b).astype(bf16) for a, b, over, _ in tasks]
    sems = pltpu.SemaphoreType.DMA
    pairs = [x for a, b, _, _ in tasks for x in (a, b)]
    results = [jax.ShapeDtypeStruct((a.shape[1] if over else a.shape[0], b.shape[1]), bf16) for a, b, over, _ in tasks]
    flops = 2 * n * rows * depth * width + sum(2 * a.size * b.shape[1] for a, b, _, _ in tasks)
    scratch = [pltpu.VMEM(lhs.shape, bf16), pltpu.VMEM(rhs.shape, bf16), *scatter_boxes(rows, width)]
    if tasks:
        scratch += [pltpu.VMEM(x.shape, bf16) for x in pairs]
        scratch += [pltpu.VMEM((2, 256, max(b.shape[1] for _, b, _, _ in tasks)), bf16), sems((2,)), sems((len(pairs),))]
    out, *made = pl.pallas_call(
        functools.partial(product_scatter_kernel, turned, [(over, places) for _, _, over, places in tasks]),
        in_specs=[ANYWHERE] * (2 + len(pairs)),
        out_specs=[pl.BlockSpec(memory_space=pltpu.VMEM)] + [ANYWHERE] * len(tasks),
        out_shape=[jax.ShapeDtypeStruct((rows, width), f32), *results],
        scratch_shapes=[*scratch, sems((2,)), *SCATTER_SEMS],
        compiler_params=params(collective_id, 60),
        cost_estimate=pl.CostEstimate(flops=flops, transcendentals=0, bytes_accessed=48 << 20),
        name="product_scatter",
    )(lhs, rhs, *pairs)
    return out, made


SLOTS = 4


def chunks_of(still, moved):
    out = []
    for t, rows in enumerate(still):
        out += [(t, None, r, 128) for r in range(0, rows, 128)]
    for t, (rows, size) in enumerate(moved):
        out += [(len(still) + t, d, r, size) for d in ORDER for r in range(0, rows, size)]
    return out


def line_kernel(still, moved, *refs):
    kinds = len(still) + len(moved)
    small_ref, refs = refs[0], refs[1:]
    ins, refs = refs[:kinds], refs[kinds:]
    small_out, refs = refs[0], refs[1:]
    outs, refs = refs[:kinds], refs[kinds:]
    first, refs = refs[:kinds], refs[kinds:]
    second, refs = refs[:kinds], refs[kinds:]
    come, refs = refs[: len(moved)], refs[len(moved) :]
    small_come, small_sum, small_in, small_back, small_sems, small_line, *refs = refs
    small_line_sems, refs = (small_line, refs[0]), refs[1:]
    small_move, refs = (small_sems, refs[0]), refs[1:]
    g_buf, a_buf, t_buf, b_buf, u_buf, loads, stores, *sems = refs
    move = [sems[2 * t : 2 * t + 2] for t in range(len(moved))]
    sems = sems[2 * len(moved) :]
    go_in, cross, back = sems[0:2], sems[2:4], sems[4:6]
    me, place = lax.axis_index("fsdp"), lax.axis_index("seq")
    is_end = (place == 0) | (place == 3)
    chunks = chunks_of(still, moved)
    inward = jnp.where(place < 2, 1, 2)
    outward = jnp.where(place < 2, 0, 3)
    opposite = 3 - inward
    barrier = pltpu.get_barrier_semaphore()
    for d in range(1, 8):
        pl.semaphore_signal(barrier, inc=1, device_id={"fsdp": other(me, d)}, device_id_type=pl.DeviceIdType.MESH)

    @pl.when(is_end)
    def _():
        pl.semaphore_signal(barrier, inc=1, device_id={"seq": inward}, device_id_type=pl.DeviceIdType.MESH)
        pl.semaphore_wait(barrier, 8)

    @pl.when(jnp.logical_not(is_end))
    def _():
        for peer in (outward, opposite):
            pl.semaphore_signal(barrier, inc=1, device_id={"seq": peer}, device_id_type=pl.DeviceIdType.MESH)
        pl.semaphore_wait(barrier, 9)

    def moving(t, d):
        ref = ins[len(still) + t]
        return link(ref.at[other(me, d)], come[t].at[me], move[t], d, "fsdp", other(me, d))

    def arrival(t, d):
        owner = other(me, d)
        return link(come[t].at[owner], come[t].at[owner], move[t], d, "fsdp", owner)

    def small_moving(d):
        return link(small_ref.at[other(me, d)], small_come.at[me], small_move, d, "fsdp", other(me, d))

    def small_arrival(d):
        there = small_come.at[other(me, d)]
        return link(there, there, small_move, d, "fsdp", other(me, d))

    def small_hop(src, dst, slot, peer):
        return link(src, dst, small_line_sems, slot, "seq", peer)

    for d in range(1, 8):
        small_moving(d).start()
    small_come[me] = small_ref[me]
    plan = [(t, d) for t in range(len(moved)) for d in ORDER[1:]]
    begun = []

    def feed(count):
        while plan and count:
            t, d = plan.pop(0)
            moving(t, d).start()
            begun.append((t, d))
            count -= 1

    def view(refs, k):
        t, d, r, rows = chunks[k]
        if d is None:
            return refs[t].at[pl.ds(r, rows)]
        return refs[t].at[other(me, d), pl.ds(r, rows)]

    def windows(k):
        t, d, r, rows = chunks[k]
        buf = box(u_buf, k, SLOTS)
        if d is None:
            return [(buf, outs[t].at[pl.ds(r, rows)])]
        kinds = outs[t].shape[0]
        c = ins[t].shape[2] // kinds
        columns = pl.ds(pl.multiple_of(other(me, d) * c, 128), c)
        return [(buf.at[:, pl.ds(i * c, c)], outs[t].at[i, pl.ds(r, rows), columns]) for i in range(kinds)]

    def source(k):
        t, d, r, rows = chunks[k]
        if d is None:
            return ins[t].at[pl.ds(r, rows)]
        if d == 0:
            return ins[t].at[me, pl.ds(r, rows)]
        return come[t - len(still)].at[other(me, d), pl.ds(r, rows)]

    def await_source(k):
        t, d, r, rows = chunks[k]
        if d and r == 0:
            arrival(t - len(still), d).wait_recv()

    def box(buf, k, depth):
        t, d, r, rows = chunks[k]
        return buf.at[k % depth, pl.ds(0, rows), pl.ds(0, ins[t].shape[-1])]

    def add(dst, left, right):
        rows = dst.shape[0]

        def body(i, _):
            here = pl.ds(pl.multiple_of(i * 16, 16), 16)
            dst[here] = (left[here].astype(f32) + right[here].astype(f32)).astype(bf16)
            return 0

        lax.fori_loop(0, rows // 16, body, 0)

    def end_send(k):
        return link(source(k), view(first, k), go_in, k, "seq", inward)

    def mid_cross(k):
        return link(box(t_buf, k, SLOTS), view(second, k), cross, k, "seq", opposite)

    def mid_back(k):
        return [link(src, dst, back, k, "seq", outward) for src, dst in windows(k)]

    def store(k):
        return [pltpu.make_async_copy(src, dst, stores.at[k % SLOTS]) for src, dst in windows(k)]

    def all_back(k):
        return link(box(u_buf, k, SLOTS), box(u_buf, k, SLOTS), back, k, "seq", outward)

    def all_stored(k):
        return pltpu.make_async_copy(box(u_buf, k, SLOTS), box(u_buf, k, SLOTS), stores.at[k % SLOTS])

    def finish(k):
        link(view(second, k), view(second, k), cross, k, "seq", opposite).wait_recv()
        load = pltpu.make_async_copy(view(second, k), box(b_buf, k, 2), loads.at[2])
        load.start()
        if k >= SLOTS:
            all_back(k - SLOTS).wait_send()
            all_stored(k - SLOTS).wait()
        load.wait()
        add(box(u_buf, k, SLOTS), box(t_buf, k, SLOTS), box(b_buf, k, 2))
        for copy in mid_back(k) + store(k):
            copy.start()

    count = len(chunks)
    feed(3)
    for d in range(1, 8):
        small_arrival(d).wait_recv()
    small_sum[...] = jnp.sum(small_come[...], axis=0)

    @pl.when(is_end)
    def _():
        small_hop(small_sum, small_in, 0, inward).start()

    @pl.when(jnp.logical_not(is_end))
    def _():
        small_hop(small_in, small_in, 0, outward).wait_recv()
        small_sum[...] = small_sum[...] + small_in[...]
        small_hop(small_sum, small_back, 1, opposite).start()

    for k in range(count):
        if k % 2 == 1:
            feed(1)
        await_source(k)

        @pl.when(is_end)
        def _():
            end_send(k).start()

        @pl.when(jnp.logical_not(is_end))
        def _():
            own = pltpu.make_async_copy(source(k), box(g_buf, k, 2), loads.at[0])
            own.start()
            link(view(first, k), view(first, k), go_in, k, "seq", outward).wait_recv()
            got = pltpu.make_async_copy(view(first, k), box(a_buf, k, 2), loads.at[1])
            got.start()
            if k >= SLOTS:
                mid_cross(k - SLOTS).wait_send()
            own.wait()
            got.wait()
            add(box(t_buf, k, SLOTS), box(g_buf, k, 2), box(a_buf, k, 2))
            mid_cross(k).start()
            if k >= 1:
                finish(k - 1)

    @pl.when(jnp.logical_not(is_end))
    def _():
        small_hop(small_back, small_back, 1, opposite).wait_recv()
        small_hop(small_sum, small_back, 1, opposite).wait_send()
        small_out[...] = small_sum[...] + small_back[...]
        small_hop(small_out, small_out, 2, outward).start()

    @pl.when(is_end)
    def _():
        small_hop(small_out, small_out, 2, inward).wait_recv()
        small_hop(small_sum, small_in, 0, inward).wait_send()
        for k in range(count):
            all_back(k).wait_recv()
            end_send(k).wait_send()

    @pl.when(jnp.logical_not(is_end))
    def _():
        finish(count - 1)
        small_hop(small_out, small_out, 2, outward).wait_send()
        for k in range(max(0, count - SLOTS), count):
            mid_cross(k).wait_send()
            all_back(k).wait_send()
            all_stored(k).wait()

    for t, d in begun:
        moving(t, d).wait_send()
    for d in range(1, 8):
        small_moving(d).wait_send()


def line_sum(small, still, moved, kinds, collective_id):
    if lax.axis_size("seq") != 4 or lax.axis_size("fsdp") != 8:
        out = []
        for x, count in zip(moved, kinds):
            n, rows, c = x.shape
            x = lax.psum(lax.all_to_all(x, "fsdp", split_axis=0, concat_axis=0, tiled=True), "seq")
            out.append(x.reshape(n, rows, count, c // count).transpose(2, 1, 0, 3).reshape(count, rows, n * (c // count)))
        small = lax.psum(lax.psum_scatter(small, "fsdp", scatter_dimension=0), "seq")
        return small, [lax.psum(x, "seq") for x in still], out
    still_rows = [x.shape[0] for x in still]
    moved_rows = [(x.shape[1], 128 if x.shape[2] > 1024 else 256) for x in moved]
    arrays = [*still, *moved]
    shapes = [jax.ShapeDtypeStruct(x.shape, bf16) for x in arrays]
    results = shapes[: len(still)] + [
        jax.ShapeDtypeStruct((count, x.shape[1], x.shape[0] * (x.shape[2] // count)), bf16) for x, count in zip(moved, kinds)
    ]
    count = len(chunks_of(still_rows, moved_rows))
    inside = pl.BlockSpec(memory_space=pltpu.VMEM)
    rows = max([128] + [size for _, size in moved_rows])
    width = max(x.shape[-1] for x in arrays)
    outs = pl.pallas_call(
        functools.partial(line_kernel, still_rows, moved_rows),
        in_specs=[inside] + [ANYWHERE] * len(arrays),
        out_specs=[inside] + [ANYWHERE] * (3 * len(arrays) + len(moved)),
        out_shape=[jax.ShapeDtypeStruct(small.shape[1:], f32)] + results + shapes * 2 + shapes[len(still) :],
        scratch_shapes=[pltpu.VMEM(small.shape, f32)]
        + [pltpu.VMEM(small.shape[1:], f32)] * 3
        + [pltpu.SemaphoreType.DMA((8,)), pltpu.SemaphoreType.DMA((3,)), pltpu.SemaphoreType.DMA((3,)), pltpu.SemaphoreType.DMA((8,))]
        + [pltpu.VMEM((depth, rows, width), bf16) for depth in (2, 2, SLOTS, 2, SLOTS)]
        + [pltpu.SemaphoreType.DMA((3,)), pltpu.SemaphoreType.DMA((SLOTS,))]
        + [pltpu.SemaphoreType.DMA((8,))] * (2 * len(moved))
        + [pltpu.SemaphoreType.DMA((count,))] * 6,
        compiler_params=params(collective_id, 40),
        name="line_sum",
    )(small, *arrays)
    small, *outs = outs
    return small, outs[: len(still)], outs[len(still) : len(arrays)]


def shards(
    tokens,
    doc_starts,
    norm_in,
    w_query,
    w_key,
    w_value,
    mix_bias,
    w_out,
    norm_mid,
    w_gate,
    w_up,
    w_down,
    cotangent,
):
    rows = tokens.shape[2]
    width = tokens.shape[3]
    n = lax.axis_size("fsdp")
    s = lax.axis_size("seq")
    own = NSEG * rows
    total = n * own
    seg_len = rows * n
    heads = HEADS // n
    cw = heads * HEAD_DIM
    fw = w_gate.shape[1] // n

    wgu = to_columns_in_turns([w_gate, w_up], 7)
    flat_in = tokens.reshape(own, width)
    all_in, gains, wqkv = front(flat_in, jnp.stack([norm_in, norm_mid]), [w_query, w_key, w_value], 0)
    gain_in, gain_mid = gains[0][None], gains[1][None]

    def normed(rows_in):
        rows_in = rows_in.astype(f32)
        inverse = lax.rsqrt(jnp.mean(rows_in * rows_in, axis=1, keepdims=True) + norm_eps)
        return rows_in * inverse, inverse

    flat_in = flat_in.astype(f32)
    normed_in, inv_in = normed(flat_in)
    start_row = doc_starts[0]
    docs = doc_number(start_row, jnp.arange(NSEG * seg_len, dtype=jnp.int32)).reshape(NSEG, seg_len)
    side = (docs == docs[1, 0]).astype(f32)[:, :, None]
    doc_col, doc_row = docs[:, :, None], docs[:, None, :]
    blend = jax.nn.sigmoid(mix_bias)
    blend_row = jnp.repeat(blend, HEAD_DIM)[None]
    h_in, qkv, dy, mixed, diff, lse, memory, norm_vec = attend(
        all_in, gain_in, wqkv, cotangent.reshape(own, width), doc_col, doc_row, side, blend_row, heads, 4
    )
    h_in, dy = h_in.reshape(total, width), dy.reshape(total, width)
    mixed = mixed.reshape(total, cw)

    attn_sum, _ = product_scatter(mixed.reshape(n, own, cw), w_out, False, [], 3)
    residual = flat_in + attn_sum
    inv_mid = lax.rsqrt(jnp.mean(residual * residual, axis=1, keepdims=True) + norm_eps)
    normed_mid = residual * inv_mid
    h_mid = (normed_mid * gain_mid).astype(bf16)
    h_mid, inner, d_gu, d_hmid = mlp(h_mid, wgu, w_down, dy.reshape(n, own, width), 1)
    h_mid, inner, d_gu = (x.reshape(total, x.shape[2]) for x in (h_mid, inner, d_gu))

    gain_mid_term = jnp.sum(normed_mid * d_hmid, axis=0)
    d_resid = cotangent.reshape(own, width).astype(f32) + norm_back(d_hmid * gain_mid, normed_mid, inv_mid)
    d_attn, part_down, part_gu = gather_grads(d_resid.astype(bf16), inner, dy, h_mid, d_gu, 2)
    d_attn = d_attn.reshape(total, width)
    part_gu = part_gu.reshape(n, width // n, 2 * fw)
    grad_down = lax.psum(part_down, "seq").astype(f32)

    d_mixed = mm_t(d_attn, w_out).reshape(n, NSEG, rows, cw)
    d_qkv, bias_rows = attention_back(
        qkv, d_mixed, diff, lse, doc_col, doc_row, side, blend_row, memory, norm_vec, heads
    )
    d_qkv = d_qkv.reshape(total, 3 * cw)
    bias_term = jnp.sum(bias_rows.reshape(heads, HEAD_DIM), axis=1) * blend * (1.0 - blend)

    d_hin, (part_mlp, part_out, part_qkv) = product_scatter(
        d_qkv.reshape(n, own, 3 * cw),
        wqkv,
        True,
        [(inner, w_down, False, (1, 4, 5, 6)), (mixed, d_attn, True, ()), (h_in, d_qkv, True, ())],
        5,
    )
    mlp_sum = lax.psum_scatter(part_mlp, "fsdp", scatter_dimension=0, tiled=True)
    block_out = (residual + mlp_sum.astype(f32)).astype(bf16).reshape(tokens.shape)
    part_qkv = part_qkv.reshape(n, width // n, 3 * cw)
    gain_in_term = jnp.sum(normed_in * d_hin, axis=0)
    per = width // n
    terms = jnp.stack([gain_in_term.reshape(n, per), gain_mid_term.reshape(n, per)], axis=1)
    mine = (jnp.arange(n) == lax.axis_index("fsdp"))[:, None, None]
    bias = jnp.where(mine, jnp.pad(bias_term, (0, per - heads))[None, None], 0.0)
    terms = jnp.concatenate([terms, bias, jnp.zeros((n, 5, per), f32)], axis=1)
    small, (sum_out,), (sum_gu, sum_qkv) = line_sum(terms, [part_out], [part_gu, part_qkv], [2, 3], 6)
    grad_out = sum_out.astype(f32)
    grad_gate, grad_up = sum_gu[0].astype(f32), sum_gu[1].astype(f32)
    grad_q, grad_k, grad_v = (sum_qkv[i].astype(f32) for i in range(3))
    grad_tokens = (d_resid + norm_back(d_hin * gain_in, normed_in, inv_in)).reshape(tokens.shape)

    return (
        block_out,
        grad_tokens,
        small[0],
        grad_q,
        grad_k,
        grad_v,
        small[2, :heads],
        grad_out,
        small[1],
        grad_gate,
        grad_up,
        grad_down,
    )


def solution(mesh):
    whole = P("seq", None, "fsdp", None)
    matrix, vector = P("fsdp", None), P("fsdp")
    return jax.shard_map(
        shards,
        mesh=mesh,
        in_specs=(whole, P("seq", None), vector, matrix, matrix, matrix, vector, matrix, vector, matrix, matrix, matrix, whole),
        out_specs=(whole, whole, vector, matrix, matrix, matrix, vector, matrix, vector, matrix, matrix, matrix),
        check_vma=False,
    )
```

time: 1170 us -> 894 us (0.76)
  matrix products: 166 us -> 7.1 us
  local copies, waits for them, and re-layouts: 137 us -> 20.9 us
  blocking collectives: 79.9 us -> 0 us
  Pallas kernels: 730 us -> 798 us
  other arithmetic: 25.1 us -> 40.5 us
    pallas_call x7, Pallas kernels: 290 us -> 407 us  [the longest x1 100 us: mlp(): pl.pallas_call(mlp_kernel, in_specs=[ANYWHERE] * 4, out_specs=[ANYWHERE]...]
    dot_general x8 -> x0, matrix products: 105 us -> none  [the longest x4 52.7 us: t_mm(): lax.dot_general(a, b, (((0,), (0,)), ((), ())), preferred_element_type=f32)]
    pallas_call x1, Pallas kernels: 414 us -> 356 us  [line_sum(): pl.pallas_call(functools.partial(line_kernel, still_rows, moved_rows), in...]
    dot_general x4 -> x1, matrix products: 60.6 us -> 7.1 us  [mm_t(): lax.dot_general(a, b, (((1,), (1,)), ((), ())), preferred_element_type=f32)]
    all_gather x1 -> x0, blocking collectives: 39.2 us -> none  [shards(): lax.all_gather(jnp.stack([norm_in, norm_mid]), 'fsdp', axis=1, tiled=True)]
    all_to_all x1 -> x0, blocking collectives: 31.8 us -> none  [to_columns(): out = lax.all_to_all(parts, 'fsdp', split_axis=1, concat_axis=0, tiled=True)]
    convert_element_type x2 -> x0, local copies, waits for them, and re-layouts: 26.8 us -> none  [to_rows(): parts = parts.reshape(n, rows, count, c // count).astype(f32)]
    unnamed x95 -> x52, local copies, waits for them, and re-layouts: 44 us -> 18.2 us
  transfers between devices with their start and end apart: 6 -> 3, of which waited for: 0 -> 0; matrix products, arithmetic and copies ran while one was open for 21% -> 5% of each run, Pallas kernels for 50% -> 69%
where the time goes in v2:
time: 894 us; the launch traced here: 882 us
  Pallas kernels  798 us (89%)
  other arithmetic  40.5 us (5%)
  local copies, waits for them, and re-layouts  20.9 us (2%)
  between operations  14.5 us (2%)
    pallas_call x1, Pallas kernels, line_sum(): pl.pallas_call(functools.partial(line_kernel, still_rows, moved_rows), in...  356 us
    pallas_call x1, Pallas kernels, mlp(): pl.pallas_call(mlp_kernel, in_specs=[ANYWHERE] * 4, out_specs=[ANYWHERE]...  100 us
    pallas_call x2, Pallas kernels, product_scatter(): pl.pallas_call(functools.partial(product_scatter_kernel, turned, [(over,...  94.8 us
    pallas_call x1, Pallas kernels, front(): pl.pallas_call(functools.partial(front_kernel, count), in_specs=[ANYWHERE...  74.5 us
    pallas_call x1, Pallas kernels, gather_grads(): pl.pallas_call(gather_grads_kernel, in_specs=[ANYWHERE] * 5, out_specs=[A...  65.8 us
    pallas_call x1, Pallas kernels, attend(): pl.pallas_call(functools.partial(attend_kernel, heads), in_specs=[ANYWHER...  43.9 us
    pallas_call x1, Pallas kernels, attention_back(): pl.pallas_call(functools.partial(attention_back_kernel, heads), grid=(NSE...  34.6 us
    pallas_call x1, Pallas kernels, to_columns_in_turns(): pl.pallas_call(functools.partial(move_kernel, count, share), in_specs=[AN...  28.3 us
  transfers between devices with their start and end apart: 3, of which 0 were waited for; matrix products, arithmetic and copies ran while one was open for 5% of the time, Pallas kernels for 69%

profile of v2, /device:TPU:0, one launch (start us, length us, event | category | flops | bytes accessed | tf_op | source)
XLA Modules:
  0.0 881.7 jit_solution(15788786756220100680)
XLA Ops:
  7.2 2.2 copy-done.2
  9.4 2.2 copy-done.3
  11.6 28.3 %move.1 = bf16[512,2048]{1,0:T(8,128)(2,1)} custom-call(bf16[256,8192]{1,0:T(8,128)(2,1)S(1)} %copy-done.2, bf16[256,8192]{1,0:T(8,128)(2,1)S(1)} %copy-done.3), custom_call_target="tpu_custom_call" | custom-call | tf_op jit(solution)/shard_map/move/pallas_call | solution.py:445
  40.7 0.9 sub.26.doc_col
  42.3 1.2 copy-done.8
  43.5 1.2 copy-done.9
  44.7 74.5 %front.1 = (bf16[8,256,2048]{2,1,0:T(8,128)(2,1)S(1)}, f32[8,8,256]{2,1,0:T(8,128)S(1)}, bf16[2048,768]{1,0:T(8,128)(2,1)S(1)}) custom-call(bf16[256,2048]{1,0:T(8,128)(2,1)S(1)} %bitcast.70, f32[8,256]{1,0:T(8,128)S(1)} %maximum_maximum_fusion.1.refs_1_, bf16[256,2048]{1,0:T(8,128)(2,1)S(1)} %copy-done.7, bf16[256,2048]{1,0:T(8,128)(2,1)S(1)} %copy-done.8, ...), custom_call_target="tpu_custom_call" | custom-call | tf_op jit(solution)/shard_map/front/pallas_call | solution.py:501
  119.2 3.4 copy-done.14
  122.6 1.7 copy-done.15
  124.4 0.8 compare_convert_fusion.side_ref
  125.6 43.9 %attend.1 = (bf16[8,256,2048]{2,1,0:T(8,128)(2,1)}, bf16[8,2,128,768]{3,2,1,0:T(8,128)(2,1)}, bf16[8,256,2048]{2,1,0:T(8,128)(2,1)}, bf16[8,2,128,256]{3,2,1,0:T...) custom-call(bf16[8,256,2048]{2,1,0:T(8,128)(2,1)} %copy-done.14, ...), custom_call_target="tpu_custom_call" | custom-call | flops 7516192768 | bytes 33554432 | tf_op jit(solution)/shard_map/attend/pallas_call | solution.py:608
  169.5 0.6 copy-done.10
  170.1 1.0 copy-done.16
  171.7 42.0 %product_scatter.2 = f32[256,2048]{1,0:T(8,128)} custom-call(bf16[8,256,256]{2,1,0:T(8,128)(2,1)} %bitcast.79, bf16[256,2048]{1,0:T(8,128)(2,1)} %refs_1_.2), custom_call_target="tpu_custom_call" | custom-call | flops 2147483648 | bytes 50331648 | tf_op jit(solution)/shard_map/product_scatter/pallas_call | solution.py:1061
  213.7 1.9 multiply_reduce_fusion.3
  215.6 1.3 copy-done.17
  216.9 1.2 multiply_convert_fusion.own_ref
  218.2 100.1 %mlp.1 = (bf16[8,256,2048]{2,1,0:T(8,128)(2,1)}, bf16[8,256,1024]{2,1,0:T(8,128)(2,1)}, bf16[8,256,2048]{2,1,0:T(8,128)(2,1)}, f32[256,2048]{1,0:T(8,128)}) custom-call(bf16[256,2048]{1,0:T(8,128)(2,1)} %multiply_convert_fusion.own_ref, bf16[2048,2048]{1,0:T(8,128)(2,1)} %bitcast.97, bf16[1024,2048]{1,0:T(8,128)(2,1)} %refs_3_.3, ...), custom_call_target="tpu_custom_call" | custom-call | flops 42949672960 | bytes 67108864 | tf_op jit(solution)/shard_map/mlp/pallas_call | solution.py:879
  318.3 2.9 multiply_reduce_fusion
  321.8 1.7 fusion.10.x_ref
  323.4 65.8 %gather_grads.1 = (bf16[8,256,2048]{2,1,0:T(8,128)(2,1)}, bf16[1024,2048]{1,0:T(8,128)(2,1)}, bf16[2048,2048]{1,0:T(8,128)(2,1)}) custom-call(bf16[256,2048]{1,0:T(8,128)(2,1)} %fusion.10.x_ref, bf16[2048,1024]{1,0:T(8,128)(2,1)} %bitcast.106, bf16[2048,2048]{1,0:T(8,128)(2,1)} %bitcast.101, bf16[2048,2048]{1,0:T(8,128)(2,1)} %bitcast.104, ...), custom_call_target="tpu_custom_call" | custom-call | flops 25769803776 | bytes 50331648 | tf_op jit(solution)/shard_map/gather_grads/pallas_call | solution.py:971
  389.4 1.1 copy-done.24
  390.5 7.1 fusion.8.dmix_ref
  397.6 34.6 %attention_back.1 = (bf16[8,2,128,768]{3,2,1,0:T(8,128)(2,1)}, f32[1,256]{1,0:T(1,128)}) custom-call(bf16[8,2,128,768]{3,2,1,0:T(8,128)(2,1)} %get-tuple-element.44.qkv_ref, f32[8,2,128,256]{3,2,1,0:T(8,128)} %fusion.8.dmix_ref, f32[8,2,128,256]{3,2,1,0:T(8,128)} %get-tuple-element.51.diff_ref, f32[2,2,1024,1]{3,2,1,0:T(8,128)} %get-tuple-element.52.lse_ref, ...), custom_call_target="tpu_custom_call" | custom-call | flops 2684354560 | bytes 16777216 | tf_op jit(solution)/shard_map/attention_back/pallas_call | solution.py:239
  432.2 52.8 %product_scatter.3 = (f32[256,2048]{1,0:T(8,128)}, bf16[2048,2048]{1,0:T(8,128)(2,1)}, bf16[256,2048]{1,0:T(8,128)(2,1)}, bf16[2048,768]{1,0:T(8,128)(2,1)}) custom-call(bf16[8,256,768]{2,1,0:T(8,128)(2,1)} %bitcast.98, bf16[2048,768]{1,0:T(8,128)(2,1)} %copy-done.15, bf16[2048,1024]{1,0:T(8,128)(2,1)} %bitcast.107, bf16[1024,2048]{1,0:T(8,128)(2,1)} %refs_3_.3, ...), custom_call_target="tpu_custom_call" | custom-call | flops 23622320128 | bytes 50331648 | tf_op jit(solution)/shard_map/product_scatter/pallas_call | solution.py:1061
  486.0 2.3 fusion.7
  488.3 356.4 %line_sum.1 = (f32[8,256]{1,0:T(8,128)S(1)}, bf16[256,2048]{1,0:T(8,128)(2,1)S(1)}, bf16[2,256,8192]{2,1,0:T(8,128)(2,1)}, bf16[3,256,2048]{2,1,0:T(8,128)(2,1)S...) custom-call(f32[8,8,256]{2,1,0:T(8,128)S(1)} %maximum_maximum_fusion, ...), custom_call_target="tpu_custom_call" | custom-call | tf_op jit(solution)/shard_map/line_sum/pallas_call | solution.py:1318
  844.7 1.6 convert_element_type.87
  847.3 2.9 bitcast_convert_fusion.2
  850.3 11.8 %bitcast_convert_fusion = (f32[256,8192]{1,0:T(8,128)}, f32[256,8192]{1,0:T(8,128)}) fusion(bf16[2,256,8192]{2,1,0:T(8,128)(2,1)} %get-tuple-element.66), kind=kLoop, calls=%fused_computation | loop fusion | flops 4194304 | bytes 25165824 | tf_op jit(solution)/shard_map/convert_element_type | solution.py:1427
  862.1 6.7 convert_element_type.92
  868.8 5.9 fusion.6
  (77 shorter events, 5.1 us)
Async XLA Ops:
  7.2 211.0 %all-gather.2.cloned.1.call-start = ((), (), s32[]{:S(2)}) async-start(), calls=%async_computation.1 | async-start | bytes 10485760 | tf_op jit(solution)/shard_map/all_gather | solution.py:455
  7.2 2.2 copy-start.2
  9.4 2.2 copy-start.3
  39.9 0.7 copy-start.23
  39.9 2.3 copy-start.21
  39.9 2.3 copy-start.22
  39.9 2.4 copy-start
  39.9 2.4 copy-start.7
  40.0 822.1 %all-reduce.3.cloned.1.call-start = ((), (), s32[]{:S(2)}) async-start(), calls=%async_computation.3 | async-start | bytes 8388608 | tf_op jit(solution)/shard_map/psum | solution.py:1400
  40.6 84.6 %copy-start.11 = (s32[2048]{0:T(1024)}, s32[2048]{0:T(1024)S(1)}, u32[]{:S(2)}) copy-start(s32[2048]{0:T(1024)S(1)} %broadcast_add_fusion) | copy-start | bytes 24580
  41.5 83.7 %copy-start.1 = (s32[2,1024,1]{2,1,0:T(8,128)}, s32[2,1024,1]{2,1,0:T(8,128)S(1)}, u32[]{:S(2)}) copy-start(s32[2,1024,1]{2,1,0:T(8,128)S(1)} %sub.26.doc_col) | copy-start | bytes 24580
  42.3 1.2 copy-start.8
  43.5 1.2 copy-start.9
  44.7 79.6 %copy-start.25 = (f32[2]{0:T(128)S(1)}, f32[2]{0:T(128)}, u32[]{:S(2)}) copy-start(f32[2]{0:T(128)} %param.19) | copy-start | bytes 28
  119.2 3.4 copy-start.14
  122.6 1.7 copy-start.15
  124.3 1.3 copy-start.4
  125.2 44.3 %copy-start.5 = (f32[2,1024,1]{2,1,0:T(8,128)}, f32[2,1024,1]{2,1,0:T(8,128)S(1)}, u32[]{:S(2)}) copy-start(f32[2,1024,1]{2,1,0:T(8,128)S(1)} %compare_convert_fusion.side_ref) | copy-start | bytes 24580
  125.2 44.2 %copy-start.12 = (f32[2,128]{1,0:T(2,128)}, f32[2,128]{1,0:T(2,128)S(1)}, u32[]{:S(2)}) copy-start(f32[2,128]{1,0:T(2,128)S(1)} %broadcast_in_dim.38) | copy-start | bytes 3076
  169.5 0.7 copy-start.10
  170.1 1.0 copy-start.16
  171.1 0.6 copy-start.13
  215.6 1.3 copy-start.17
  318.3 3.0 copy-start.18
  318.3 3.5 copy-start.19
  389.3 1.2 copy-start.24
  389.3 479.4 %reduce-scatter.2.cloned.1.call-start = ((), (), s32[]{:S(2)}) async-start(), calls=%async_computation.2 | async-start | bytes 9437184 | tf_op jit(solution)/shard_map/reduce_scatter | solution.py:1416
  485.1 0.7 copy-start.20
  485.2 3.1 copy-start.6
Sparse Core Ops, SparseCore 0:
  40.1 149.9 all-gather.1
  389.4 198.5 all-reduce.2
  591.9 96.5 reduce-scatter.1

commit v3 on v2

--- a/solution.py
+++ b/solution.py
@@ -291,7 +291,7 @@
 GATHER_SEMS = [pltpu.SemaphoreType.DMA] + [pltpu.SemaphoreType.DMA((PIECES,))] * 14
 
 
-def gather_parts(x_ref, out_ref, local_sem, *sems):
+def gather_parts(x_ref, out_ref, local_sem, *sems, own_first=False):
     me = lax.axis_index("fsdp")
     sib, xn, yn, far_owner = flip(me, 1), flip(me, 2), flip(me, 4), other(me, 6)
     rows = x_ref.shape[0] // PIECES
@@ -322,14 +322,15 @@
         return send(mine(c), at(me, c), sems, c, peer)
 
     def begin():
+        local.start()
         for j in range(PIECES):
             c, d = j, (j + half) % PIECES
             go(functools.partial(begin_one, c, over_x, xn))
             go(functools.partial(begin_one, d, over_y, yn))
         for c in range(PIECES):
             go(functools.partial(begin_one, c, own, sib))
-        local.start()
-        local.wait()
+        if own_first:
+            local.wait()
 
     def near(j):
         c, d = j, (j + half) % PIECES
@@ -354,6 +355,8 @@
     def end():
         for make in started:
             make().wait_send()
+        if not own_first:
+            local.wait()
 
     near_steps = [functools.partial(near, j) for j in range(PIECES)]
     far_steps = [functools.partial(beyond, j) for j in range(half)]
@@ -375,7 +378,7 @@
     return pltpu.CompilerParams(collective_id=collective_id, has_side_effects=True, vmem_limit_bytes=mib << 20)
 
 
-ANYWHERE = pl.BlockSpec(memory_space=pl.ANY)
+ANYWHERE = pl.BlockSpec(memory_space=pltpu.HBM)
 
 
 def move_steps(ins, out_ref, first, rows, sems, local_sem):
@@ -655,14 +658,14 @@
     return i + quotient(i, 4) * (2 - 4 * rest(quotient(i, 2), 2))
 
 
-def mlp_kernel(own_ref, wgu_ref, wd_ref, dy_ref, h_out, inner_out, dgu_out, out_ref, *refs):
+def mlp_kernel(own_ref, wgu_ref, wd_ref, dy_ref, h_out, inner_out, dgu_out, down_out, out_ref, *refs):
     wgu, wd, h, dy, inner, dgu, mine, side, near, last, weight_sems, dy_sems, h_sems, inner_sems, dgu_sems, *sems = refs
     gather_sems, sems = sems[:15], sems[15:]
     me = lax.axis_index("fsdp")
     sib, xn, yn = flip(me, 1), flip(me, 2), flip(me, 4)
     tokens, width = own_ref.shape
     fw = wd.shape[0]
-    begin, near0, near1, near2, near3, far0, far1, wait_from, gather_end = gather_parts(own_ref, h, *gather_sems)
+    begin, near0, near1, near2, near3, far0, far1, wait_from, gather_end = gather_parts(own_ref, h, *gather_sems, own_first=True)
     back = scatter_parts(mine, side, near, last, out_ref, sems)
     loads = [
         pltpu.make_async_copy(wgu_ref, wgu, weight_sems.at[0]),
@@ -672,9 +675,11 @@
         load.start()
 
     def load_dy(i):
-        return pltpu.make_async_copy(dy_ref.at[xor(me, nth_block(i))], dy.at[rest(i, 2)], dy_sems.at[rest(i, 2)])
-
-    load_dy(0).start()
+        owner = xor(me, nth_block(i))
+        return pltpu.make_async_copy(dy_ref.at[owner], dy.at[owner], dy_sems.at[i])
+
+    for i in range(8):
+        load_dy(i).start()
     greet([sib, xn, yn])
     begin()
     back_x, back_far = back["combine"](2), back["combine"](6)
@@ -699,13 +704,17 @@
     tile = fw // 4
     wide = width // 4
 
-    def store(i, ref, out, store_sems):
+    def store(i):
         slot = rest(i, 2)
-        return pltpu.make_async_copy(ref.at[slot], out.at[xor(me, nth_block(i))], store_sems.at[slot])
+        return pltpu.make_async_copy(dgu.at[slot], dgu_out.at[xor(me, nth_block(i))], dgu_sems.at[slot])
 
     def keep(i):
         owner = xor(me, nth_block(i))
         return pltpu.make_async_copy(h.at[owner], h_out.at[owner], h_sems.at[i])
+
+    def keep_inner(i):
+        owner = xor(me, nth_block(i))
+        return pltpu.make_async_copy(inner.at[owner], inner_out.at[owner], inner_sems.at[i])
 
     def body(i, _):
         slot = rest(i, 2)
@@ -721,14 +730,9 @@
                         for fn in fns:
                             fn()
 
-        @pl.when(i < 7)
-        def _():
-            load_dy(i + 1).start()
-
         @pl.when(i > 1)
         def _():
-            store(i - 2, inner, inner_out, inner_sems).wait()
-            store(i - 2, dgu, dgu_out, dgu_sems).wait()
+            store(i - 2).wait()
 
         for t in range(4):
             point(t)
@@ -739,14 +743,14 @@
             cols = slice(t * tile, (t + 1) * tile)
             gate = jnp.dot(left, wgu[:, cols], preferred_element_type=f32)
             up = jnp.dot(left, wgu[:, fw + t * tile : fw + (t + 1) * tile], preferred_element_type=f32)
-            back_in = dots(dy[slot], wd[cols], 1, 1)
+            back_in = dots(dy[owner], wd[cols], 1, 1)
             sig = jax.nn.sigmoid(gate)
             act = gate * sig
-            inner[slot, :, cols] = (act * up).astype(bf16)
+            inner[owner, :, cols] = (act * up).astype(bf16)
             dgu[slot, :, cols] = (back_in * up * (sig * (1.0 + gate * (1.0 - sig)))).astype(bf16)
             dgu[slot, :, fw + t * tile : fw + (t + 1) * tile] = (back_in * act).astype(bf16)
-        store(i, inner, inner_out, inner_sems).start()
-        store(i, dgu, dgu_out, dgu_sems).start()
+        keep_inner(i).start()
+        store(i).start()
         for t in range(4):
             point(4 + t)
             cols = slice(t * wide, (t + 1) * wide)
@@ -762,12 +766,26 @@
     back["combine"](4)()
     back["onward"](2)
     back["combine"](0)()
+    store(6).wait()
+    store(7).wait()
+
+    def keep_down(t):
+        return pltpu.make_async_copy(dgu.at[t % 2], down_out.at[pl.ds(t * tile, tile)], dgu_sems.at[t % 2])
+
+    for t in range(4):
+        if t > 1:
+            keep_down(t - 2).wait()
+        left = inner[:, :, t * tile : (t + 1) * tile].reshape(8 * tokens, tile)
+        for at in range(0, width, wide):
+            right = dy[:, :, at : at + wide].reshape(8 * tokens, wide)
+            dgu[t % 2, :, at : at + wide] = dots(left, right, 0, 0).astype(bf16)
+        keep_down(t).start()
     back["finish"]()
-    for i in (6, 7):
-        store(i, inner, inner_out, inner_sems).wait()
-        store(i, dgu, dgu_out, dgu_sems).wait()
+    keep_down(2).wait()
+    keep_down(3).wait()
     for i in range(8):
         keep(i).wait()
+        keep_inner(i).wait()
     gather_end()
 
 
@@ -874,27 +892,29 @@
         d_gate = (back_in * up * (sig * (1.0 + gate * (1.0 - sig)))).astype(bf16)
         d_gu = jnp.concatenate([d_gate, (back_in * (gate * sig)).astype(bf16)], axis=1)
         d_h = lax.psum_scatter(mm_t(d_gu, wgu).astype(bf16), "fsdp", scatter_dimension=0, tiled=True).astype(f32)
-        return h, inner.reshape(n, rows, fw), d_gu.reshape(n, rows, 2 * fw), d_h
+        down = t_mm(inner, dy.reshape(n * rows, width)).astype(bf16)
+        return h, inner.reshape(n, rows, fw), d_gu.reshape(n, rows, 2 * fw), down, d_h
     sems = pltpu.SemaphoreType.DMA
     return pl.pallas_call(
         mlp_kernel,
         in_specs=[ANYWHERE] * 4,
-        out_specs=[ANYWHERE] * 3 + [pl.BlockSpec(memory_space=pltpu.VMEM)],
+        out_specs=[ANYWHERE] * 4 + [pl.BlockSpec(memory_space=pltpu.VMEM)],
         out_shape=[
             jax.ShapeDtypeStruct((n, rows, width), bf16),
             jax.ShapeDtypeStruct((n, rows, fw), bf16),
             jax.ShapeDtypeStruct((n, rows, 2 * fw), bf16),
+            jax.ShapeDtypeStruct((fw, width), bf16),
             jax.ShapeDtypeStruct((rows, width), f32),
         ],
         scratch_shapes=[
             pltpu.VMEM(wgu.shape, bf16),
             pltpu.VMEM(w_down.shape, bf16),
             pltpu.VMEM((n, rows, width), bf16),
-            pltpu.VMEM((2, rows, width), bf16),
-            pltpu.VMEM((2, rows, fw), bf16),
+            pltpu.VMEM((n, rows, width), bf16),
+            pltpu.VMEM((n, rows, fw), bf16),
             pltpu.VMEM((2, rows, 2 * fw), bf16),
             *scatter_boxes(rows, width),
-            *[sems((k,)) for k in (2, 2, 8, 2, 2)],
+            *[sems((k,)) for k in (2, 8, 8, 8, 2)],
             *GATHER_SEMS,
             *SCATTER_SEMS,
         ],
@@ -940,168 +960,133 @@
         store(i).wait()
 
 
-def gather_grads_kernel(x_ref, inner_ref, dy_ref, h_ref, dgu_ref, out_ref, down_ref, gu_ref, inner, dy, h, dgu, box, load_sems, sems, *refs):
+def gather_products_kernel(x_ref, h_ref, dgu_ref, inner_ref, wd_ref, out_ref, gu_ref, mlp_ref, h, dgu, inner, wd, box, load_sems, sems, *refs):
     loads = [
         pltpu.make_async_copy(src, dst, load_sems.at[i])
-        for i, (src, dst) in enumerate(((inner_ref, inner), (dy_ref, dy), (h_ref, h), (dgu_ref, dgu)))
+        for i, (src, dst) in enumerate(((h_ref, h), (dgu_ref, dgu), (inner_ref, inner), (wd_ref, wd)))
     ]
-    for load in loads:
-        load.start()
     me = lax.axis_index("fsdp")
     greet([other(me, d) for d in (1, 2, 4)])
     begin, near0, near1, near2, near3, far0, far1, wait_from, end = gather_parts(x_ref, out_ref, *refs)
     begin()
+    for load in loads:
+        load.start()
     loads[0].wait()
     loads[1].wait()
-    product_tiles(inner, dy, box, down_ref, sems, True, {1: [near0], 3: [near1]})
+    product_tiles(h, dgu, box, gu_ref, sems, True, {1: [near0], 3: [near1], 5: [near2], 7: [near3]})
     loads[2].wait()
     loads[3].wait()
-    product_tiles(h, dgu, box, gu_ref, sems, True, {1: [near2], 3: [near3], 5: [far0], 7: [far1]})
+    product_tiles(inner, wd, box, mlp_ref, sems, False, {3: [far0], 7: [far1]})
     for d in (1, 3, 5, 7):
         wait_from(d)
     end()
 
 
-def gather_grads(x, inner, dy, h, dgu, collective_id):
+def gather_products(x, h, dgu, inner, w_down, collective_id):
     n = lax.axis_size("fsdp")
     if n != 8:
-        return lax.all_gather(x, "fsdp", axis=0), t_mm(inner, dy).astype(bf16), t_mm(h, dgu).astype(bf16)
-    total, width = dy.shape
+        return lax.all_gather(x, "fsdp", axis=0), t_mm(h, dgu).astype(bf16), mm(inner, w_down).astype(bf16)
+    total, width = h.shape
     sems = pltpu.SemaphoreType.DMA
     return pl.pallas_call(
-        gather_grads_kernel,
+        gather_products_kernel,
         in_specs=[ANYWHERE] * 5,
         out_specs=[ANYWHERE] * 3,
         out_shape=[
             jax.ShapeDtypeStruct((n, *x.shape), bf16),
-            jax.ShapeDtypeStruct((inner.shape[1], width), bf16),
             jax.ShapeDtypeStruct((width, dgu.shape[1]), bf16),
+            jax.ShapeDtypeStruct((total, width), bf16),
         ],
-        scratch_shapes=[pltpu.VMEM(a.shape, bf16) for a in (inner, dy, h, dgu)]
+        scratch_shapes=[pltpu.VMEM(a.shape, bf16) for a in (h, dgu, inner, w_down)]
         + [pltpu.VMEM((2, 256, max(width, dgu.shape[1])), bf16), sems((4,)), sems((2,)), *GATHER_SEMS],
         compiler_params=params(collective_id, 56),
         cost_estimate=pl.CostEstimate(
             flops=2 * total * width * (inner.shape[1] + dgu.shape[1]), transcendentals=0, bytes_accessed=48 << 20
         ),
-        name="gather_grads",
-    )(x, inner, dy, h, dgu)
-
-
-def product_scatter_kernel(turned, tasks, *refs):
-    (lhs_ref, rhs_ref), refs = refs[:2], refs[2:]
-    task_ins, refs = refs[: 2 * len(tasks)], refs[2 * len(tasks) :]
-    out_ref, refs = refs[0], refs[1:]
-    task_outs, refs = refs[: len(tasks)], refs[len(tasks) :]
-    (lhs, rhs, mine, side, near, last), refs = refs[:6], refs[6:]
-    task_boxes, refs = refs[: 2 * len(tasks)], refs[2 * len(tasks) :]
-    if tasks:
-        box, store_sems, task_sems, *refs = refs
-    load_sems, *sems = refs
+        name="gather_products",
+    )(x, h, dgu, inner, w_down)
+
+
+def block_products(me, lhs, rhs, mine, turned, back, block):
+    wide = mine.shape[2] // 4
+    left = lhs[xor(me, block)]
+    for t in range(4):
+        cols = slice(t * wide, (t + 1) * wide)
+        made = dots(left, rhs[cols], 1, 1) if turned else dots(left, rhs[:, cols], 1, 0)
+        mine[block, :, cols] = made.astype(bf16)
+    if block % 2 == 1:
+        back["to_core"](block).start()
+
+
+def product_scatter_kernel(lhs_ref, rhs_ref, out_ref, lhs, rhs, mine, side, near, last, load_sems, *sems):
     me = lax.axis_index("fsdp")
     loads = [pltpu.make_async_copy(lhs_ref, lhs, load_sems.at[0]), pltpu.make_async_copy(rhs_ref, rhs, load_sems.at[1])]
-    task_loads = [pltpu.make_async_copy(task_ins[i], task_boxes[i], task_sems.at[i]) for i in range(2 * len(tasks))]
-    for load in loads + task_loads:
+    for load in loads:
         load.start()
     greet([other(me, d) for d in (1, 2, 4)])
     back = scatter_parts(mine, side, near, last, out_ref, sems)
-    width = out_ref.shape[1]
-    wide = width // 4
-    combined = {2: back["combine"](6), 4: back["combine"](4), 6: back["combine"](2)}
     for load in loads:
         load.wait()
-
-    def body(i, _):
-        block = 6 - 2 * lax.div(i, 2) + lax.rem(i, 2)
-        owner = xor(me, block)
-        left = lhs[owner]
-        for t in range(4):
-            cols = slice(t * wide, (t + 1) * wide)
-            made = dots(left, rhs[cols], 1, 1) if turned else dots(left, rhs[:, cols], 1, 0)
-            mine[block, :, cols] = made.astype(bf16)
-
-        @pl.when(lax.rem(block, 2) == 1)
-        def _():
-            back["to_core"](block).start()
-
-        for step, fn in combined.items():
-
-            @pl.when(i == step)
-            def _():
-                fn()
-
-        return 0
-
-    lax.fori_loop(0, 8, body, 0)
-    todo = [lambda: back["combine"](0)(), lambda: back["onward"](0), lambda: back["onward"](1), lambda: back["onward"](2)]
-    for k, (over_rows, places) in enumerate(tasks):
-        task_loads[2 * k].wait()
-        task_loads[2 * k + 1].wait()
-        hooks = {place: [todo.pop(0)] for place in places}
-        product_tiles(task_boxes[2 * k], task_boxes[2 * k + 1], box, task_outs[k], store_sems, over_rows, hooks)
-    for fn in todo:
-        fn()
+    for block in (6, 7, 4, 5, 2, 3, 0, 1):
+        block_products(me, lhs, rhs, mine, False, back, block)
+        if block in (4, 2, 0):
+            back["combine"](block + 2)()
+    back["combine"](0)()
+    for which in range(3):
+        back["onward"](which)
     back["finish"]()
 
 
-def product_scatter(lhs, rhs, turned, tasks, collective_id):
+def product_scatter(lhs, rhs, collective_id):
     n, rows, depth = lhs.shape
-    width = rhs.shape[0] if turned else rhs.shape[1]
+    width = rhs.shape[1]
     if n != 8:
-        made = (mm_t if turned else mm)(lhs.reshape(n * rows, depth), rhs).astype(bf16)
-        made = lax.psum_scatter(made, "fsdp", scatter_dimension=0, tiled=True).astype(f32)
-        return made, [(t_mm if over else mm)(a, b).astype(bf16) for a, b, over, _ in tasks]
+        made = mm(lhs.reshape(n * rows, depth), rhs).astype(bf16)
+        return lax.psum_scatter(made, "fsdp", scatter_dimension=0, tiled=True).astype(f32)
     sems = pltpu.SemaphoreType.DMA
-    pairs = [x for a, b, _, _ in tasks for x in (a, b)]
-    results = [jax.ShapeDtypeStruct((a.shape[1] if over else a.shape[0], b.shape[1]), bf16) for a, b, over, _ in tasks]
-    flops = 2 * n * rows * depth * width + sum(2 * a.size * b.shape[1] for a, b, _, _ in tasks)
-    scratch = [pltpu.VMEM(lhs.shape, bf16), pltpu.VMEM(rhs.shape, bf16), *scatter_boxes(rows, width)]
-    if tasks:
-        scratch += [pltpu.VMEM(x.shape, bf16) for x in pairs]
-        scratch += [pltpu.VMEM((2, 256, max(b.shape[1] for _, b, _, _ in tasks)), bf16), sems((2,)), sems((len(pairs),))]
-    out, *made = pl.pallas_call(
-        functools.partial(product_scatter_kernel, turned, [(over, places) for _, _, over, places in tasks]),
-        in_specs=[ANYWHERE] * (2 + len(pairs)),
-        out_specs=[pl.BlockSpec(memory_space=pltpu.VMEM)] + [ANYWHERE] * len(tasks),
-        out_shape=[jax.ShapeDtypeStruct((rows, width), f32), *results],
-        scratch_shapes=[*scratch, sems((2,)), *SCATTER_SEMS],
-        compiler_params=params(collective_id, 60),
-        cost_estimate=pl.CostEstimate(flops=flops, transcendentals=0, bytes_accessed=48 << 20),
+    return pl.pallas_call(
+        product_scatter_kernel,
+        in_specs=[ANYWHERE] * 2,
+        out_specs=pl.BlockSpec(memory_space=pltpu.VMEM),
+        out_shape=jax.ShapeDtypeStruct((rows, width), f32),
+        scratch_shapes=[pltpu.VMEM(lhs.shape, bf16), pltpu.VMEM(rhs.shape, bf16), *scatter_boxes(rows, width), sems((2,)), *SCATTER_SEMS],
+        compiler_params=params(collective_id, 40),
+        cost_estimate=pl.CostEstimate(flops=2 * n * rows * depth * width, transcendentals=0, bytes_accessed=8 << 20),
         name="product_scatter",
-    )(lhs, rhs, *pairs)
-    return out, made
+    )(lhs, rhs)
 
 
 SLOTS = 4
 
 
-def chunks_of(still, moved):
-    out = []
-    for t, rows in enumerate(still):
-        out += [(t, None, r, 128) for r in range(0, rows, 128)]
-    for t, (rows, size) in enumerate(moved):
-        out += [(len(still) + t, d, r, size) for d in ORDER for r in range(0, rows, size)]
-    return out
-
-
-def line_kernel(still, moved, *refs):
-    kinds = len(still) + len(moved)
-    small_ref, refs = refs[0], refs[1:]
-    ins, refs = refs[:kinds], refs[kinds:]
-    small_out, refs = refs[0], refs[1:]
+def chunks_of(gu_rows, out_rows, qkv_rows):
+    out = [(0, d, r, 64) for d in ORDER for r in range(0, gu_rows, 64)]
+    out += [(1, None, r, 64) for r in range(0, out_rows, 64)]
+    return out + [(2, d, r, 128) for d in ORDER for r in range(0, qkv_rows, 128)]
+
+
+def finish_kernel(*refs):
+    small_ref, normed_ref, gu_ref, dqkv_ref, wqkv_ref, mixed_ref, dattn_ref, hin_ref, *refs = refs
+    small_out, dhin_ref, part_out, part_qkv, *refs = refs
+    ins = [gu_ref, part_out, part_qkv]
+    kinds = 3
     outs, refs = refs[:kinds], refs[kinds:]
     first, refs = refs[:kinds], refs[kinds:]
     second, refs = refs[:kinds], refs[kinds:]
-    come, refs = refs[: len(moved)], refs[len(moved) :]
-    small_come, small_sum, small_in, small_back, small_sems, small_line, *refs = refs
-    small_line_sems, refs = (small_line, refs[0]), refs[1:]
-    small_move, refs = (small_sems, refs[0]), refs[1:]
+    come, refs = {0: refs[0], 2: refs[1]}, refs[2:]
+    (dqkv, wqkv, mixed, dattn, hin, tiles), refs = refs[:6], refs[6:]
+    (mine, side, near, last), refs = refs[:4], refs[4:]
+    (task_loads, box_sems), refs = refs[:2], refs[2:]
+    scatter_sems, refs = refs[: len(SCATTER_SEMS)], refs[len(SCATTER_SEMS) :]
+    small_work, small_come, small_sum, small_in, small_back, *refs = refs
+    small_move, small_line_sems, refs = refs[0:2], refs[2:4], refs[4:]
     g_buf, a_buf, t_buf, b_buf, u_buf, loads, stores, *sems = refs
-    move = [sems[2 * t : 2 * t + 2] for t in range(len(moved))]
-    sems = sems[2 * len(moved) :]
+    move = {0: sems[0:2], 2: sems[2:4]}
+    sems = sems[4:]
     go_in, cross, back = sems[0:2], sems[2:4], sems[4:6]
     me, place = lax.axis_index("fsdp"), lax.axis_index("seq")
     is_end = (place == 0) | (place == 3)
-    chunks = chunks_of(still, moved)
+    chunks = chunks_of(gu_ref.shape[1], part_out.shape[0], part_qkv.shape[1])
     inward = jnp.where(place < 2, 1, 2)
     outward = jnp.where(place < 2, 0, 3)
     opposite = 3 - inward
@@ -1121,15 +1106,14 @@
         pl.semaphore_wait(barrier, 9)
 
     def moving(t, d):
-        ref = ins[len(still) + t]
-        return link(ref.at[other(me, d)], come[t].at[me], move[t], d, "fsdp", other(me, d))
+        return link(ins[t].at[other(me, d)], come[t].at[me], move[t], d, "fsdp", other(me, d))
 
     def arrival(t, d):
         owner = other(me, d)
         return link(come[t].at[owner], come[t].at[owner], move[t], d, "fsdp", owner)
 
     def small_moving(d):
-        return link(small_ref.at[other(me, d)], small_come.at[me], small_move, d, "fsdp", other(me, d))
+        return link(small_work.at[other(me, d)], small_come.at[me], small_move, d, "fsdp", other(me, d))
 
     def small_arrival(d):
         there = small_come.at[other(me, d)]
@@ -1138,10 +1122,7 @@
     def small_hop(src, dst, slot, peer):
         return link(src, dst, small_line_sems, slot, "seq", peer)
 
-    for d in range(1, 8):
-        small_moving(d).start()
-    small_come[me] = small_ref[me]
-    plan = [(t, d) for t in range(len(moved)) for d in ORDER[1:]]
+    plan = [(t, d) for t in (0, 2) for d in ORDER[1:]]
     begun = []
 
     def feed(count):
@@ -1173,12 +1154,12 @@
             return ins[t].at[pl.ds(r, rows)]
         if d == 0:
             return ins[t].at[me, pl.ds(r, rows)]
-        return come[t - len(still)].at[other(me, d), pl.ds(r, rows)]
+        return come[t].at[other(me, d), pl.ds(r, rows)]
 
     def await_source(k):
         t, d, r, rows = chunks[k]
         if d and r == 0:
-            arrival(t - len(still), d).wait_recv()
+            arrival(t, d).wait_recv()
 
     def box(buf, k, depth):
         t, d, r, rows = chunks[k]
@@ -1225,23 +1206,97 @@
             copy.start()
 
     count = len(chunks)
+    way = scatter_parts(mine, side, near, last, dhin_ref, scatter_sems)
+    pairs = ((dqkv_ref, dqkv), (wqkv_ref, wqkv), (mixed_ref, mixed), (dattn_ref, dattn), (hin_ref, hin))
+    fetches = [pltpu.make_async_copy(src, dst, task_loads.at[i]) for i, (src, dst) in enumerate(pairs)]
+
+    def products(block):
+        return lambda: block_products(me, dqkv, wqkv, mine, True, way, block)
+
+    def fetched(*which):
+        def run():
+            for i in which:
+                fetches[i].wait()
+
+        return run
+
+    def put(j, columns):
+        src = tiles.at[j % 2, :, pl.ds(0, columns)]
+        return pltpu.make_async_copy(src, part_out if j == 0 else part_qkv.at[j - 1], box_sems.at[j % 2])
+
+    def out_tile():
+        for at in range(0, tiles.shape[2], 512):
+            right = dattn[:, :, at : at + 512].reshape(-1, 512)
+            tiles[0, :, at : at + 512] = dots(mixed[...].reshape(-1, mixed.shape[2]), right, 0, 0).astype(bf16)
+        put(0, tiles.shape[2]).start()
+
+    columns = dqkv.shape[2]
+
+    def qkv_tile(j):
+        def run():
+            if j >= 2:
+                put(j - 2, tiles.shape[2] if j == 2 else columns).wait()
+            rows = part_qkv.shape[1]
+            left = hin[:, :, (j - 1) * rows : j * rows].reshape(-1, rows)
+            for at in range(0, columns, 256):
+                right = dqkv[:, :, at : at + 256].reshape(-1, 256)
+                tiles[j % 2, :, at : at + 256] = dots(left, right, 0, 0).astype(bf16)
+            put(j, columns).start()
+
+        return run
+
+    def all_put():
+        put(7, columns).wait()
+        put(8, columns).wait()
+
+    def small_start():
+        small_work[...] = small_ref[...]
+        c = small_work.shape[2]
+        for j in range(8):
+            here = slice(j * c, (j + 1) * c)
+            small_work[j, 0:1] = jnp.sum(normed_ref[:, here] * dhin_ref[:, here], axis=0, keepdims=True)
+        for d in range(1, 8):
+            small_moving(d).start()
+        small_come[me] = small_work[me]
+
+    def small_first():
+        for d in range(1, 8):
+            small_arrival(d).wait_recv()
+        small_sum[...] = jnp.sum(small_come[...], axis=0)
+
+        @pl.when(is_end)
+        def _():
+            small_hop(small_sum, small_in, 0, inward).start()
+
+        @pl.when(jnp.logical_not(is_end))
+        def _():
+            small_hop(small_in, small_in, 0, outward).wait_recv()
+            small_sum[...] = small_sum[...] + small_in[...]
+            small_hop(small_sum, small_back, 1, opposite).start()
+
+    work = {
+        0: [fetched(0, 1), products(6), products(7)],
+        1: [products(4), way["combine"](6), products(5)],
+        2: [products(2), way["combine"](4), products(3)],
+        3: [products(0), way["combine"](2), products(1)],
+        4: [way["combine"](0), fetched(2, 3), out_tile],
+        5: [lambda: way["onward"](0), fetched(4), qkv_tile(1)],
+        6: [lambda: way["onward"](1), qkv_tile(2)],
+        7: [lambda: way["onward"](2), qkv_tile(3)],
+        8: [qkv_tile(4), qkv_tile(5)],
+        9: [qkv_tile(6), qkv_tile(7)],
+        10: [qkv_tile(8), all_put],
+        12: [way["finish"]],
+        13: [small_start],
+        18: [small_first],
+    }
+    for fetch in fetches:
+        fetch.start()
     feed(3)
-    for d in range(1, 8):
-        small_arrival(d).wait_recv()
-    small_sum[...] = jnp.sum(small_come[...], axis=0)
-
-    @pl.when(is_end)
-    def _():
-        small_hop(small_sum, small_in, 0, inward).start()
-
-    @pl.when(jnp.logical_not(is_end))
-    def _():
-        small_hop(small_in, small_in, 0, outward).wait_recv()
-        small_sum[...] = small_sum[...] + small_in[...]
-        small_hop(small_sum, small_back, 1, opposite).start()
-
     for k in range(count):
-        if k % 2 == 1:
+        if k % 4 == 3 and k < 16:
+            feed(1)
+        if k >= 18 and k % 2 == 0:
             feed(1)
         await_source(k)
 
@@ -1265,6 +1320,9 @@
             if k >= 1:
                 finish(k - 1)
 
+        for fn in work.get(k, ()):
+            fn()
+
     @pl.when(jnp.logical_not(is_end))
     def _():
         small_hop(small_back, small_back, 1, opposite).wait_recv()
@@ -1295,43 +1353,61 @@
         small_moving(d).wait_send()
 
 
-def line_sum(small, still, moved, kinds, collective_id):
-    if lax.axis_size("seq") != 4 or lax.axis_size("fsdp") != 8:
-        out = []
-        for x, count in zip(moved, kinds):
-            n, rows, c = x.shape
+def finish(small, normed, gu, dqkv, wqkv, mixed, dattn, hin, collective_id):
+    n, per, _ = gu.shape
+    rows, width = normed.shape
+    cw = mixed.shape[2]
+    if lax.axis_size("seq") != 4 or n != 8:
+        total = n * rows
+        dhin = mm_t(dqkv.reshape(total, 3 * cw), wqkv).astype(bf16)
+        dhin = lax.psum_scatter(dhin, "fsdp", scatter_dimension=0, tiled=True).astype(f32)
+        small = small.at[:, 0].set(jnp.sum(normed * dhin, axis=0).reshape(n, per))
+        out = lax.psum(t_mm(mixed.reshape(total, cw), dattn.reshape(total, width)).astype(bf16), "seq")
+        qkv = t_mm(hin.reshape(total, width), dqkv.reshape(total, 3 * cw)).astype(bf16).reshape(n, per, 3 * cw)
+        moved = []
+        for x, count in ((gu, 2), (qkv, 3)):
+            c = x.shape[2] // count
             x = lax.psum(lax.all_to_all(x, "fsdp", split_axis=0, concat_axis=0, tiled=True), "seq")
-            out.append(x.reshape(n, rows, count, c // count).transpose(2, 1, 0, 3).reshape(count, rows, n * (c // count)))
+            moved.append(x.reshape(n, per, count, c).transpose(2, 1, 0, 3).reshape(count, per, n * c))
         small = lax.psum(lax.psum_scatter(small, "fsdp", scatter_dimension=0), "seq")
-        return small, [lax.psum(x, "seq") for x in still], out
-    still_rows = [x.shape[0] for x in still]
-    moved_rows = [(x.shape[1], 128 if x.shape[2] > 1024 else 256) for x in moved]
-    arrays = [*still, *moved]
-    shapes = [jax.ShapeDtypeStruct(x.shape, bf16) for x in arrays]
-    results = shapes[: len(still)] + [
-        jax.ShapeDtypeStruct((count, x.shape[1], x.shape[0] * (x.shape[2] // count)), bf16) for x, count in zip(moved, kinds)
-    ]
-    count = len(chunks_of(still_rows, moved_rows))
+        return small, dhin, out, *moved
+    qkv = jax.ShapeDtypeStruct((n, per, 3 * cw), bf16)
+    out = jax.ShapeDtypeStruct((cw, width), bf16)
+    gu_shape = jax.ShapeDtypeStruct(gu.shape, bf16)
+    count = len(chunks_of(per, cw, per))
     inside = pl.BlockSpec(memory_space=pltpu.VMEM)
-    rows = max([128] + [size for _, size in moved_rows])
-    width = max(x.shape[-1] for x in arrays)
-    outs = pl.pallas_call(
-        functools.partial(line_kernel, still_rows, moved_rows),
-        in_specs=[inside] + [ANYWHERE] * len(arrays),
-        out_specs=[inside] + [ANYWHERE] * (3 * len(arrays) + len(moved)),
-        out_shape=[jax.ShapeDtypeStruct(small.shape[1:], f32)] + results + shapes * 2 + shapes[len(still) :],
-        scratch_shapes=[pltpu.VMEM(small.shape, f32)]
+    sems = pltpu.SemaphoreType.DMA
+    small_sum, dhin, _, _, sum_gu, sum_out, sum_qkv, *_ = pl.pallas_call(
+        finish_kernel,
+        in_specs=[inside] * 2 + [ANYWHERE] * 6,
+        out_specs=[inside] * 2 + [ANYWHERE] * 13,
+        out_shape=[
+            jax.ShapeDtypeStruct(small.shape[1:], f32),
+            jax.ShapeDtypeStruct((rows, width), f32),
+            out,
+            qkv,
+            jax.ShapeDtypeStruct((2, per, gu.shape[2] // 2 * n), bf16),
+            out,
+            jax.ShapeDtypeStruct((3, per, cw * n), bf16),
+            *[gu_shape, out, qkv] * 2,
+            gu_shape,
+            qkv,
+        ],
+        scratch_shapes=[pltpu.VMEM(x.shape, bf16) for x in (dqkv, wqkv, mixed, dattn, hin)]
+        + [pltpu.VMEM((2, per, width), bf16)]
+        + scatter_boxes(rows, width)
+        + [sems((5,)), sems((2,)), *SCATTER_SEMS]
+        + [pltpu.VMEM(small.shape, f32)] * 2
         + [pltpu.VMEM(small.shape[1:], f32)] * 3
-        + [pltpu.SemaphoreType.DMA((8,)), pltpu.SemaphoreType.DMA((3,)), pltpu.SemaphoreType.DMA((3,)), pltpu.SemaphoreType.DMA((8,))]
-        + [pltpu.VMEM((depth, rows, width), bf16) for depth in (2, 2, SLOTS, 2, SLOTS)]
-        + [pltpu.SemaphoreType.DMA((3,)), pltpu.SemaphoreType.DMA((SLOTS,))]
-        + [pltpu.SemaphoreType.DMA((8,))] * (2 * len(moved))
-        + [pltpu.SemaphoreType.DMA((count,))] * 6,
-        compiler_params=params(collective_id, 40),
-        name="line_sum",
-    )(small, *arrays)
-    small, *outs = outs
-    return small, outs[: len(still)], outs[len(still) : len(arrays)]
+        + [sems((8,)), sems((8,)), sems((3,)), sems((3,))]
+        + [pltpu.VMEM((depth, 128, gu.shape[2]), bf16) for depth in (2, 2, SLOTS, 2, SLOTS)]
+        + [sems((3,)), sems((SLOTS,))]
+        + [sems((8,))] * 4
+        + [sems((count,))] * 6,
+        compiler_params=params(collective_id, 60),
+        name="finish",
+    )(small, normed, gu, dqkv, wqkv, mixed, dattn, hin)
+    return small_sum, dhin, sum_out, sum_gu, sum_qkv
 
 
 def shards(
@@ -1384,45 +1460,45 @@
     h_in, dy = h_in.reshape(total, width), dy.reshape(total, width)
     mixed = mixed.reshape(total, cw)
 
-    attn_sum, _ = product_scatter(mixed.reshape(n, own, cw), w_out, False, [], 3)
+    attn_sum = product_scatter(mixed.reshape(n, own, cw), w_out, 3)
     residual = flat_in + attn_sum
     inv_mid = lax.rsqrt(jnp.mean(residual * residual, axis=1, keepdims=True) + norm_eps)
     normed_mid = residual * inv_mid
     h_mid = (normed_mid * gain_mid).astype(bf16)
-    h_mid, inner, d_gu, d_hmid = mlp(h_mid, wgu, w_down, dy.reshape(n, own, width), 1)
+    h_mid, inner, d_gu, part_down, d_hmid = mlp(h_mid, wgu, w_down, dy.reshape(n, own, width), 1)
     h_mid, inner, d_gu = (x.reshape(total, x.shape[2]) for x in (h_mid, inner, d_gu))
 
     gain_mid_term = jnp.sum(normed_mid * d_hmid, axis=0)
     d_resid = cotangent.reshape(own, width).astype(f32) + norm_back(d_hmid * gain_mid, normed_mid, inv_mid)
-    d_attn, part_down, part_gu = gather_grads(d_resid.astype(bf16), inner, dy, h_mid, d_gu, 2)
-    d_attn = d_attn.reshape(total, width)
+    d_attn, part_gu, part_mlp = gather_products(d_resid.astype(bf16), h_mid, d_gu, inner, w_down, 2)
     part_gu = part_gu.reshape(n, width // n, 2 * fw)
     grad_down = lax.psum(part_down, "seq").astype(f32)
 
-    d_mixed = mm_t(d_attn, w_out).reshape(n, NSEG, rows, cw)
+    d_mixed = mm_t(d_attn.reshape(total, width), w_out).reshape(n, NSEG, rows, cw)
     d_qkv, bias_rows = attention_back(
         qkv, d_mixed, diff, lse, doc_col, doc_row, side, blend_row, memory, norm_vec, heads
     )
-    d_qkv = d_qkv.reshape(total, 3 * cw)
     bias_term = jnp.sum(bias_rows.reshape(heads, HEAD_DIM), axis=1) * blend * (1.0 - blend)
 
-    d_hin, (part_mlp, part_out, part_qkv) = product_scatter(
+    mlp_sum = lax.psum_scatter(part_mlp, "fsdp", scatter_dimension=0, tiled=True)
+    block_out = (residual + mlp_sum.astype(f32)).astype(bf16).reshape(tokens.shape)
+    per = width // n
+    mine = (jnp.arange(n) == lax.axis_index("fsdp"))[:, None, None]
+    bias = jnp.where(mine, jnp.pad(bias_term, (0, per - heads))[None, None], 0.0)
+    terms = jnp.concatenate(
+        [jnp.zeros((n, 1, per), f32), gain_mid_term.reshape(n, 1, per), bias, jnp.zeros((n, 5, per), f32)], axis=1
+    )
+    small, d_hin, sum_out, sum_gu, sum_qkv = finish(
+        terms,
+        normed_in,
+        part_gu,
         d_qkv.reshape(n, own, 3 * cw),
         wqkv,
-        True,
-        [(inner, w_down, False, (1, 4, 5, 6)), (mixed, d_attn, True, ()), (h_in, d_qkv, True, ())],
-        5,
+        mixed.reshape(n, own, cw),
+        d_attn,
+        h_in.reshape(n, own, width),
+        6,
     )
-    mlp_sum = lax.psum_scatter(part_mlp, "fsdp", scatter_dimension=0, tiled=True)
-    block_out = (residual + mlp_sum.astype(f32)).astype(bf16).reshape(tokens.shape)
-    part_qkv = part_qkv.reshape(n, width // n, 3 * cw)
-    gain_in_term = jnp.sum(normed_in * d_hin, axis=0)
-    per = width // n
-    terms = jnp.stack([gain_in_term.reshape(n, per), gain_mid_term.reshape(n, per)], axis=1)
-    mine = (jnp.arange(n) == lax.axis_index("fsdp"))[:, None, None]
-    bias = jnp.where(mine, jnp.pad(bias_term, (0, per - heads))[None, None], 0.0)
-    terms = jnp.concatenate([terms, bias, jnp.zeros((n, 5, per), f32)], axis=1)
-    small, (sum_out,), (sum_gu, sum_qkv) = line_sum(terms, [part_out], [part_gu, part_qkv], [2, 3], 6)
     grad_out = sum_out.astype(f32)
     grad_gate, grad_up = sum_gu[0].astype(f32), sum_gu[1].astype(f32)
     grad_q, grad_k, grad_v = (sum_qkv[i].astype(f32) for i in range(3))

time: 894 us -> 815 us (0.912)
  Pallas kernels: 798 us -> 719 us
    pallas_call x4 -> x3, Pallas kernels: 517 us -> 446 us  [the longest x1 365 us: finish(): pl.pallas_call(finish_kernel, in_specs=[inside] * 2 + [ANYWHERE] * 6, out...]
    pallas_call x1, Pallas kernels: 34.6 us -> 25.6 us  [attention_back(): pl.pallas_call(functools.partial(attention_back_kernel, heads), grid=(NSE...]
    unnamed x52 -> x54, local copies, waits for them, and re-layouts: 18.2 us -> 15.5 us
  transfers between devices with their start and end apart: 3 -> 3, of which waited for: 0 -> 0; matrix products, arithmetic and copies ran while one was open for 5% -> 6% of each run, Pallas kernels for 69% -> 74%
where the time goes in v3:
time: 815 us; the launch traced here: 802 us
  Pallas kernels  719 us (88%)
  other arithmetic  41.3 us (5%)
  local copies, waits for them, and re-layouts  20 us (2%)
  between operations  14.3 us (2%)
    pallas_call x1, Pallas kernels, finish(): pl.pallas_call(finish_kernel, in_specs=[inside] * 2 + [ANYWHERE] * 6, out...  365 us
    pallas_call x1, Pallas kernels, mlp(): pl.pallas_call(mlp_kernel, in_specs=[ANYWHERE] * 4, out_specs=[ANYWHERE]...  100 us
    pallas_call x1, Pallas kernels, front(): pl.pallas_call(functools.partial(front_kernel, count), in_specs=[ANYWHERE...  74.5 us
    pallas_call x1, Pallas kernels, attend(): pl.pallas_call(functools.partial(attend_kernel, heads), in_specs=[ANYWHER...  43.9 us
    pallas_call x1, Pallas kernels, gather_products(): pl.pallas_call(gather_products_kernel, in_specs=[ANYWHERE] * 5, out_specs...  41.6 us
    pallas_call x1, Pallas kernels, product_scatter(): pl.pallas_call(product_scatter_kernel, in_specs=[ANYWHERE] * 2, out_specs...  40.1 us
    pallas_call x1, Pallas kernels, to_columns_in_turns(): pl.pallas_call(functools.partial(move_kernel, count, share), in_specs=[AN...  28.3 us
    pallas_call x1, Pallas kernels, attention_back(): pl.pallas_call(functools.partial(attention_back_kernel, heads), grid=(NSE...  25.6 us
  transfers between devices with their start and end apart: 3, of which 0 were waited for; matrix products, arithmetic and copies ran while one was open for 6% of the time, Pallas kernels for 74%

profile of v3, /device:TPU:0, one launch (start us, length us, event | category | flops | bytes accessed | tf_op | source)
XLA Modules:
  0.0 801.6 jit_solution(4593714576774761804)
XLA Ops:
  7.2 2.2 copy-done.2
  9.4 2.2 copy-done.3
  11.6 28.3 %move.1 = bf16[512,2048]{1,0:T(8,128)(2,1)} custom-call(bf16[256,8192]{1,0:T(8,128)(2,1)S(1)} %copy-done.2, bf16[256,8192]{1,0:T(8,128)(2,1)S(1)} %copy-done.3), custom_call_target="tpu_custom_call" | custom-call | tf_op jit(solution)/shard_map/move/pallas_call | solution.py:448
  40.7 0.9 sub.26.doc_col
  42.3 1.2 copy-done.9
  43.5 1.2 copy-done.10
  44.7 74.5 %front.1 = (bf16[8,256,2048]{2,1,0:T(8,128)(2,1)S(1)}, f32[8,8,256]{2,1,0:T(8,128)S(1)}, bf16[2048,768]{1,0:T(8,128)(2,1)S(1)}) custom-call(bf16[256,2048]{1,0:T(8,128)(2,1)S(1)} %bitcast.65, f32[8,256]{1,0:T(8,128)S(1)} %maximum_maximum_fusion.1.refs_1_, bf16[256,2048]{1,0:T(8,128)(2,1)S(1)} %copy-done.8, bf16[256,2048]{1,0:T(8,128)(2,1)S(1)} %copy-done.9, ...), custom_call_target="tpu_custom_call" | custom-call | tf_op jit(solution)/shard_map/front/pallas_call | solution.py:504
  119.2 1.7 copy-done.6
  120.9 3.4 copy-done.15
  124.6 0.7 compare_convert_fusion.side_ref
  125.5 43.9 %attend.1 = (bf16[8,256,2048]{2,1,0:T(8,128)(2,1)}, bf16[8,2,128,768]{3,2,1,0:T(8,128)(2,1)}, bf16[8,256,2048]{2,1,0:T(8,128)(2,1)}, bf16[8,2,128,256]{3,2,1,0:T...) custom-call(bf16[8,256,2048]{2,1,0:T(8,128)(2,1)} %copy-done.15, ...), custom_call_target="tpu_custom_call" | custom-call | flops 7516192768 | bytes 33554432 | tf_op jit(solution)/shard_map/attend/pallas_call | solution.py:611
  169.5 40.1 %product_scatter.1 = f32[256,2048]{1,0:T(8,128)S(1)} custom-call(bf16[8,256,256]{2,1,0:T(8,128)(2,1)S(1)} %bitcast.67, bf16[256,2048]{1,0:T(8,128)(2,1)S(1)} %copy-done.16), custom_call_target="tpu_custom_call" | custom-call | flops 2147483648 | bytes 8388608 | tf_op jit(solution)/shard_map/product_scatter/pallas_call | solution.py:1047
  209.6 1.8 multiply_reduce_fusion.4
  211.5 1.3 copy-done.18
  212.8 1.2 multiply_convert_fusion.own_ref
  214.0 100.1 %mlp.1 = (bf16[8,256,2048]{2,1,0:T(8,128)(2,1)}, bf16[8,256,1024]{2,1,0:T(8,128)(2,1)}, bf16[8,256,2048]{2,1,0:T(8,128)(2,1)}, bf16[1024,2048]{1,0:T(8,128)(2,1)}, f32[256,2048]{1,0:T(8,128)}) custom-call(bf16[256,2048]{1,0:T(8,128)(2,1)} %multiply_convert_fusion.own_ref, bf16[2048,2048]{1,0:T(8,128)(2,1)} %bitcast.92, bf16[1024,2048]{1,0:T(8,128)(2,1)} %wd_ref.3, ...), custom_call_target="tpu_custom_call" | custom-call | flops 42949672960 | bytes 67108864 | tf_op jit(solution)/shard_map/mlp/pallas_call | solution.py:898
  314.3 2.9 multiply_reduce_fusion.1
  317.7 1.6 fusion.2.x_ref
  319.4 41.6 %gather_products.1 = (bf16[8,256,2048]{2,1,0:T(8,128)(2,1)}, bf16[2048,2048]{1,0:T(8,128)(2,1)}, bf16[2048,2048]{1,0:T(8,128)(2,1)}) custom-call(bf16[256,2048]{1,0:T(8,128)(2,1)} %fusion.2.x_ref, bf16[2048,2048]{1,0:T(8,128)(2,1)} %bitcast.93, bf16[2048,2048]{1,0:T(8,128)(2,1)} %bitcast.94, bf16[2048,1024]{1,0:T(8,128)(2,1)} %bitcast.95, ...), custom_call_target="tpu_custom_call" | custom-call | flops 25769803776 | bytes 50331648 | tf_op jit(solution)/shard_map/gather_products/pallas_call | solution.py:991
  361.1 1.1 copy-done.17
  362.2 7.1 fusion.dmix_ref
  369.3 25.6 %attention_back.1 = (bf16[8,2,128,768]{3,2,1,0:T(8,128)(2,1)}, f32[1,256]{1,0:T(1,128)}) custom-call(bf16[8,2,128,768]{3,2,1,0:T(8,128)(2,1)} %get-tuple-element.48.qkv_ref, f32[8,2,128,256]{3,2,1,0:T(8,128)} %fusion.dmix_ref, f32[8,2,128,256]{3,2,1,0:T(8,128)} %get-tuple-element.50.diff_ref, f32[2,2,1024,1]{3,2,1,0:T(8,128)} %get-tuple-element.51.lse_ref, ...), custom_call_target="tpu_custom_call" | custom-call | flops 2684354560 | bytes 16777216 | tf_op jit(solution)/shard_map/attention_back/pallas_call | solution.py:239
  394.9 0.8 reduce_sum.68
  395.8 0.7 maximum_maximum_fusion.refs_0_
  396.6 364.6 %finish.1 = (f32[8,256]{1,0:T(8,128)}, f32[256,2048]{1,0:T(8,128)}, bf16[256,2048]{1,0:T(8,128)(2,1)}, bf16[8,256,768]{2,1,0:T(8,128)(2,1)}, bf16[2,256,8192]{2,...) custom-call(f32[8,8,256]{2,1,0:T(8,128)} %maximum_maximum_fusion.ref, ...), custom_call_target="tpu_custom_call" | custom-call | tf_op jit(solution)/shard_map/finish/pallas_call | solution.py:1380
  761.1 2.9 convert_element_type.87
  764.6 1.5 slice_bitcast_fusion.1
  766.1 1.3 fusion.4
  767.5 2.9 bitcast_convert_fusion.2
  770.4 11.8 %bitcast_convert_fusion = (f32[256,8192]{1,0:T(8,128)}, f32[256,8192]{1,0:T(8,128)}) fusion(bf16[2,256,8192]{2,1,0:T(8,128)(2,1)} %get-tuple-element.62), kind=kLoop, calls=%fused_computation | loop fusion | flops 4194304 | bytes 25165824 | tf_op jit(solution)/shard_map/convert_element_type | solution.py:1503
  782.2 6.7 convert_element_type.92
  788.9 5.9 multiply_add_fusion
  (79 shorter events, 3.4 us)
Async XLA Ops:
  7.2 206.8 %all-gather.2.cloned.1.call-start = ((), (), s32[]{:S(2)}) async-start(), calls=%async_computation.1 | async-start | bytes 10485760 | tf_op jit(solution)/shard_map/all_gather | solution.py:458
  7.2 2.2 copy-start.2
  9.4 2.2 copy-start.3
  39.9 0.7 copy-start.25
  39.9 2.3 copy-start.23
  39.9 2.3 copy-start.24
  39.9 2.4 copy-start
  39.9 2.3 copy-start.8
  40.0 742.3 %all-reduce.3.cloned.1.call-start = ((), (), s32[]{:S(2)}) async-start(), calls=%async_computation.3 | async-start | bytes 8388608 | tf_op jit(solution)/shard_map/psum | solution.py:1475
  40.6 84.8 %copy-start.12 = (s32[2048]{0:T(1024)}, s32[2048]{0:T(1024)S(1)}, u32[]{:S(2)}) copy-start(s32[2048]{0:T(1024)S(1)} %broadcast_add_fusion) | copy-start | bytes 24580
  41.5 83.9 %copy-start.1 = (s32[2,1024,1]{2,1,0:T(8,128)}, s32[2,1024,1]{2,1,0:T(8,128)S(1)}, u32[]{:S(2)}) copy-start(s32[2,1024,1]{2,1,0:T(8,128)S(1)} %sub.26.doc_col) | copy-start | bytes 24580
  42.3 1.2 copy-start.9
  43.5 1.2 copy-start.10
  44.7 79.9 %copy-start.26 = (f32[2]{0:T(128)S(1)}, f32[2]{0:T(128)}, u32[]{:S(2)}) copy-start(f32[2]{0:T(128)} %param.19) | copy-start | bytes 28
  119.2 1.7 copy-start.6
  120.9 3.4 copy-start.15
  124.3 1.2 copy-start.4
  125.4 44.1 %copy-start.5 = (f32[2,1024,1]{2,1,0:T(8,128)}, f32[2,1024,1]{2,1,0:T(8,128)S(1)}, u32[]{:S(2)}) copy-start(f32[2,1024,1]{2,1,0:T(8,128)S(1)} %compare_convert_fusion.side_ref) | copy-start | bytes 24580
  125.4 44.0 %copy-start.13 = (f32[2,128]{1,0:T(2,128)}, f32[2,128]{1,0:T(2,128)S(1)}, u32[]{:S(2)}) copy-start(f32[2,128]{1,0:T(2,128)S(1)} %broadcast_in_dim.39) | copy-start | bytes 3076
  125.5 43.9 %copy-start.16 = (bf16[256,2048]{1,0:T(8,128)(2,1)S(1)}, bf16[256,2048]{1,0:T(8,128)(2,1)}, u32[]{:S(2)}) copy-start(bf16[256,2048]{1,0:T(8,128)(2,1)} %rhs_ref.1) | copy-start | bytes 3145732
  169.4 40.1 %copy-start.7 = (bf16[8,2,128,256]{3,2,1,0:T(8,128)(2,1)}, bf16[8,2,128,256]{3,2,1,0:T(8,128)(2,1)S(1)}, u32[]{:S(2)}) copy-start(bf16[8,2,128,256]{3,2,1,0:T(8,128)(2,1)S(1)} %get-tuple-element.41) | copy-start | bytes 3145732
  169.5 40.1 %copy-start.11 = (f32[2,128,128]{2,1,0:T(8,128)}, f32[2,128,128]{2,1,0:T(8,128)S(1)}, u32[]{:S(2)}) copy-start(f32[2,128,128]{2,1,0:T(8,128)S(1)} %get-tuple-element.52.mem_ref) | copy-start | bytes 393220
  169.5 40.1 %copy-start.14 = (f32[2,1,128]{2,1,0:T(1,128)}, f32[2,1,128]{2,1,0:T(1,128)S(1)}, u32[]{:S(2)}) copy-start(f32[2,1,128]{2,1,0:T(1,128)S(1)} %get-tuple-element.53.nv_ref) | copy-start | bytes 3076
  211.5 1.3 copy-start.18
  314.2 474.7 %reduce-scatter.2.cloned.1.call-start = ((), (), s32[]{:S(2)}) async-start(), calls=%async_computation.2 | async-start | bytes 9437184 | tf_op jit(solution)/shard_map/reduce_scatter | solution.py:1483
  314.2 3.0 copy-start.19
  314.3 3.5 copy-start.20
  361.0 1.2 copy-start.17
  761.1 3.0 copy-start.21
  764.1 3.4 copy-start.22
Sparse Core Ops, SparseCore 0:
  40.1 149.9 all-gather.1
  314.3 217.1 all-reduce.2
  535.3 96.3 reduce-scatter.1

commit v4 on v3

--- a/solution.py
+++ b/solution.py
@@ -49,212 +49,256 @@
     return jnp.where(u > 0, 1.0, jnp.exp(jnp.minimum(u, 0.0)))
 
 
-def attention_head(h, heads, segment, qkv_ref, doc_col, doc_row, side_ref, blend_ref, mixed_ref, diff_ref, lse_ref, mem_ref, nv_ref):
+def when(condition):
+    if isinstance(condition, bool):
+        return (lambda run: run()) if condition else (lambda run: None)
+    return pl.when(condition)
+
+
+def docs_at(starts_ref, places):
+    total = -1
+    for k in range(starts_ref.shape[0]):
+        total = total + (starts_ref[k] <= places).astype(jnp.int32)
+    return total
+
+
+def cross_doc(starts_ref, length):
+    total = -1
+    for k in range(starts_ref.shape[0]):
+        total = total + jnp.where(starts_ref[k] <= length, 1, 0)
+    return total
+
+
+def in_cross(starts_ref, length, segment, first, count):
+    places = lax.broadcasted_iota(jnp.int32, (count, 1), 0) + (segment * length + first)
+    return (docs_at(starts_ref, places) == cross_doc(starts_ref, length)).astype(f32)
+
+
+def may_see(starts_ref, length, segment, first, block, span):
+    rows = lax.broadcasted_iota(jnp.int32, (block, 1), 0) + first
+    cols = lax.broadcasted_iota(jnp.int32, (1, span), 1)
+    own = docs_at(starts_ref, rows + segment * length)
+    return (cols <= rows) & (docs_at(starts_ref, cols + segment * length) == own)
+
+
+def head_columns(kind, h, heads):
+    at = kind * heads * HEAD_DIM + h * HEAD_DIM
+    return slice(at, at + HEAD_DIM) if isinstance(at, int) else pl.ds(pl.multiple_of(at, HEAD_DIM), HEAD_DIM)
+
+
+def attention_head(h, heads, segment, starts_ref, blend_ref, qkv_ref, mixed_ref, diff_ref, lse_ref, mem_ref, nv_ref):
     n, _, rows, _ = qkv_ref.shape
-    cw = heads * HEAD_DIM
+    length = n * rows
     take = max(1, 256 // rows)
     block = take * rows
     scale = HEAD_DIM ** (-0.5)
-
-    def part(kind, h, lo, hi):
-        cols = slice(kind * cw + h * HEAD_DIM, kind * cw + (h + 1) * HEAD_DIM)
-        return qkv_ref[lo:hi, 0, :, cols].reshape((hi - lo) * rows, HEAD_DIM)
-
-    cols = slice(h * HEAD_DIM, (h + 1) * HEAD_DIM)
-
-    @pl.when(segment == 0)
+    cols = head_columns(0, h, heads)
+
+    def part(kind, lo, hi):
+        return qkv_ref[lo:hi, 0, :, head_columns(kind, h, heads)].reshape((hi - lo) * rows, HEAD_DIM)
+
+    @when(segment == 0)
     def _():
-        fk = phi(part(1, h, 0, n).astype(f32)) * side_ref[0]
-        mem_ref[h] = dots(fk, part(2, h, 0, n).astype(f32), 0, 0, highest)
+        fk = phi(part(1, 0, n).astype(f32)) * in_cross(starts_ref, length, 0, 0, length)
+        mem_ref[h] = dots(fk, part(2, 0, n).astype(f32), 0, 0, highest)
         nv_ref[h] = jnp.sum(fk, axis=0, keepdims=True)
 
     blend = blend_ref[:, cols]
     for i in range(n // take):
         lo, hi = i * take, (i + 1) * take
         span = (i + 1) * block
-        q = part(0, h, lo, hi)
-        s = dots(q, part(1, h, 0, hi), 1, 1) * scale
-        at = lax.broadcasted_iota(jnp.int32, (block, span), 0) + i * block
-        allowed = (lax.broadcasted_iota(jnp.int32, (block, span), 1) <= at) & (
-            doc_row[0, :, :span] == doc_col[0, i * block : (i + 1) * block]
-        )
-        s = jnp.where(allowed, s, -1000000000.0)
+        q = part(0, lo, hi)
+        s = dots(q, part(1, 0, hi), 1, 1) * scale
+        s = jnp.where(may_see(starts_ref, length, segment, i * block, block, span), s, -1000000000.0)
         top = jnp.max(s, axis=1, keepdims=True)
         p = jnp.exp(s - top)
         tot = jnp.sum(p, axis=1, keepdims=True)
         lse_ref[h, 0, i * block : (i + 1) * block] = top + jnp.log(tot)
-        direct = dots((p / tot).astype(bf16), part(2, h, 0, hi), 1, 0)
+        direct = dots((p / tot).astype(bf16), part(2, 0, hi), 1, 0)
         shape = (take, rows, HEAD_DIM)
 
-        @pl.when(segment == 0)
+        @when(segment == 0)
         def _():
             mixed_ref[lo:hi, 0, :, cols] = ((1.0 - blend) * direct).astype(bf16).reshape(shape)
             diff_ref[lo:hi, 0, :, cols] = (-direct).reshape(shape)
 
-        @pl.when(segment != 0)
+        @when(segment != 0)
         def _():
             fq = phi(q.astype(f32))
             numer = dots(fq, mem_ref[h], 1, 0, highest)
             den = jnp.sum(fq * nv_ref[h], axis=1, keepdims=True) + 1.0
-            ret = side_ref[0, i * block : (i + 1) * block] * numer / den
+            ret = in_cross(starts_ref, length, 1, i * block, block) * numer / den
             mixed_ref[lo:hi, 0, :, cols] = (blend * ret + (1.0 - blend) * direct).astype(bf16).reshape(shape)
             diff_ref[lo:hi, 0, :, cols] = (ret - direct).reshape(shape)
 
 
-def attention_kernel(heads, *refs):
+def attention_kernel(heads, starts_ref, blend_ref, *refs):
     for h in range(heads):
-        attention_head(h, heads, pl.program_id(0), *refs)
-
-
-def attention_back_kernel(
-    heads, qkv_ref, dmix_ref, diff_ref, lse_ref, doc_col, doc_row, side_ref, blend_ref, mem_ref, nv_ref,
-    out_ref, bias_ref, dk_acc, dv_acc, dmem, dnv,
-):
+        attention_head(h, heads, pl.program_id(0), starts_ref, blend_ref, *refs)
+
+
+def back_block(i, h, heads, segment, starts_ref, blend_ref, qkv_ref, dmix_ref, diff_ref, lse_ref, mem_ref, nv_ref, out_ref, bias_ref, dk_acc, dv_acc, dmem, dnv):
     n, _, rows, _ = qkv_ref.shape
     length = n * rows
-    cw = heads * HEAD_DIM
     take = max(1, 256 // rows)
     block = take * rows
     scale = HEAD_DIM ** (-0.5)
-    step = pl.program_id(0)
     shape = (take, rows, HEAD_DIM)
-
-    def part(kind, h, lo, hi):
-        cols = slice(kind * cw + h * HEAD_DIM, kind * cw + (h + 1) * HEAD_DIM)
-        return qkv_ref[lo:hi, 0, :, cols].reshape((hi - lo) * rows, HEAD_DIM)
-
-    @pl.when(step == 0)
+    cols = head_columns(0, h, heads)
+    blend = blend_ref[:, cols]
+    lo, hi = i * take, (i + 1) * take
+    span = (i + 1) * block
+    here = slice(i * block, (i + 1) * block)
+
+    def part(kind, lo, hi):
+        return qkv_ref[lo:hi, 0, :, head_columns(kind, h, heads)].reshape((hi - lo) * rows, HEAD_DIM)
+
+    if i == 0:
+        dk_acc[h] = jnp.zeros(dk_acc.shape[1:], f32)
+        dv_acc[h] = jnp.zeros(dv_acc.shape[1:], f32)
+    q, k, v = part(0, lo, hi), part(1, 0, hi), part(2, 0, hi)
+    dmix = dmix_ref[lo:hi, 0, :, cols].reshape(block, HEAD_DIM)
+    bias_ref[:, cols] += jnp.sum(dmix * diff_ref[lo:hi, 0, :, cols].reshape(block, HEAD_DIM), axis=0, keepdims=True)
+    ddir = ((1.0 - blend) * dmix).astype(bf16)
+    s = dots(q, k, 1, 1) * scale
+    allowed = may_see(starts_ref, length, segment, i * block, block, span)
+    e = jnp.exp(jnp.where(allowed, s, -1000000000.0) - lse_ref[h, 0, here])
+    dp = dots(ddir, v, 1, 1)
+    bal = jnp.sum(e * dp, axis=1, keepdims=True)
+    ds = (e * (dp - bal)).astype(bf16)
+    dv_acc[h, :span] += dots(e.astype(bf16), ddir, 0, 0)
+    dk_acc[h, :span] += dots(ds, q, 0, 0) * scale
+    dq = dots(ds, k, 1, 0) * scale
+
+    @when(segment == 0)
+    def _():
+        out_ref[lo:hi, 0, :, cols] = dq.astype(bf16).reshape(shape)
+
+    @when(segment != 0)
+    def _():
+        q32 = q.astype(f32)
+        fq = phi(q32)
+        numer = dots(fq, mem_ref[h], 1, 0, highest)
+        den = jnp.sum(fq * nv_ref[h], axis=1, keepdims=True) + 1.0
+        dnum = in_cross(starts_ref, length, 1, i * block, block) * (blend * dmix) / den
+        dden = -jnp.sum(dnum * numer, axis=1, keepdims=True) / den
+        dmem[h] += dots(fq, dnum, 0, 0, highest)
+        dnv[h] += jnp.sum(dden * fq, axis=0, keepdims=True)
+        dfq = dots(dnum, mem_ref[h], 1, 1, highest) + dden * nv_ref[h]
+        out_ref[lo:hi, 0, :, cols] = (dq + dfq * phi_slope(q32)).astype(bf16).reshape(shape)
+
+
+def back_end(h, heads, segment, starts_ref, qkv_ref, out_ref, dk_acc, dv_acc, dmem, dnv):
+    n, _, rows, _ = qkv_ref.shape
+    length = n * rows
+    whole = (n, rows, HEAD_DIM)
+    kcols, vcols = head_columns(1, h, heads), head_columns(2, h, heads)
+
+    @when(segment != 0)
+    def _():
+        out_ref[:, 0, :, kcols] = dk_acc[h].astype(bf16).reshape(whole)
+        out_ref[:, 0, :, vcols] = dv_acc[h].astype(bf16).reshape(whole)
+
+    @when(segment == 0)
+    def _():
+        k32 = qkv_ref[:, 0, :, kcols].reshape(length, HEAD_DIM).astype(f32)
+        v32 = qkv_ref[:, 0, :, vcols].reshape(length, HEAD_DIM).astype(f32)
+        key_set = in_cross(starts_ref, length, 0, 0, length)
+        mem_v = key_set * dots(phi(k32), dmem[h], 1, 0, highest)
+        mem_k = key_set * (dots(v32, dmem[h], 1, 1, highest) + dnv[h]) * phi_slope(k32)
+        out_ref[:, 0, :, kcols] = (dk_acc[h] + mem_k).astype(bf16).reshape(whole)
+        out_ref[:, 0, :, vcols] = (dv_acc[h] + mem_v).astype(bf16).reshape(whole)
+
+
+def attention_back_kernel(heads, starts_ref, blend_ref, qkv_ref, dmix_ref, diff_ref, lse_ref, mem_ref, nv_ref, out_ref, bias_ref, dk_acc, dv_acc, dmem, dnv):
+    n, _, rows, _ = qkv_ref.shape
+
+    @pl.when(pl.program_id(0) == 0)
     def _():
         bias_ref[...] = jnp.zeros_like(bias_ref)
         dmem[...] = jnp.zeros_like(dmem)
         dnv[...] = jnp.zeros_like(dnv)
 
+    segment = NSEG - 1 - pl.program_id(0)
     for h in range(heads):
-        cols = slice(h * HEAD_DIM, (h + 1) * HEAD_DIM)
-        blend = blend_ref[:, cols]
-        dk_acc[...] = jnp.zeros_like(dk_acc)
-        dv_acc[...] = jnp.zeros_like(dv_acc)
-        for i in range(n // take):
-            lo, hi = i * take, (i + 1) * take
-            span = (i + 1) * block
-            here = slice(i * block, (i + 1) * block)
-            q, k, v = part(0, h, lo, hi), part(1, h, 0, hi), part(2, h, 0, hi)
-            dmix = dmix_ref[lo:hi, 0, :, cols].reshape(block, HEAD_DIM)
-            bias_ref[:, cols] += jnp.sum(dmix * diff_ref[lo:hi, 0, :, cols].reshape(block, HEAD_DIM), axis=0, keepdims=True)
-            ddir = ((1.0 - blend) * dmix).astype(bf16)
-            s = dots(q, k, 1, 1) * scale
-            at = lax.broadcasted_iota(jnp.int32, (block, span), 0) + i * block
-            allowed = (lax.broadcasted_iota(jnp.int32, (block, span), 1) <= at) & (
-                doc_row[0, :, :span] == doc_col[0, here]
+        for i in range(n * rows // (max(1, 256 // rows) * rows)):
+            back_block(
+                i, h, heads, segment, starts_ref, blend_ref, qkv_ref, dmix_ref, diff_ref, lse_ref, mem_ref, nv_ref,
+                out_ref, bias_ref, dk_acc, dv_acc, dmem, dnv,
             )
-            e = jnp.exp(jnp.where(allowed, s, -1000000000.0) - lse_ref[h, 0, here])
-            dp = dots(ddir, v, 1, 1)
-            bal = jnp.sum(e * dp, axis=1, keepdims=True)
-            ds = (e * (dp - bal)).astype(bf16)
-            dv_acc[:span] += dots(e.astype(bf16), ddir, 0, 0)
-            dk_acc[:span] += dots(ds, q, 0, 0) * scale
-            dq = dots(ds, k, 1, 0) * scale
-
-            @pl.when(step != 0)
-            def _():
-                out_ref[lo:hi, 0, :, cols] = dq.astype(bf16).reshape(shape)
-
-            @pl.when(step == 0)
-            def _():
-                q32 = q.astype(f32)
-                fq = phi(q32)
-                numer = dots(fq, mem_ref[h], 1, 0, highest)
-                den = jnp.sum(fq * nv_ref[h], axis=1, keepdims=True) + 1.0
-                dnum = side_ref[0, here] * (blend * dmix) / den
-                dden = -jnp.sum(dnum * numer, axis=1, keepdims=True) / den
-                dmem[h] += dots(fq, dnum, 0, 0, highest)
-                dnv[h] += jnp.sum(dden * fq, axis=0, keepdims=True)
-                dfq = dots(dnum, mem_ref[h], 1, 1, highest) + dden * nv_ref[h]
-                out_ref[lo:hi, 0, :, cols] = (dq + dfq * phi_slope(q32)).astype(bf16).reshape(shape)
-
-        whole = (n, rows, HEAD_DIM)
-        kcols = slice(cw + h * HEAD_DIM, cw + (h + 1) * HEAD_DIM)
-        vcols = slice(2 * cw + h * HEAD_DIM, 2 * cw + (h + 1) * HEAD_DIM)
-
-        @pl.when(step == 0)
-        def _():
-            out_ref[:, 0, :, kcols] = dk_acc[...].astype(bf16).reshape(whole)
-            out_ref[:, 0, :, vcols] = dv_acc[...].astype(bf16).reshape(whole)
-
-        @pl.when(step != 0)
-        def _():
-            k32 = part(1, h, 0, n).astype(f32)
-            v32 = part(2, h, 0, n).astype(f32)
-            key_set = side_ref[0]
-            mem_v = key_set * dots(phi(k32), dmem[h], 1, 0, highest)
-            mem_k = key_set * (dots(v32, dmem[h], 1, 1, highest) + dnv[h]) * phi_slope(k32)
-            out_ref[:, 0, :, kcols] = (dk_acc[...] + mem_k).astype(bf16).reshape(whole)
-            out_ref[:, 0, :, vcols] = (dv_acc[...] + mem_v).astype(bf16).reshape(whole)
+        back_end(h, heads, segment, starts_ref, qkv_ref, out_ref, dk_acc, dv_acc, dmem, dnv)
 
 
 def attention_specs(n, rows, heads, pick):
     length = n * rows
     cw = heads * HEAD_DIM
+    starts = pl.BlockSpec(memory_space=pltpu.SMEM)
     wide = pl.BlockSpec((n, 1, rows, 3 * cw), lambda g: (0, pick(g), 0, 0))
     narrow = pl.BlockSpec((n, 1, rows, cw), lambda g: (0, pick(g), 0, 0))
     lse = pl.BlockSpec((heads, 1, length, 1), lambda g: (0, pick(g), 0, 0))
-    col = pl.BlockSpec((1, length, 1), lambda g: (pick(g), 0, 0))
-    row = pl.BlockSpec((1, 1, length), lambda g: (pick(g), 0, 0))
     line = pl.BlockSpec((1, cw), lambda g: (0, 0))
     mem = pl.BlockSpec((heads, HEAD_DIM, HEAD_DIM), lambda g: (0, 0, 0))
     nv = pl.BlockSpec((heads, 1, HEAD_DIM), lambda g: (0, 0, 0))
-    return wide, narrow, lse, col, row, line, mem, nv
-
-
-def attention(qkv, doc_col, doc_row, side, blend, heads):
+    return starts, wide, narrow, lse, line, mem, nv
+
+
+def attention(starts_row, blend_row, qkv, heads):
     n, _, rows, _ = qkv.shape
     length = n * rows
     cw = heads * HEAD_DIM
-    wide, narrow, lse, col, row, line, mem, nv = attention_specs(n, rows, heads, lambda g: g)
+    starts, wide, narrow, lse, line, mem, nv = attention_specs(n, rows, heads, lambda g: g)
     pairs = heads * NSEG * length * length // 2
     return pl.pallas_call(
         functools.partial(attention_kernel, heads),
         grid=(NSEG,),
-        in_specs=[wide, col, row, col, line],
+        in_specs=[starts, line, wide],
         out_specs=[narrow, narrow, lse, mem, nv],
-        out_shape=[
-            jax.ShapeDtypeStruct((n, NSEG, rows, cw), bf16),
-            jax.ShapeDtypeStruct((n, NSEG, rows, cw), f32),
-            jax.ShapeDtypeStruct((heads, NSEG, length, 1), f32),
-            jax.ShapeDtypeStruct((heads, HEAD_DIM, HEAD_DIM), f32),
-            jax.ShapeDtypeStruct((heads, 1, HEAD_DIM), f32),
-        ],
+        out_shape=attention_shapes(n, rows, heads),
         compiler_params=pltpu.CompilerParams(vmem_limit_bytes=48 << 20),
         cost_estimate=pl.CostEstimate(flops=pairs * 4 * HEAD_DIM, transcendentals=pairs, bytes_accessed=8 << 20),
         name="attention",
-    )(qkv, doc_col, doc_row, side, blend)
-
-
-def attention_back(qkv, dmix, diff, lse_rows, doc_col, doc_row, side, blend, mem_all, nv_all, heads):
+    )(starts_row, blend_row, qkv)
+
+
+def attention_shapes(n, rows, heads):
+    return [
+        jax.ShapeDtypeStruct((n, NSEG, rows, heads * HEAD_DIM), bf16),
+        jax.ShapeDtypeStruct((n, NSEG, rows, heads * HEAD_DIM), f32),
+        jax.ShapeDtypeStruct((heads, NSEG, n * rows, 1), f32),
+        jax.ShapeDtypeStruct((heads, HEAD_DIM, HEAD_DIM), f32),
+        jax.ShapeDtypeStruct((heads, 1, HEAD_DIM), f32),
+    ]
+
+
+def back_boxes(n, rows, heads):
+    return [
+        pltpu.VMEM((heads, n * rows, HEAD_DIM), f32),
+        pltpu.VMEM((heads, n * rows, HEAD_DIM), f32),
+        pltpu.VMEM((heads, HEAD_DIM, HEAD_DIM), f32),
+        pltpu.VMEM((heads, 1, HEAD_DIM), f32),
+    ]
+
+
+def attention_back(starts_row, blend_row, qkv, dmix, diff, lse_rows, mem_all, nv_all, heads):
     n, _, rows, _ = qkv.shape
     length = n * rows
     cw = heads * HEAD_DIM
-    wide, narrow, lse, col, row, line, mem, nv = attention_specs(n, rows, heads, lambda g: NSEG - 1 - g)
+    starts, wide, narrow, lse, line, mem, nv = attention_specs(n, rows, heads, lambda g: NSEG - 1 - g)
     pairs = heads * NSEG * length * length // 2
     return pl.pallas_call(
         functools.partial(attention_back_kernel, heads),
         grid=(NSEG,),
-        in_specs=[wide, narrow, narrow, lse, col, row, col, line, mem, nv],
+        in_specs=[starts, line, wide, narrow, narrow, lse, mem, nv],
         out_specs=[wide, line],
         out_shape=[
             jax.ShapeDtypeStruct((n, NSEG, rows, 3 * cw), bf16),
             jax.ShapeDtypeStruct((1, cw), f32),
         ],
-        scratch_shapes=[
-            pltpu.VMEM((length, HEAD_DIM), f32),
-            pltpu.VMEM((length, HEAD_DIM), f32),
-            pltpu.VMEM((heads, HEAD_DIM, HEAD_DIM), f32),
-            pltpu.VMEM((heads, 1, HEAD_DIM), f32),
-        ],
+        scratch_shapes=back_boxes(n, rows, heads),
         compiler_params=pltpu.CompilerParams(vmem_limit_bytes=56 << 20),
         cost_estimate=pl.CostEstimate(flops=pairs * 10 * HEAD_DIM, transcendentals=pairs, bytes_accessed=16 << 20),
         name="attention_back",
-    )(qkv, dmix, diff, lse_rows, doc_col, doc_row, side, blend, mem_all, nv_all)
+    )(starts_row, blend_row, qkv, dmix, diff, lse_rows, mem_all, nv_all)
 
 
 def flip(index, bit):
@@ -517,7 +561,7 @@
     return x, gains[:, :kinds].transpose(1, 0, 2).reshape(kinds, n * c), w
 
 
-def attend_kernel(heads, all_ref, gain_ref, w_ref, dy_ref, doc_col, doc_row, side_ref, blend_ref, *refs):
+def attend_kernel(heads, all_ref, gain_ref, w_ref, dy_ref, starts_ref, blend_ref, *refs):
     h_out, qkv_out, dy_out, mixed_ref, diff_ref, lse_ref, mem_ref, nv_ref, x, w, hid, qkv, load_sems, x_sems, h_sems, q_sems, *sems = refs
     n, tokens, width = all_ref.shape
     rows = tokens // NSEG
@@ -568,32 +612,31 @@
     store(n - 1).wait()
     keep = pltpu.make_async_copy(qkv, qkv_out, q_sems.at[0])
     keep.start()
-    hooks = {(0, 0): near2, (0, heads - 1): near3, (1, 0): far0, (1, heads - 1): far1} if heads > 1 else {}
-
-    def segment(i, _):
-        here = pl.ds(i, 1)
-        for h in range(heads):
-            for (seg, at), fn in hooks.items():
-                if at == h:
-
-                    @pl.when(i == seg)
-                    def _():
-                        fn()
-
-            attention_head(
-                h, heads, i, qkv.at[:, here], doc_col.at[here], doc_row.at[here], side_ref.at[here], blend_ref,
-                mixed_ref.at[:, here], diff_ref.at[:, here], lse_ref.at[:, here], mem_ref, nv_ref,
-            )
+    hooks = {0: near2, heads - 1: near3, heads: far0, 2 * heads - 1: far1}
+
+    def turn(i, _):
+        segment, h = lax.div(i, heads), lax.rem(i, heads)
+        here = pl.ds(segment, 1)
+        for at, fn in hooks.items():
+
+            @pl.when(i == at)
+            def _():
+                fn()
+
+        attention_head(
+            h, heads, segment, starts_ref, blend_ref, qkv.at[:, here], mixed_ref.at[:, here], diff_ref.at[:, here],
+            lse_ref.at[:, here], mem_ref, nv_ref,
+        )
         return 0
 
-    lax.fori_loop(0, NSEG, segment, 0)
+    lax.fori_loop(0, NSEG * heads, turn, 0)
     for d in (1, 3, 5, 7):
         wait_from(d)
     end()
     keep.wait()
 
 
-def attend(x_all, gain, wqkv, dy, doc_col, doc_row, side, blend, heads, collective_id):
+def attend(x_all, gain, wqkv, dy, starts, blend, heads, collective_id):
     n, tokens, width = x_all.shape
     rows = tokens // NSEG
     cw = heads * HEAD_DIM
@@ -603,24 +646,20 @@
         h_in = (here * inverse * gain).astype(bf16)
         qkv = mm(h_in, wqkv).astype(bf16).reshape(n, NSEG, rows, 3 * cw)
         dy = lax.all_gather(dy, "fsdp", axis=0)
-        return h_in.reshape(x_all.shape), qkv, dy, *attention(qkv, doc_col, doc_row, side, blend, heads)
+        return h_in.reshape(x_all.shape), qkv, dy, *attention(starts, blend, qkv, heads)
     length = n * rows
     sems = pltpu.SemaphoreType.DMA
     inside = pl.BlockSpec(memory_space=pltpu.VMEM)
     pairs = heads * NSEG * length * length // 2
     return pl.pallas_call(
         functools.partial(attend_kernel, heads),
-        in_specs=[ANYWHERE, inside, ANYWHERE, ANYWHERE] + [inside] * 4,
+        in_specs=[ANYWHERE, inside, ANYWHERE, ANYWHERE, pl.BlockSpec(memory_space=pltpu.SMEM), inside],
         out_specs=[ANYWHERE] * 3 + [inside] * 5,
         out_shape=[
             jax.ShapeDtypeStruct(x_all.shape, bf16),
             jax.ShapeDtypeStruct((n, NSEG, rows, 3 * cw), bf16),
             jax.ShapeDtypeStruct((n, *dy.shape), bf16),
-            jax.ShapeDtypeStruct((n, NSEG, rows, cw), bf16),
-            jax.ShapeDtypeStruct((n, NSEG, rows, cw), f32),
-            jax.ShapeDtypeStruct((heads, NSEG, length, 1), f32),
-            jax.ShapeDtypeStruct((heads, HEAD_DIM, HEAD_DIM), f32),
-            jax.ShapeDtypeStruct((heads, 1, HEAD_DIM), f32),
+            *attention_shapes(n, rows, heads),
         ],
         scratch_shapes=[
             pltpu.VMEM((2, tokens, width), bf16),
@@ -635,7 +674,7 @@
             flops=pairs * 4 * HEAD_DIM + 6 * n * tokens * width * cw, transcendentals=pairs, bytes_accessed=32 << 20
         ),
         name="attend",
-    )(x_all, gain, wqkv, dy, doc_col, doc_row, side, blend)
+    )(x_all, gain, wqkv, dy, starts, blend)
 
 
 def quotient(a, b):
@@ -960,56 +999,171 @@
         store(i).wait()
 
 
-def gather_products_kernel(x_ref, h_ref, dgu_ref, inner_ref, wd_ref, out_ref, gu_ref, mlp_ref, h, dgu, inner, wd, box, load_sems, sems, *refs):
+def line_places():
+    place = lax.axis_index("seq")
+    inward = jnp.where(place < 2, 1, 2)
+    return (place == 0) | (place == 3), inward, jnp.where(place < 2, 0, 3), 3 - inward
+
+
+def greet_line(bits):
+    me = lax.axis_index("fsdp")
+    is_end, inward, outward, opposite = line_places()
+    barrier = pltpu.get_barrier_semaphore()
+    for d in bits:
+        pl.semaphore_signal(barrier, inc=1, device_id={"fsdp": other(me, d)}, device_id_type=pl.DeviceIdType.MESH)
+
+    @pl.when(is_end)
+    def _():
+        pl.semaphore_signal(barrier, inc=1, device_id={"seq": inward}, device_id_type=pl.DeviceIdType.MESH)
+        pl.semaphore_wait(barrier, len(bits) + 1)
+
+    @pl.when(jnp.logical_not(is_end))
+    def _():
+        for peer in (outward, opposite):
+            pl.semaphore_signal(barrier, inc=1, device_id={"seq": peer}, device_id_type=pl.DeviceIdType.MESH)
+        pl.semaphore_wait(barrier, len(bits) + 2)
+
+
+HEAD_STEPS = 12
+
+
+def head_rows(rows):
+    return rows * 3 // 8
+
+
+def head_line(own, came, half, crossed, total, sems):
+    is_end, inward, outward, opposite = line_places()
+    rows = own.shape[0] // HEAD_STEPS
+    go_in, cross, back = sems[0:2], sems[2:4], sems[4:6]
+
+    def at(ref, c):
+        return ref.at[pl.ds(c * rows, rows)]
+
+    def add(dst, left, right):
+        def body(i, _):
+            here = pl.ds(pl.multiple_of(i * 16, 16), 16)
+            dst[here] = (left[here].astype(f32) + right[here].astype(f32)).astype(bf16)
+            return 0
+
+        lax.fori_loop(0, rows // 16, body, 0)
+
+    def first(c):
+        return link(at(own, c), at(came, c), go_in, c, "seq", inward)
+
+    def second(c):
+        return link(at(half, c), at(crossed, c), cross, c, "seq", opposite)
+
+    def third(c):
+        return link(at(total, c), at(total, c), back, c, "seq", outward)
+
+    def begin():
+        @pl.when(is_end)
+        def _():
+            for c in range(HEAD_STEPS):
+                first(c).start()
+
+    def step(j):
+        def run():
+            @pl.when(jnp.logical_not(is_end))
+            def _():
+                if j < HEAD_STEPS:
+                    link(at(came, j), at(came, j), go_in, j, "seq", outward).wait_recv()
+                    add(at(half, j), at(own, j), at(came, j))
+                    second(j).start()
+                if j >= 2:
+                    c = j - 2
+                    link(at(crossed, c), at(crossed, c), cross, c, "seq", opposite).wait_recv()
+                    add(at(total, c), at(half, c), at(crossed, c))
+                    third(c).start()
+
+        return run
+
+    def end():
+        @pl.when(is_end)
+        def _():
+            for c in range(HEAD_STEPS):
+                link(at(total, c), at(total, c), back, c, "seq", inward).wait_recv()
+                first(c).wait_send()
+
+        @pl.when(jnp.logical_not(is_end))
+        def _():
+            for c in range(HEAD_STEPS):
+                second(c).wait_send()
+                third(c).wait_send()
+
+    return begin, [step(j) for j in range(HEAD_STEPS + 2)], end
+
+
+def gather_products_kernel(x_ref, h_ref, dgu_ref, inner_ref, wd_ref, down_ref, out_ref, gu_ref, mlp_ref, head_ref, h, dgu, inner, wd, box, *refs):
+    (own, came, half, crossed, total), refs = refs[:5], refs[5:]
+    load_sems, sems, line_sems, refs = refs[0], refs[1], refs[2:8], refs[8:]
+    line_begin, steps, line_end = head_line(own, came, half, crossed, total, line_sems)
+    head = pltpu.make_async_copy(down_ref.at[pl.ds(0, own.shape[0])], own, load_sems.at[4])
+    head.start()
     loads = [
         pltpu.make_async_copy(src, dst, load_sems.at[i])
         for i, (src, dst) in enumerate(((h_ref, h), (dgu_ref, dgu), (inner_ref, inner), (wd_ref, wd)))
     ]
-    me = lax.axis_index("fsdp")
-    greet([other(me, d) for d in (1, 2, 4)])
+    greet_line((1, 2, 4))
     begin, near0, near1, near2, near3, far0, far1, wait_from, end = gather_parts(x_ref, out_ref, *refs)
     begin()
+    head.wait()
+    line_begin()
     for load in loads:
         load.start()
     loads[0].wait()
     loads[1].wait()
-    product_tiles(h, dgu, box, gu_ref, sems, True, {1: [near0], 3: [near1], 5: [near2], 7: [near3]})
+    hooks = {i: [steps[i - 1]] for i in range(1, 8)}
+    for i, fn in ((1, near0), (3, near1), (5, near2), (7, near3)):
+        hooks[i].append(fn)
+    product_tiles(h, dgu, box, gu_ref, sems, True, hooks)
     loads[2].wait()
     loads[3].wait()
-    product_tiles(inner, wd, box, mlp_ref, sems, False, {3: [far0], 7: [far1]})
+    hooks = {0: [steps[7]], 2: [steps[8]], 3: [far0], 4: [steps[9]], 6: [steps[10]], 7: [far1]}
+    product_tiles(inner, wd, box, mlp_ref, sems, False, hooks)
+    for step in steps[11:]:
+        step()
     for d in (1, 3, 5, 7):
         wait_from(d)
+    line_end()
+    out = pltpu.make_async_copy(total, head_ref, load_sems.at[4])
+    out.start()
     end()
-
-
-def gather_products(x, h, dgu, inner, w_down, collective_id):
+    out.wait()
+
+
+def gather_products(x, h, dgu, inner, w_down, down, collective_id):
     n = lax.axis_size("fsdp")
-    if n != 8:
-        return lax.all_gather(x, "fsdp", axis=0), t_mm(h, dgu).astype(bf16), mm(inner, w_down).astype(bf16)
+    ahead = head_rows(down.shape[0])
+    if n != 8 or lax.axis_size("seq") != 4:
+        head = lax.psum(down[:ahead], "seq")
+        return lax.all_gather(x, "fsdp", axis=0), t_mm(h, dgu).astype(bf16), mm(inner, w_down).astype(bf16), head
     total, width = h.shape
     sems = pltpu.SemaphoreType.DMA
     return pl.pallas_call(
         gather_products_kernel,
-        in_specs=[ANYWHERE] * 5,
-        out_specs=[ANYWHERE] * 3,
+        in_specs=[ANYWHERE] * 6,
+        out_specs=[ANYWHERE] * 4,
         out_shape=[
             jax.ShapeDtypeStruct((n, *x.shape), bf16),
             jax.ShapeDtypeStruct((width, dgu.shape[1]), bf16),
             jax.ShapeDtypeStruct((total, width), bf16),
+            jax.ShapeDtypeStruct((ahead, width), bf16),
         ],
         scratch_shapes=[pltpu.VMEM(a.shape, bf16) for a in (h, dgu, inner, w_down)]
-        + [pltpu.VMEM((2, 256, max(width, dgu.shape[1])), bf16), sems((4,)), sems((2,)), *GATHER_SEMS],
+        + [pltpu.VMEM((2, 256, max(width, dgu.shape[1])), bf16), *[pltpu.VMEM((ahead, width), bf16)] * 5]
+        + [sems((5,)), sems((2,)), *[sems((HEAD_STEPS,))] * 6, *GATHER_SEMS],
         compiler_params=params(collective_id, 56),
         cost_estimate=pl.CostEstimate(
             flops=2 * total * width * (inner.shape[1] + dgu.shape[1]), transcendentals=0, bytes_accessed=48 << 20
         ),
         name="gather_products",
-    )(x, h, dgu, inner, w_down)
+    )(x, h, dgu, inner, w_down, down)
 
 
 def block_products(me, lhs, rhs, mine, turned, back, block):
     wide = mine.shape[2] // 4
-    left = lhs[xor(me, block)]
+    left = lhs[xor(me, block)].reshape(-1, lhs.shape[-1])
     for t in range(4):
         cols = slice(t * wide, (t + 1) * wide)
         made = dots(left, rhs[cols], 1, 1) if turned else dots(left, rhs[:, cols], 1, 0)
@@ -1056,27 +1210,32 @@
     )(lhs, rhs)
 
 
-SLOTS = 4
-
-
-def chunks_of(gu_rows, out_rows, qkv_rows):
-    out = [(0, d, r, 64) for d in ORDER for r in range(0, gu_rows, 64)]
+SLOTS = 6
+LAG = 3
+
+
+def chunks_of(gu_rows, out_rows, qkv_rows, down_rows):
+    out = [(3, None, r, 64) for r in range(head_rows(down_rows), down_rows, 64)]
+    out += [(0, d, r, 64) for d in ORDER for r in range(0, gu_rows, 64)]
     out += [(1, None, r, 64) for r in range(0, out_rows, 64)]
     return out + [(2, d, r, 128) for d in ORDER for r in range(0, qkv_rows, 128)]
 
 
 def finish_kernel(*refs):
-    small_ref, normed_ref, gu_ref, dqkv_ref, wqkv_ref, mixed_ref, dattn_ref, hin_ref, *refs = refs
-    small_out, dhin_ref, part_out, part_qkv, *refs = refs
-    ins = [gu_ref, part_out, part_qkv]
-    kinds = 3
+    starts_ref, blend_ref, small_ref, x_ref, inv_ref, gain_ref, dres_ref, *refs = refs
+    (gu_ref, wqkv_ref, mixed_ref, dattn_ref, hin_ref, wout_ref, qkv_ref, diff_ref, lse_ref, mem_ref, nv_ref, down_ref), refs = refs[:12], refs[12:]
+    small_out, dx_ref, part_out, part_qkv, *refs = refs
+    ins = [gu_ref, part_out, part_qkv, down_ref]
+    kinds = 4
     outs, refs = refs[:kinds], refs[kinds:]
     first, refs = refs[:kinds], refs[kinds:]
     second, refs = refs[:kinds], refs[kinds:]
     come, refs = {0: refs[0], 2: refs[1]}, refs[2:]
-    (dqkv, wqkv, mixed, dattn, hin, tiles), refs = refs[:6], refs[6:]
-    (mine, side, near, last), refs = refs[:4], refs[4:]
-    (task_loads, box_sems), refs = refs[:2], refs[2:]
+    (wqkv, mixed, wout, qkv, diff, lse, mem, nv, dqkv, dmix, bias, tiles), refs = refs[:12], refs[12:]
+    back_refs, refs = refs[:4], refs[4:]
+    (big, side, near, last), refs = refs[:4], refs[4:]
+    dattn = mine = hin = big
+    (fetch_sems, box_sems), refs = refs[:2], refs[2:]
     scatter_sems, refs = refs[: len(SCATTER_SEMS)], refs[len(SCATTER_SEMS) :]
     small_work, small_come, small_sum, small_in, small_back, *refs = refs
     small_move, small_line_sems, refs = refs[0:2], refs[2:4], refs[4:]
@@ -1084,9 +1243,11 @@
     move = {0: sems[0:2], 2: sems[2:4]}
     sems = sems[4:]
     go_in, cross, back = sems[0:2], sems[2:4], sems[4:6]
+    heads = mem.shape[0]
+    seg_rows = qkv.shape[2]
     me, place = lax.axis_index("fsdp"), lax.axis_index("seq")
     is_end = (place == 0) | (place == 3)
-    chunks = chunks_of(gu_ref.shape[1], part_out.shape[0], part_qkv.shape[1])
+    chunks = chunks_of(gu_ref.shape[1], part_out.shape[0], part_qkv.shape[1], down_ref.shape[0])
     inward = jnp.where(place < 2, 1, 2)
     outward = jnp.where(place < 2, 0, 3)
     opposite = 3 - inward
@@ -1206,9 +1367,50 @@
             copy.start()
 
     count = len(chunks)
-    way = scatter_parts(mine, side, near, last, dhin_ref, scatter_sems)
-    pairs = ((dqkv_ref, dqkv), (wqkv_ref, wqkv), (mixed_ref, mixed), (dattn_ref, dattn), (hin_ref, hin))
-    fetches = [pltpu.make_async_copy(src, dst, task_loads.at[i]) for i, (src, dst) in enumerate(pairs)]
+    way = scatter_parts(mine, side, near, last, dx_ref, scatter_sems)
+    pairs = (
+        (dattn_ref, dattn), (wout_ref, wout), (mixed_ref, mixed), (qkv_ref, qkv), (diff_ref, diff), (lse_ref, lse),
+        (mem_ref, mem), (nv_ref, nv), (wqkv_ref, wqkv), (hin_ref, hin),
+    )
+    fetches = [pltpu.make_async_copy(src, dst, fetch_sems.at[i]) for i, (src, dst) in enumerate(pairs)]
+
+    def d_mixed():
+        bias[...] = jnp.zeros_like(bias)
+        for ref in back_refs[2:]:
+            ref[...] = jnp.zeros_like(ref)
+
+        def body(i, _):
+            dmix[i] = dots(dattn[i], wout[...], 1, 1).reshape(dmix.shape[1:])
+            return 0
+
+        lax.fori_loop(0, 8, body, 0)
+
+    def attention_part(segment, i):
+        def run():
+            here = slice(segment, segment + 1)
+
+            def body(h, _):
+                back_block(
+                    i, h, heads, segment, starts_ref, blend_ref, qkv.at[:, here], dmix.at[:, here], diff.at[:, here],
+                    lse.at[:, here], mem, nv, dqkv.at[:, here], bias, *back_refs,
+                )
+                return 0
+
+            lax.fori_loop(0, heads, body, 0)
+
+        return run
+
+    def attention_end(segment):
+        def run():
+            here = slice(segment, segment + 1)
+
+            def body(h, _):
+                back_end(h, heads, segment, starts_ref, qkv.at[:, here], dqkv.at[:, here], *back_refs)
+                return 0
+
+            lax.fori_loop(0, heads, body, 0)
+
+        return run
 
     def products(block):
         return lambda: block_products(me, dqkv, wqkv, mine, True, way, block)
@@ -1230,7 +1432,7 @@
             tiles[0, :, at : at + 512] = dots(mixed[...].reshape(-1, mixed.shape[2]), right, 0, 0).astype(bf16)
         put(0, tiles.shape[2]).start()
 
-    columns = dqkv.shape[2]
+    columns = dqkv.shape[3]
 
     def qkv_tile(j):
         def run():
@@ -1239,7 +1441,7 @@
             rows = part_qkv.shape[1]
             left = hin[:, :, (j - 1) * rows : j * rows].reshape(-1, rows)
             for at in range(0, columns, 256):
-                right = dqkv[:, :, at : at + 256].reshape(-1, 256)
+                right = dqkv[:, :, :, at : at + 256].reshape(-1, 256)
                 tiles[j % 2, :, at : at + 256] = dots(left, right, 0, 0).astype(bf16)
             put(j, columns).start()
 
@@ -1252,12 +1454,26 @@
     def small_start():
         small_work[...] = small_ref[...]
         c = small_work.shape[2]
+        inverse = inv_ref[...]
         for j in range(8):
             here = slice(j * c, (j + 1) * c)
-            small_work[j, 0:1] = jnp.sum(normed_ref[:, here] * dhin_ref[:, here], axis=0, keepdims=True)
+            normed = x_ref[:, here].astype(f32) * inverse
+            small_work[j, 0:1] = jnp.sum(normed * dx_ref[:, here], axis=0, keepdims=True)
+        lanes = lax.broadcasted_iota(jnp.int32, (1, c), 1)
+        row = jnp.zeros((1, c), f32)
+        for h in range(heads):
+            cols = slice(h * HEAD_DIM, (h + 1) * HEAD_DIM)
+            gate = blend_ref[:, cols]
+            row = row + jnp.where(lanes == h, jnp.sum(bias[:, cols] * gate * (1.0 - gate), axis=1, keepdims=True), 0.0)
+        small_work[me, 2:3] = row
         for d in range(1, 8):
             small_moving(d).start()
         small_come[me] = small_work[me]
+        for r in range(0, dx_ref.shape[0], 64):
+            here = slice(r, r + 64)
+            normed = x_ref[here].astype(f32) * inv_ref[here]
+            t = dx_ref[here] * gain_ref[...]
+            dx_ref[here] = dres_ref[here] + norm_back(t, normed, inv_ref[here])
 
     def small_first():
         for d in range(1, 8):
@@ -1274,38 +1490,51 @@
             small_sum[...] = small_sum[...] + small_in[...]
             small_hop(small_sum, small_back, 1, opposite).start()
 
+    blocks = 8 * qkv.shape[2] // 256
     work = {
-        0: [fetched(0, 1), products(6), products(7)],
-        1: [products(4), way["combine"](6), products(5)],
-        2: [products(2), way["combine"](4), products(3)],
-        3: [products(0), way["combine"](2), products(1)],
-        4: [way["combine"](0), fetched(2, 3), out_tile],
-        5: [lambda: way["onward"](0), fetched(4), qkv_tile(1)],
-        6: [lambda: way["onward"](1), qkv_tile(2)],
-        7: [lambda: way["onward"](2), qkv_tile(3)],
-        8: [qkv_tile(4), qkv_tile(5)],
-        9: [qkv_tile(6), qkv_tile(7)],
-        10: [qkv_tile(8), all_put],
-        12: [way["finish"]],
-        13: [small_start],
-        18: [small_first],
+        0: [fetched(0, 1), d_mixed],
+        1: [fetched(2, 3, 4, 5, 6, 7, 8)],
+        10: [products(4), products(5)],
+        11: [way["combine"](6), products(2), products(3)],
+        12: [way["combine"](4), products(0), products(1)],
+        13: [way["combine"](2)],
+        14: [way["combine"](0)],
+        19: [lambda: way["onward"](0)],
+        20: [lambda: way["onward"](1)],
+        21: [lambda: way["onward"](2)],
+        26: [way["finish"], fetches[9].start],
+        27: [small_start],
+        28: [fetched(9), qkv_tile(1), qkv_tile(2)],
+        29: [qkv_tile(3), qkv_tile(4)],
+        30: [qkv_tile(5), qkv_tile(6)],
+        31: [qkv_tile(7), qkv_tile(8)],
+        32: [all_put],
+        38: [small_first],
     }
-    for fetch in fetches:
+    for i in range(4):
+        work[1 + i] = work.get(1 + i, []) + [attention_part(1, i)]
+        work[5 + i] = ([attention_end(1)] if i == 0 else []) + [attention_part(0, i)]
+    work[9] = [attention_end(0), out_tile, products(6), products(7)]
+    for fetch in fetches[:9]:
         fetch.start()
     feed(3)
+    ahead = 4
     for k in range(count):
         if k % 4 == 3 and k < 16:
             feed(1)
-        if k >= 18 and k % 2 == 0:
-            feed(1)
-        await_source(k)
+        if k >= 33:
+            feed(2)
 
         @pl.when(is_end)
         def _():
-            end_send(k).start()
+            for j in range(ahead + 1) if k == 0 else [k + ahead]:
+                if j < count:
+                    await_source(j)
+                    end_send(j).start()
 
         @pl.when(jnp.logical_not(is_end))
         def _():
+            await_source(k)
             own = pltpu.make_async_copy(source(k), box(g_buf, k, 2), loads.at[0])
             own.start()
             link(view(first, k), view(first, k), go_in, k, "seq", outward).wait_recv()
@@ -1317,8 +1546,8 @@
             got.wait()
             add(box(t_buf, k, SLOTS), box(g_buf, k, 2), box(a_buf, k, 2))
             mid_cross(k).start()
-            if k >= 1:
-                finish(k - 1)
+            if k >= LAG:
+                finish(k - LAG)
 
         for fn in work.get(k, ()):
             fn()
@@ -1340,7 +1569,8 @@
 
     @pl.when(jnp.logical_not(is_end))
     def _():
-        finish(count - 1)
+        for k in range(count - LAG, count):
+            finish(k)
         small_hop(small_out, small_out, 2, outward).wait_send()
         for k in range(max(0, count - SLOTS), count):
             mid_cross(k).wait_send()
@@ -1353,50 +1583,62 @@
         small_moving(d).wait_send()
 
 
-def finish(small, normed, gu, dqkv, wqkv, mixed, dattn, hin, collective_id):
+def finish(starts, blend, small, x, inv, gain, dres, gu, wqkv, mixed, dattn, hin, wout, qkv, diff, lse, mem, nv, down, collective_id):
     n, per, _ = gu.shape
-    rows, width = normed.shape
-    cw = mixed.shape[2]
-    if lax.axis_size("seq") != 4 or n != 8:
+    rows, width = x.shape
+    heads = mem.shape[0]
+    cw = heads * HEAD_DIM
+    if lax.axis_size("seq") != 4 or n != 8 or heads == 1:
         total = n * rows
-        dhin = mm_t(dqkv.reshape(total, 3 * cw), wqkv).astype(bf16)
-        dhin = lax.psum_scatter(dhin, "fsdp", scatter_dimension=0, tiled=True).astype(f32)
+        dmix = mm_t(dattn.reshape(total, width), wout).reshape(diff.shape)
+        dqkv, bias = attention_back(starts, blend, qkv, dmix, diff, lse, mem, nv, heads)
+        dqkv = dqkv.reshape(total, 3 * cw)
+        dhin = lax.psum_scatter(mm_t(dqkv, wqkv).astype(bf16), "fsdp", scatter_dimension=0, tiled=True).astype(f32)
+        normed = x.astype(f32) * inv
         small = small.at[:, 0].set(jnp.sum(normed * dhin, axis=0).reshape(n, per))
+        bias = jnp.sum((bias * blend * (1.0 - blend)).reshape(heads, HEAD_DIM), axis=1)
+        own = (jnp.arange(n) == lax.axis_index("fsdp"))[:, None]
+        small = small.at[:, 2].set(jnp.where(own, jnp.pad(bias, (0, per - heads))[None], 0.0))
+        dx = dres + norm_back(dhin * gain, normed, inv)
         out = lax.psum(t_mm(mixed.reshape(total, cw), dattn.reshape(total, width)).astype(bf16), "seq")
-        qkv = t_mm(hin.reshape(total, width), dqkv.reshape(total, 3 * cw)).astype(bf16).reshape(n, per, 3 * cw)
+        made = t_mm(hin.reshape(total, width), dqkv).astype(bf16).reshape(n, per, 3 * cw)
         moved = []
-        for x, count in ((gu, 2), (qkv, 3)):
-            c = x.shape[2] // count
-            x = lax.psum(lax.all_to_all(x, "fsdp", split_axis=0, concat_axis=0, tiled=True), "seq")
-            moved.append(x.reshape(n, per, count, c).transpose(2, 1, 0, 3).reshape(count, per, n * c))
+        for y, count in ((gu, 2), (made, 3)):
+            c = y.shape[2] // count
+            y = lax.psum(lax.all_to_all(y, "fsdp", split_axis=0, concat_axis=0, tiled=True), "seq")
+            moved.append(y.reshape(n, per, count, c).transpose(2, 1, 0, 3).reshape(count, per, n * c))
         small = lax.psum(lax.psum_scatter(small, "fsdp", scatter_dimension=0), "seq")
-        return small, dhin, out, *moved
-    qkv = jax.ShapeDtypeStruct((n, per, 3 * cw), bf16)
+        return small, dx, out, *moved, lax.psum(down, "seq")
+    made = jax.ShapeDtypeStruct((n, per, 3 * cw), bf16)
     out = jax.ShapeDtypeStruct((cw, width), bf16)
     gu_shape = jax.ShapeDtypeStruct(gu.shape, bf16)
-    count = len(chunks_of(per, cw, per))
+    count = len(chunks_of(per, cw, per, down.shape[0]))
+    down_shape = jax.ShapeDtypeStruct(down.shape, bf16)
     inside = pl.BlockSpec(memory_space=pltpu.VMEM)
     sems = pltpu.SemaphoreType.DMA
-    small_sum, dhin, _, _, sum_gu, sum_out, sum_qkv, *_ = pl.pallas_call(
+    small_sum, dx, _, _, sum_gu, sum_out, sum_qkv, sum_down, *_ = pl.pallas_call(
         finish_kernel,
-        in_specs=[inside] * 2 + [ANYWHERE] * 6,
-        out_specs=[inside] * 2 + [ANYWHERE] * 13,
+        in_specs=[pl.BlockSpec(memory_space=pltpu.SMEM)] + [inside] * 6 + [ANYWHERE] * 12,
+        out_specs=[inside] * 2 + [ANYWHERE] * 16,
         out_shape=[
             jax.ShapeDtypeStruct(small.shape[1:], f32),
             jax.ShapeDtypeStruct((rows, width), f32),
             out,
-            qkv,
+            made,
             jax.ShapeDtypeStruct((2, per, gu.shape[2] // 2 * n), bf16),
             out,
             jax.ShapeDtypeStruct((3, per, cw * n), bf16),
-            *[gu_shape, out, qkv] * 2,
+            down_shape,
+            *[gu_shape, out, made, down_shape] * 2,
             gu_shape,
-            qkv,
+            made,
         ],
-        scratch_shapes=[pltpu.VMEM(x.shape, bf16) for x in (dqkv, wqkv, mixed, dattn, hin)]
+        scratch_shapes=[pltpu.VMEM(y.shape, y.dtype) for y in (wqkv, mixed, wout, qkv, diff, lse, mem, nv)]
+        + [pltpu.VMEM(qkv.shape, bf16), pltpu.VMEM(diff.shape, f32), pltpu.VMEM((1, cw), f32)]
         + [pltpu.VMEM((2, per, width), bf16)]
+        + back_boxes(n, qkv.shape[2], heads)
         + scatter_boxes(rows, width)
-        + [sems((5,)), sems((2,)), *SCATTER_SEMS]
+        + [sems((10,)), sems((2,)), *SCATTER_SEMS]
         + [pltpu.VMEM(small.shape, f32)] * 2
         + [pltpu.VMEM(small.shape[1:], f32)] * 3
         + [sems((8,)), sems((8,)), sems((3,)), sems((3,))]
@@ -1404,10 +1646,10 @@
         + [sems((3,)), sems((SLOTS,))]
         + [sems((8,))] * 4
         + [sems((count,))] * 6,
-        compiler_params=params(collective_id, 60),
+        compiler_params=params(collective_id, 62),
         name="finish",
-    )(small, normed, gu, dqkv, wqkv, mixed, dattn, hin)
-    return small_sum, dhin, sum_out, sum_gu, sum_qkv
+    )(starts, blend, small, x, inv, gain, dres, gu, wqkv, mixed, dattn, hin, wout, qkv, diff, lse, mem, nv, down)
+    return small_sum, dx, sum_out, sum_gu, sum_qkv, sum_down
 
 
 def shards(
@@ -1448,14 +1690,10 @@
 
     flat_in = flat_in.astype(f32)
     normed_in, inv_in = normed(flat_in)
-    start_row = doc_starts[0]
-    docs = doc_number(start_row, jnp.arange(NSEG * seg_len, dtype=jnp.int32)).reshape(NSEG, seg_len)
-    side = (docs == docs[1, 0]).astype(f32)[:, :, None]
-    doc_col, doc_row = docs[:, :, None], docs[:, None, :]
     blend = jax.nn.sigmoid(mix_bias)
     blend_row = jnp.repeat(blend, HEAD_DIM)[None]
     h_in, qkv, dy, mixed, diff, lse, memory, norm_vec = attend(
-        all_in, gain_in, wqkv, cotangent.reshape(own, width), doc_col, doc_row, side, blend_row, heads, 4
+        all_in, gain_in, wqkv, cotangent.reshape(own, width), doc_starts[0], blend_row, heads, 4
     )
     h_in, dy = h_in.reshape(total, width), dy.reshape(total, width)
     mixed = mixed.reshape(total, cw)
@@ -1470,39 +1708,40 @@
 
     gain_mid_term = jnp.sum(normed_mid * d_hmid, axis=0)
     d_resid = cotangent.reshape(own, width).astype(f32) + norm_back(d_hmid * gain_mid, normed_mid, inv_mid)
-    d_attn, part_gu, part_mlp = gather_products(d_resid.astype(bf16), h_mid, d_gu, inner, w_down, 2)
+    d_attn, part_gu, part_mlp, sum_head = gather_products(d_resid.astype(bf16), h_mid, d_gu, inner, w_down, part_down, 2)
     part_gu = part_gu.reshape(n, width // n, 2 * fw)
-    grad_down = lax.psum(part_down, "seq").astype(f32)
-
-    d_mixed = mm_t(d_attn.reshape(total, width), w_out).reshape(n, NSEG, rows, cw)
-    d_qkv, bias_rows = attention_back(
-        qkv, d_mixed, diff, lse, doc_col, doc_row, side, blend_row, memory, norm_vec, heads
-    )
-    bias_term = jnp.sum(bias_rows.reshape(heads, HEAD_DIM), axis=1) * blend * (1.0 - blend)
 
     mlp_sum = lax.psum_scatter(part_mlp, "fsdp", scatter_dimension=0, tiled=True)
     block_out = (residual + mlp_sum.astype(f32)).astype(bf16).reshape(tokens.shape)
     per = width // n
-    mine = (jnp.arange(n) == lax.axis_index("fsdp"))[:, None, None]
-    bias = jnp.where(mine, jnp.pad(bias_term, (0, per - heads))[None, None], 0.0)
-    terms = jnp.concatenate(
-        [jnp.zeros((n, 1, per), f32), gain_mid_term.reshape(n, 1, per), bias, jnp.zeros((n, 5, per), f32)], axis=1
-    )
-    small, d_hin, sum_out, sum_gu, sum_qkv = finish(
+    terms = jnp.pad(gain_mid_term.reshape(n, 1, per), ((0, 0), (1, 6), (0, 0)))
+    small, grad_tokens, sum_out, sum_gu, sum_qkv, sum_down = finish(
+        doc_starts[0],
+        blend_row,
         terms,
-        normed_in,
+        tokens.reshape(own, width),
+        inv_in,
+        gain_in,
+        d_resid,
         part_gu,
-        d_qkv.reshape(n, own, 3 * cw),
         wqkv,
         mixed.reshape(n, own, cw),
         d_attn,
         h_in.reshape(n, own, width),
+        w_out,
+        qkv,
+        diff,
+        lse,
+        memory,
+        norm_vec,
+        part_down,
         6,
     )
+    grad_down = jnp.concatenate([sum_head, sum_down[sum_head.shape[0] :]]).astype(f32)
+    grad_tokens = grad_tokens.reshape(tokens.shape)
     grad_out = sum_out.astype(f32)
     grad_gate, grad_up = sum_gu[0].astype(f32), sum_gu[1].astype(f32)
     grad_q, grad_k, grad_v = (sum_qkv[i].astype(f32) for i in range(3))
-    grad_tokens = (d_resid + norm_back(d_hin * gain_in, normed_in, inv_in)).reshape(tokens.shape)
 
     return (
         block_out,

time: 815 us -> 801 us (0.983)
  other arithmetic: 41.3 us -> 31.4 us
    pallas_call x3 -> x2, Pallas kernels: 432 us -> 437 us  [the longest x1 381 us: finish(): pl.pallas_call(finish_kernel, in_specs=[pl.BlockSpec(memory_space=pltpu.S...]
  transfers between devices with their start and end apart: 3 -> 2, of which waited for: 0 -> 0; matrix products, arithmetic and copies ran while one was open for 6% -> 4% of each run, Pallas kernels for 74% -> 68%
where the time goes in v4:
time: 801 us; the launch traced here: 789 us
  Pallas kernels  723 us (90%)
  other arithmetic  31.4 us (4%)
  local copies, waits for them, and re-layouts  19.7 us (2%)
  between operations  14.8 us (2%)
    pallas_call x1, Pallas kernels, finish(): pl.pallas_call(finish_kernel, in_specs=[pl.BlockSpec(memory_space=pltpu.S...  381 us
    pallas_call x1, Pallas kernels, mlp(): pl.pallas_call(mlp_kernel, in_specs=[ANYWHERE] * 4, out_specs=[ANYWHERE]...  100 us
    pallas_call x1, Pallas kernels, front(): pl.pallas_call(functools.partial(front_kernel, count), in_specs=[ANYWHERE...  74.5 us
    pallas_call x1, Pallas kernels, gather_products(): pl.pallas_call(gather_products_kernel, in_specs=[ANYWHERE] * 6, out_specs...  55.5 us
    pallas_call x1, Pallas kernels, attend(): pl.pallas_call(functools.partial(attend_kernel, heads), in_specs=[ANYWHER...  43.6 us
    pallas_call x1, Pallas kernels, product_scatter(): pl.pallas_call(product_scatter_kernel, in_specs=[ANYWHERE] * 2, out_specs...  40.1 us
    pallas_call x1, Pallas kernels, to_columns_in_turns(): pl.pallas_call(functools.partial(move_kernel, count, share), in_specs=[AN...  28.3 us
  transfers between devices with their start and end apart: 2, of which 0 were waited for; matrix products, arithmetic and copies ran while one was open for 4% of the time, Pallas kernels for 68%

profile of v4, /device:TPU:0, one launch (start us, length us, event | category | flops | bytes accessed | tf_op | source)
XLA Modules:
  0.0 789.4 jit_solution(410371447510840024)
XLA Ops:
  7.2 2.2 copy-done.1
  9.4 2.2 copy-done.2
  11.6 28.3 %move.1 = bf16[512,2048]{1,0:T(8,128)(2,1)} custom-call(bf16[256,8192]{1,0:T(8,128)(2,1)S(1)} %copy-done.1, bf16[256,8192]{1,0:T(8,128)(2,1)S(1)} %copy-done.2), custom_call_target="tpu_custom_call" | custom-call | tf_op jit(solution)/shard_map/move/pallas_call | solution.py:492
  40.1 0.5 copy-done.24
  40.7 0.5 copy-done
  41.1 0.3 copy-done.7
  41.5 1.2 copy-done.9
  42.7 74.5 %front.1 = (bf16[8,256,2048]{2,1,0:T(8,128)(2,1)S(1)}, f32[8,8,256]{2,1,0:T(8,128)S(1)}, bf16[2048,768]{1,0:T(8,128)(2,1)S(1)}) custom-call(bf16[256,2048]{1,0:T(8,128)(2,1)S(1)} %bitcast.45, f32[8,256]{1,0:T(8,128)S(1)} %maximum_maximum_fusion.refs_1_, bf16[256,2048]{1,0:T(8,128)(2,1)S(1)} %copy-done.7, bf16[256,2048]{1,0:T(8,128)(2,1)S(1)} %copy-done.8, ...), custom_call_target="tpu_custom_call" | custom-call | tf_op jit(solution)/shard_map/front/pallas_call | solution.py:548
  117.2 1.7 copy-done.3
  118.9 3.4 copy-done.17
  122.4 43.6 %attend.1 = (bf16[8,256,2048]{2,1,0:T(8,128)(2,1)}, bf16[8,2,128,768]{3,2,1,0:T(8,128)(2,1)}, bf16[8,256,2048]{2,1,0:T(8,128)(2,1)}, bf16[8,2,128,256]{3,2,1,0:T...) custom-call(bf16[8,256,2048]{2,1,0:T(8,128)(2,1)} %copy-done.17, ...), custom_call_target="tpu_custom_call" | custom-call | flops 7516192768 | bytes 33554432 | tf_op jit(solution)/shard_map/attend/pallas_call | solution.py:654
  166.1 40.1 %product_scatter.1 = f32[256,2048]{1,0:T(8,128)S(1)} custom-call(bf16[8,256,256]{2,1,0:T(8,128)(2,1)S(1)} %bitcast.46, bf16[256,2048]{1,0:T(8,128)(2,1)S(1)} %copy-done.5), custom_call_target="tpu_custom_call" | custom-call | flops 2147483648 | bytes 8388608 | tf_op jit(solution)/shard_map/product_scatter/pallas_call | solution.py:1201
  206.2 0.4 multiply_reduce_fusion.3
  206.6 1.4 multiply_convert_fusion.own_ref
  208.1 100.2 %mlp.1 = (bf16[8,256,2048]{2,1,0:T(8,128)(2,1)}, bf16[8,256,1024]{2,1,0:T(8,128)(2,1)}, bf16[8,256,2048]{2,1,0:T(8,128)(2,1)}, bf16[1024,2048]{1,0:T(8,128)(2,1)}, f32[256,2048]{1,0:T(8,128)}) custom-call(bf16[256,2048]{1,0:T(8,128)(2,1)} %multiply_convert_fusion.own_ref, bf16[2048,2048]{1,0:T(8,128)(2,1)} %bitcast.67, bf16[1024,2048]{1,0:T(8,128)(2,1)} %wd_ref.3, ...), custom_call_target="tpu_custom_call" | custom-call | flops 42949672960 | bytes 67108864 | tf_op jit(solution)/shard_map/mlp/pallas_call | solution.py:937
  308.3 2.3 multiply_reduce_fusion.1
  310.6 0.2 copy-done.20
  310.8 2.3 fusion
  313.1 55.5 %gather_products.1 = (bf16[8,256,2048]{2,1,0:T(8,128)(2,1)}, bf16[2048,2048]{1,0:T(8,128)(2,1)}, bf16[2048,2048]{1,0:T(8,128)(2,1)}, bf16[384,2048]{1,0:T(8,128)(2,1)}) custom-call(bf16[256,2048]{1,0:T(8,128)(2,1)} %get-tuple-element.66.x_ref, bf16[2048,2048]{1,0:T(8,128)(2,1)} %bitcast.68, bf16[2048,2048]{1,0:T(8,128)(2,1)} %bitcast.69, ...), custom_call_target="tpu_custom_call" | custom-call | flops 25769803776 | bytes 50331648 | tf_op jit(solution)/shard_map/gather_products/pallas_call | solution.py:1143
  368.6 0.3 multiply_reduce_fusion
  368.9 0.8 copy.25.refs_4_
  369.7 0.6 pad.4.refs_2_
  370.3 381.2 %finish.1 = (f32[8,256]{1,0:T(8,128)}, f32[256,2048]{1,0:T(8,128)}, bf16[256,2048]{1,0:T(8,128)(2,1)}, bf16[8,256,768]{2,1,0:T(8,128)(2,1)}, bf16[2,256,8192]{2,...) custom-call(s32[4]{0:T(128)} %bitcast.53, ...), custom_call_target="tpu_custom_call" | custom-call | tf_op jit(solution)/shard_map/finish/pallas_call | solution.py:1619
  751.5 2.8 convert_element_type.72
  754.3 2.0 slice.52
  756.4 1.2 slice_bitcast_fusion.1
  757.6 1.3 fusion.2
  758.9 4.3 maximum_convert_fusion
  763.2 2.9 bitcast_convert_fusion.2
  766.2 12.0 %bitcast_convert_fusion = (f32[256,8192]{1,0:T(8,128)}, f32[256,8192]{1,0:T(8,128)}) fusion(bf16[2,256,8192]{2,1,0:T(8,128)(2,1)} %get-tuple-element.61), kind=kLoop, calls=%fused_computation.1 | loop fusion | flops 4194304 | bytes 25165824 | tf_op jit(solution)/shard_map/convert_element_type | solution.py:1743
  778.1 2.6 add_convert_fusion
  780.8 1.3 copy.27
  (61 shorter events, 0.5 us)
Async XLA Ops:
  7.2 200.9 %all-gather.2.cloned.1.call-start = ((), (), s32[]{:S(2)}) async-start(), calls=%async_computation.1 | async-start | bytes 10485760 | tf_op jit(solution)/shard_map/all_gather | solution.py:502
  7.2 2.2 copy-start.1
  9.4 2.2 copy-start.2
  11.6 29.1 %copy-start.8 = (bf16[256,2048]{1,0:T(8,128)(2,1)S(1)}, bf16[256,2048]{1,0:T(8,128)(2,1)}, u32[]{:S(2)}) copy-start(bf16[256,2048]{1,0:T(8,128)(2,1)} %refs_3_.1) | copy-start | bytes 3145732
  39.9 0.7 copy-start.24
  39.9 0.7 copy-start.25
  39.9 1.2 copy-start
  39.9 1.5 copy-start.7
  40.0 738.2 %reduce-scatter.2.cloned.1.call-start = ((), (), s32[]{:S(2)}) async-start(), calls=%async_computation.2 | async-start | bytes 9437184 | tf_op jit(solution)/shard_map/reduce_scatter | solution.py:1714
  41.5 1.2 copy-start.9
  42.7 79.6 %copy-start.26 = (f32[2]{0:T(128)S(1)}, f32[2]{0:T(128)}, u32[]{:S(2)}) copy-start(f32[2]{0:T(128)} %param.19) | copy-start | bytes 28
  42.7 79.7 %copy-start.10 = (bf16[1,2,128,2048]{3,2,1,0:T(8,128)(2,1)S(1)}, bf16[1,2,128,2048]{3,2,1,0:T(8,128)(2,1)}, u32[]{:S(2)}) copy-start(bf16[1,2,128,2048]{3,2,1,0:T(8,128)(2,1)} %param.25) | copy-start | bytes 3145732
  42.7 79.7 %copy-start.16 = (s32[1,4]{1,0:T(1,128)S(1)}, s32[1,4]{1,0:T(1,128)}, u32[]{:S(2)}) copy-start(s32[1,4]{1,0:T(1,128)} %param.14) | copy-start | bytes 52
  117.2 1.7 copy-start.3
  118.9 3.4 copy-start.17
  122.3 43.7 %copy-start.13 = (f32[1,8,256]{2,0,1:T(1,128)}, f32[1,8,256]{2,0,1:T(1,128)S(1)}, u32[]{:S(2)}) copy-start(f32[1,8,256]{2,0,1:T(1,128)S(1)} %get-tuple-element.76) | copy-start | bytes 24580
  122.4 43.6 %copy-start.14 = (f32[2,128]{1,0:T(2,128)}, f32[2,128]{1,0:T(2,128)S(1)}, u32[]{:S(2)}) copy-start(f32[2,128]{1,0:T(2,128)S(1)} %broadcast_in_dim.10) | copy-start | bytes 3076
  122.4 43.7 %copy-start.5 = (bf16[256,2048]{1,0:T(8,128)(2,1)S(1)}, bf16[256,2048]{1,0:T(8,128)(2,1)}, u32[]{:S(2)}) copy-start(bf16[256,2048]{1,0:T(8,128)(2,1)} %refs_12_.1) | copy-start | bytes 3145732
  166.0 40.2 %copy-start.4 = (f32[8,2,128,256]{3,2,1,0:T(8,128)}, f32[8,2,128,256]{3,2,1,0:T(8,128)S(1)}, u32[]{:S(2)}) copy-start(f32[8,2,128,256]{3,2,1,0:T(8,128)S(1)} %get-tuple-element.53.refs_14_) | copy-start | bytes 6291460
  166.0 40.2 %copy-start.6 = (bf16[8,2,128,256]{3,2,1,0:T(8,128)(2,1)}, bf16[8,2,128,256]{3,2,1,0:T(8,128)(2,1)S(1)}, u32[]{:S(2)}) copy-start(bf16[8,2,128,256]{3,2,1,0:T(8,128)(2,1)S(1)} %get-tuple-element.41) | copy-start | bytes 3145732
  166.0 40.2 %copy-start.12 = (f32[2,128,128]{2,1,0:T(8,128)}, f32[2,128,128]{2,1,0:T(8,128)S(1)}, u32[]{:S(2)}) copy-start(f32[2,128,128]{2,1,0:T(8,128)S(1)} %get-tuple-element.55.refs_16_) | copy-start | bytes 393220
  166.0 40.2 %copy-start.15 = (f32[2,1,128]{2,1,0:T(1,128)}, f32[2,1,128]{2,1,0:T(1,128)S(1)}, u32[]{:S(2)}) copy-start(f32[2,1,128]{2,1,0:T(1,128)S(1)} %get-tuple-element.56.refs_17_) | copy-start | bytes 3076
  206.6 104.0 %copy-start.18 = (f32[256,2048]{1,0:T(8,128)}, f32[256,2048]{1,0:T(8,128)S(1)}, u32[]{:S(2)}) copy-start(f32[256,2048]{1,0:T(8,128)S(1)} %get-tuple-element.69) | copy-start | bytes 6291460
  308.2 2.4 copy-start.11
  308.3 2.5 copy-start.20
  754.3 4.6 copy-start.23
  758.9 4.3 copy-start.21
  766.2 12.0 %copy-start.19 = (f32[256,2048]{1,0:T(8,128)S(1)}, f32[256,2048]{1,0:T(8,128)}, u32[]{:S(2)}) copy-start(f32[256,2048]{1,0:T(8,128)} %copy-done.18) | copy-start | bytes 6291460
  778.1 2.6 copy-start.22
Sparse Core Ops, SparseCore 0:
  40.1 149.9 all-gather.1
  368.7 121.8 reduce-scatter.1

commit v5 on v4

--- a/solution.py
+++ b/solution.py
@@ -418,7 +418,7 @@
     return [*steps, finish]
 
 
-def params(collective_id, mib=32):
+def params(collective_id, mib=62):
     return pltpu.CompilerParams(collective_id=collective_id, has_side_effects=True, vmem_limit_bytes=mib << 20)
 
 
@@ -669,7 +669,7 @@
             *[sems((k,)) for k in (1, 2, 2, 1)],
             *GATHER_SEMS,
         ],
-        compiler_params=params(collective_id, 48),
+        compiler_params=params(collective_id),
         cost_estimate=pl.CostEstimate(
             flops=pairs * 4 * HEAD_DIM + 6 * n * tokens * width * cw, transcendentals=pairs, bytes_accessed=32 << 20
         ),
@@ -1204,7 +1204,7 @@
         out_specs=pl.BlockSpec(memory_space=pltpu.VMEM),
         out_shape=jax.ShapeDtypeStruct((rows, width), f32),
         scratch_shapes=[pltpu.VMEM(lhs.shape, bf16), pltpu.VMEM(rhs.shape, bf16), *scatter_boxes(rows, width), sems((2,)), *SCATTER_SEMS],
-        compiler_params=params(collective_id, 40),
+        compiler_params=params(collective_id),
         cost_estimate=pl.CostEstimate(flops=2 * n * rows * depth * width, transcendentals=0, bytes_accessed=8 << 20),
         name="product_scatter",
     )(lhs, rhs)

time: 801 us -> 798 us (level)
  local copies, waits for them, and re-layouts: 19.7 us -> 10.2 us
    unnamed x55 -> x23, local copies, waits for them, and re-layouts: 13.5 us -> 2 us
  transfers between devices with their start and end apart: 2 -> 2, of which waited for: 0 -> 0; matrix products, arithmetic and copies ran while one was open for 4% -> 4% of each run, Pallas kernels for 68% -> 69%
where the time goes in v5:
time: 798 us; the launch traced here: 786 us
  Pallas kernels  727 us (91%)
  other arithmetic  33.5 us (4%)
  between operations  14.7 us (2%)
  local copies, waits for them, and re-layouts  10.2 us (1%)
    pallas_call x1, Pallas kernels, finish(): pl.pallas_call(finish_kernel, in_specs=[pl.BlockSpec(memory_space=pltpu.S...  381 us
    pallas_call x1, Pallas kernels, mlp(): pl.pallas_call(mlp_kernel, in_specs=[ANYWHERE] * 4, out_specs=[ANYWHERE]...  100 us
    pallas_call x1, Pallas kernels, front(): pl.pallas_call(functools.partial(front_kernel, count), in_specs=[ANYWHERE...  75.2 us
    pallas_call x1, Pallas kernels, gather_products(): pl.pallas_call(gather_products_kernel, in_specs=[ANYWHERE] * 6, out_specs...  55.4 us
    pallas_call x1, Pallas kernels, attend(): pl.pallas_call(functools.partial(attend_kernel, heads), in_specs=[ANYWHER...  45.1 us
    pallas_call x1, Pallas kernels, product_scatter(): pl.pallas_call(product_scatter_kernel, in_specs=[ANYWHERE] * 2, out_specs...  41.9 us
    pallas_call x1, Pallas kernels, to_columns_in_turns(): pl.pallas_call(functools.partial(move_kernel, count, share), in_specs=[AN...  28.5 us
  transfers between devices with their start and end apart: 2, of which 0 were waited for; matrix products, arithmetic and copies ran while one was open for 4% of the time, Pallas kernels for 69%

profile of v5, /device:TPU:0, one launch (start us, length us, event | category | flops | bytes accessed | tf_op | source)
XLA Modules:
  0.0 786.0 jit_solution(5455679252626718394)
XLA Ops:
  7.2 0.0 all-gather.2.cloned.1.call-start
  7.2 28.5 %move.1 = bf16[512,2048]{1,0:T(8,128)(2,1)} custom-call(bf16[256,8192]{1,0:T(8,128)(2,1)} %refs_0_.1, bf16[256,8192]{1,0:T(8,128)(2,1)} %refs_1_.1), custom_call_target="tpu_custom_call" | custom-call | tf_op jit(solution)/shard_map/move/pallas_call | solution.py:492
  35.8 0.0 reduce-scatter.2.cloned.1.call-start
  35.9 0.1 pad.9.clone
  35.9 0.5 copy-done.8
  36.5 0.7 maximum_maximum_fusion.refs_1_
  37.1 75.2 %front.1 = (bf16[8,256,2048]{2,1,0:T(8,128)(2,1)}, f32[8,8,256]{2,1,0:T(8,128)}, bf16[2048,768]{1,0:T(8,128)(2,1)}) custom-call(bf16[256,2048]{1,0:T(8,128)(2,1)} %bitcast.44, f32[8,256]{1,0:T(8,128)} %maximum_maximum_fusion.refs_1_, bf16[256,2048]{1,0:T(8,128)(2,1)} %refs_2_.1, bf16[256,2048]{1,0:T(8,128)(2,1)} %refs_3_.1, bf16[256,2048]{1,0:T(8,128)(2,1)} %refs_4_.1), custom_call_target="tpu_custom_call" | custom-call | tf_op jit(solution)/shard_map/front/pallas_call | solution.py:548
  112.4 0.8 slice_bitcast_fusion
  113.2 0.6 fusion.1
  113.8 0.6 broadcast_in_dim.10
  114.5 45.1 %attend.1 = (bf16[8,256,2048]{2,1,0:T(8,128)(2,1)}, bf16[8,2,128,768]{3,2,1,0:T(8,128)(2,1)}, bf16[8,256,2048]{2,1,0:T(8,128)(2,1)}, bf16[8,2,128,256]{3,2,1,0:T...) custom-call(bf16[8,256,2048]{2,1,0:T(8,128)(2,1)} %get-tuple-element, ...), custom_call_target="tpu_custom_call" | custom-call | flops 7516192768 | bytes 33554432 | tf_op jit(solution)/shard_map/attend/pallas_call | solution.py:654
  159.6 41.9 %product_scatter.1 = f32[256,2048]{1,0:T(8,128)} custom-call(bf16[8,256,256]{2,1,0:T(8,128)(2,1)} %bitcast.49, bf16[256,2048]{1,0:T(8,128)(2,1)} %refs_12_.1), custom_call_target="tpu_custom_call" | custom-call | flops 2147483648 | bytes 8388608 | tf_op jit(solution)/shard_map/product_scatter/pallas_call | solution.py:1201
  201.5 1.9 multiply_reduce_fusion.3
  203.5 1.4 multiply_convert_fusion.own_ref
  204.9 100.2 %mlp.1 = (bf16[8,256,2048]{2,1,0:T(8,128)(2,1)}, bf16[8,256,1024]{2,1,0:T(8,128)(2,1)}, bf16[8,256,2048]{2,1,0:T(8,128)(2,1)}, bf16[1024,2048]{1,0:T(8,128)(2,1)}, f32[256,2048]{1,0:T(8,128)}) custom-call(bf16[256,2048]{1,0:T(8,128)(2,1)} %multiply_convert_fusion.own_ref, bf16[2048,2048]{1,0:T(8,128)(2,1)} %bitcast.68, bf16[1024,2048]{1,0:T(8,128)(2,1)} %wd_ref.3, ...), custom_call_target="tpu_custom_call" | custom-call | flops 42949672960 | bytes 67108864 | tf_op jit(solution)/shard_map/mlp/pallas_call | solution.py:937
  305.1 2.3 multiply_reduce_fusion.1
  307.4 0.1 copy-done.7
  307.5 2.3 fusion
  309.8 55.4 %gather_products.1 = (bf16[8,256,2048]{2,1,0:T(8,128)(2,1)}, bf16[2048,2048]{1,0:T(8,128)(2,1)}, bf16[2048,2048]{1,0:T(8,128)(2,1)}, bf16[384,2048]{1,0:T(8,128)(2,1)}) custom-call(bf16[256,2048]{1,0:T(8,128)(2,1)} %get-tuple-element.66.x_ref, bf16[2048,2048]{1,0:T(8,128)(2,1)} %bitcast.69, bf16[2048,2048]{1,0:T(8,128)(2,1)} %bitcast.70, ...), custom_call_target="tpu_custom_call" | custom-call | flops 25769803776 | bytes 50331648 | tf_op jit(solution)/shard_map/gather_products/pallas_call | solution.py:1143
  365.2 0.3 multiply_reduce_fusion
  365.5 0.8 copy.25.refs_4_
  366.3 0.6 pad.4.refs_2_
  367.0 381.2 %finish.1 = (f32[8,256]{1,0:T(8,128)}, f32[256,2048]{1,0:T(8,128)}, bf16[256,2048]{1,0:T(8,128)(2,1)}, bf16[8,256,768]{2,1,0:T(8,128)(2,1)}, bf16[2,256,8192]{2,...) custom-call(s32[4]{0:T(128)} %bitcast.67, ...), custom_call_target="tpu_custom_call" | custom-call | tf_op jit(solution)/shard_map/finish/pallas_call | solution.py:1619
  748.2 2.8 convert_element_type.72
  751.0 2.0 slice.52
  753.0 1.2 slice_bitcast_fusion.1
  754.2 1.3 fusion.2
  755.5 4.3 maximum_convert_fusion
  759.8 2.9 bitcast_convert_fusion.2
  762.8 12.0 %bitcast_convert_fusion = (f32[256,8192]{1,0:T(8,128)}, f32[256,8192]{1,0:T(8,128)}) fusion(bf16[2,256,8192]{2,1,0:T(8,128)(2,1)} %get-tuple-element.61), kind=kLoop, calls=%fused_computation.1 | loop fusion | flops 4194304 | bytes 25165824 | tf_op jit(solution)/shard_map/convert_element_type | solution.py:1743
  774.7 2.6 add_convert_fusion
  777.4 1.3 copy.27
  (29 shorter events, 0.1 us)
Async XLA Ops:
  7.2 197.7 %all-gather.2.cloned.1.call-start = ((), (), s32[]{:S(2)}) async-start(), calls=%async_computation.1 | async-start | bytes 10485760 | tf_op jit(solution)/shard_map/all_gather | solution.py:502
  35.8 0.7 copy-start.8
  35.8 0.7 copy-start.9
  35.8 738.9 %reduce-scatter.2.cloned.1.call-start = ((), (), s32[]{:S(2)}) async-start(), calls=%async_computation.2 | async-start | bytes 9437184 | tf_op jit(solution)/shard_map/reduce_scatter | solution.py:1714
  37.1 75.2 %copy-start.10 = (f32[2]{0:T(128)S(1)}, f32[2]{0:T(128)}, u32[]{:S(2)}) copy-start(f32[2]{0:T(128)} %param.19) | copy-start | bytes 28
  159.6 41.9 %copy-start.2 = (bf16[1,2,128,2048]{3,2,1,0:T(8,128)(2,1)S(1)}, bf16[1,2,128,2048]{3,2,1,0:T(8,128)(2,1)}, u32[]{:S(2)}) copy-start(bf16[1,2,128,2048]{3,2,1,0:T(8,128)(2,1)} %param.13) | copy-start | bytes 3145732
  203.4 103.9 %copy-start = (f32[256,2048]{1,0:T(8,128)}, f32[256,2048]{1,0:T(8,128)S(1)}, u32[]{:S(2)}) copy-start(f32[256,2048]{1,0:T(8,128)S(1)} %get-tuple-element.69) | copy-start | bytes 6291460
  305.0 2.4 copy-start.3
  305.0 2.5 copy-start.7
  751.0 4.6 copy-start.6
  755.5 4.3 copy-start.4
  762.8 12.0 %copy-start.1 = (f32[256,2048]{1,0:T(8,128)S(1)}, f32[256,2048]{1,0:T(8,128)}, u32[]{:S(2)}) copy-start(f32[256,2048]{1,0:T(8,128)} %copy-done) | copy-start | bytes 6291460
  774.7 2.6 copy-start.5
Sparse Core Ops, SparseCore 0:
  35.9 149.9 all-gather.1
  365.3 121.8 reduce-scatter.1
